TPU v7x, 512 devices: a whole 4x4x16 slice. The times are simulated.
512 devices in a mesh: head: 16 (over z), ctx: 32 (over x, y, core).
Axes of the slice: x: 4, y: 4, z: 16, core: 2. Of those that a mesh axis runs over, the one named last changes fastest.
Arguments:
- x_mant: bfloat16 [4096, 16384], P('ctx', 'head'), may hold values from -4 to 4
- x_codes: int32 [4096, 512], P('ctx', 'head'), may hold values from -2 to 2
- bc_raw: bfloat16 [4096, 2048], P('ctx'), may hold values from -5 to 5
- gate_z: bfloat16 [4096, 16384], P('ctx', 'head'), may hold values from -5 to 5
- conv_x: float32 [4, 16384], P(None, 'head'), may hold values from -3 to 3
- conv_bc: float32 [4, 2048], replicated, may hold values from -3 to 3
- dt_raw: float32 [4096, 256], P('ctx', 'head'), may hold values from -4 to 4
- a_log: float32 [256], P('head'), as said below
- d_skip: float32 [256], P('head'), may hold values from 0.5 to 1.5
- norm_gain: float32 [16384], P('head'), may hold values from 0.5 to 1.5
- prompt_lengths: int32 [4], replicated, may hold values from 1 to 2112, 4096 in all
- cache_slot: int32 [4], replicated, may hold values from 0 to 63, as said below
- prefix_state: bfloat16 [64, 16384, 128], P('ctx', 'head'), may hold values from -5 to 5
- tail_x: bfloat16 [64, 3, 16384], P('ctx', None, 'head'), may hold values from -5 to 5
- tail_bc: bfloat16 [64, 3, 2048], P('ctx'), may hold values from -5 to 5
Outputs:
- mixed: bfloat16 [4096, 16384], P('ctx', 'head')
Inputs may be any that keep to these rules, and one draw needn't show every extreme that they name: `prompt_lengths`: the lengths sum to 4096, and the longest is exactly 2112. `cache_slot`: slot 63 is read by some prompt and slot 0 by another; prompts may share a slot. `a_log`: log of a positive rate per head.
All inputs are finite; a program needn't handle non-finite values.
Results may differ from a plain program's by a relative error of at most 0.0065.
Values may be sent and summed in bfloat16 or wider, within the bound.
No kernel may reach another device: no remote copies, remote signals or barrier semaphores. Data moves between devices by JAX's collectives and lax.ppermute only.
A program may use at most 64 MiB of HBM per device.

v0:
```python
import jax
import jax.numpy as jnp
from jax import lax
from jax.sharding import PartitionSpec as P

HEADS = 256
GROUPS = 8


eps_norm = 1e-05


def passed_along(array, axis, by):
    devices = lax.axis_size(axis)
    pairs = [(i, i + by) for i in range(devices) if 0 <= i + by < devices]
    return lax.ppermute(array, axis, pairs)


def from_root(value, axis, source):
    kept = jnp.where(lax.axis_index(axis) == source, value, 0).astype(value.dtype)
    return lax.psum(kept, axis)


def entering(array, axis, combine, identity):
    devices, index = (lax.axis_size(axis), lax.axis_index(axis))
    everything = jax.tree.map(lambda part: lax.all_gather(part, axis), array)
    start = jax.tree.map(
        lambda part, zero: jnp.broadcast_to(jnp.asarray(zero, part.dtype), part.shape),
        array,
        identity,
    )

    def hop(k, before):
        reached = k < index
        new = combine(before, jax.tree.map(lambda part: part[k], everything))
        return jax.tree.map(lambda a, b: jnp.where(reached, a, b), new, before)

    return lax.fori_loop(0, devices, hop, start)


def dequant(mantissa, codes):
    row_count, chan_count = mantissa.shape
    block_count = codes.shape[1]
    scaled = mantissa.astype(jnp.float32).reshape(row_count, block_count, chan_count // block_count)
    scaled = scaled * jnp.exp2(codes.astype(jnp.float32))[:, :, None]
    return scaled.reshape(row_count, chan_count)


def prompt_rows(starts, offset, row_count):
    position = jnp.arange(row_count, dtype=jnp.int32) + offset
    inside = (position[:, None] >= starts[None, :]).astype(jnp.int32)
    return jnp.sum(inside, axis=1) - 1


def pick_rows(table, prompt_id):
    hit = prompt_id[:, None] == jnp.arange(table.shape[0], dtype=jnp.int32)[None, :]
    return jnp.sum(jnp.where(hit, table[None, :], 0), axis=1)


def causal_conv(current, previous, tails, weights, prompt_id, start_loc):
    row_count, chan_count = current.shape
    lag_count = previous.shape[0]
    prompt_count = tails.shape[0]
    extended = jnp.concatenate([previous, current], axis=0)
    flat_tails = tails.reshape(prompt_count * lag_count, chan_count)
    row_start = pick_rows(start_loc, prompt_id)
    position = jnp.arange(row_count, dtype=jnp.int32)
    total = jnp.zeros((row_count, chan_count), jnp.float32)
    for shift_by in range(lag_count + 1):
        source = extended[lag_count - shift_by : lag_count - shift_by + row_count]
        earlier = position - shift_by
        index = prompt_id * lag_count + jnp.clip(earlier - row_start + lag_count, 0, lag_count - 1)
        tail_rows = jnp.take(flat_tails, index, axis=0)
        value = jnp.where((earlier < row_start)[:, None], tail_rows, source)
        total = total + weights[lag_count - shift_by][None, :] * value
    return total


def span_local(x_act, b_act, c_act, delta, log_decay, prompt_id, start_loc, prefixes):
    row_count, head_count, width = x_act.shape
    group_count, state = (b_act.shape[1], b_act.shape[2])
    per_group = head_count // group_count
    cumul = jnp.cumsum(log_decay, axis=0)
    before_sum = cumul - log_decay
    position = jnp.arange(row_count, dtype=jnp.int32)
    live = (prompt_id[:, None] == prompt_id[None, :]) & (position[:, None] >= position[None, :])
    scores = jnp.einsum("tgn,sgn->gts", c_act, b_act, preferred_element_type=jnp.float32)

    def one_head(head):
        score = lax.dynamic_index_in_dim(scores, head // per_group, 0, keepdims=False)
        level = lax.dynamic_index_in_dim(cumul, head, 1, keepdims=False)
        stride = lax.dynamic_index_in_dim(delta, head, 1, keepdims=False)
        values = lax.dynamic_index_in_dim(x_act, head, 1, keepdims=False)
        spread = jnp.where(live, level[:, None] - level[None, :], 0.0)
        weights = jnp.where(live, score * jnp.exp(spread) * stride[None, :], 0.0).astype(
            jnp.bfloat16
        )
        return jnp.dot(weights, values, preferred_element_type=jnp.float32)

    intra = lax.map(one_head, jnp.arange(head_count, dtype=jnp.int32))
    intra = jnp.transpose(intra, (1, 0, 2))
    last_prompt = prompt_id[row_count - 1]
    final = cumul[row_count - 1]
    keep = (prompt_id == last_prompt)[:, None]
    fade = jnp.where(keep, jnp.exp(jnp.where(keep, final[None, :] - cumul, 0.0)), 0.0)
    inputs = (x_act.astype(jnp.float32) * (delta * fade)[:, :, None]).astype(jnp.bfloat16)
    grouped = inputs.reshape(row_count, group_count, per_group, width)
    ends = jnp.einsum("sgkp,sgn->gkpn", grouped, b_act, preferred_element_type=jnp.float32)
    ends = ends.reshape(head_count, width, state)
    last_start = lax.dynamic_index_in_dim(start_loc, last_prompt, 0, keepdims=False)
    inside = last_start >= 0
    base = lax.dynamic_index_in_dim(
        before_sum, jnp.clip(last_start, 0, row_count - 1), 0, keepdims=False
    )
    carry_in = jnp.exp(jnp.where(inside, final - base, 0.0))
    prefix_last = lax.dynamic_index_in_dim(prefixes, last_prompt, 0, keepdims=False)
    ends = ends + jnp.where(inside, carry_in[:, None, None] * prefix_last, 0.0)
    opens = jnp.any((start_loc >= 0) & (start_loc < row_count))
    through = jnp.where(opens, 0.0, jnp.exp(final))
    return (intra, ends, through, cumul, before_sum)


def span_init(c_act, incoming, prefixes, prompt_id, start_loc, cumul, before_sum):
    row_count, group_count, state = c_act.shape
    prompt_count, head_count, width = (prefixes.shape[0], prefixes.shape[1], prefixes.shape[2])
    per_group = head_count // group_count
    c_wide = c_act.astype(jnp.float32)
    total = jnp.zeros((row_count, head_count, width), jnp.float32)
    for prompt in range(prompt_count):
        begin = start_loc[prompt]
        start_state = jnp.where(begin >= 0, prefixes[prompt], incoming)
        grouped = start_state.reshape(group_count, per_group, width, state)
        reads = jnp.einsum("tgn,gkpn->tgkp", c_wide, grouped, precision=lax.Precision.HIGHEST)
        reads = reads.reshape(row_count, head_count, width)
        base = lax.dynamic_index_in_dim(
            before_sum, jnp.clip(begin, 0, row_count - 1), 0, keepdims=False
        )
        member = (prompt_id == prompt)[:, None]
        fade = jnp.where(member, jnp.exp(jnp.where(member, cumul - base[None, :], 0.0)), 0.0)
        total = total + fade[:, :, None] * reads
    return total


def combine_states(earlier, later):
    return (earlier[0] * later[0], later[0][:, None, None] * earlier[1] + later[1])


def on_device(
    x_mant,
    x_codes,
    bc_raw,
    gate_z,
    conv_x,
    conv_bc,
    dt_raw,
    a_log,
    d_skip,
    norm_gain,
    prompt_lengths,
    cache_slot,
    prefix_state,
    tail_x,
    tail_bc,
):
    row_count = x_mant.shape[0]
    head_count = a_log.shape[0]
    width = x_mant.shape[1] // head_count
    state = prefix_state.shape[2]
    slot_count = prefix_state.shape[0]
    lag_count = tail_x.shape[1]
    prompt_count = prompt_lengths.shape[0]
    heads_group = HEADS // GROUPS
    group_here = max(1, head_count // heads_group)
    per_group = head_count // group_here
    group_cols = GROUPS * state
    ctx_place = lax.axis_index("ctx")
    head_place = lax.axis_index("head")
    offset = ctx_place * row_count
    first_group = head_place * head_count // heads_group
    starts = jnp.cumsum(prompt_lengths) - prompt_lengths
    start_loc = starts - offset
    prompt_id = prompt_rows(starts, offset, row_count)
    x_wide = dequant(x_mant, x_codes)
    x_exact = x_wide.astype(jnp.bfloat16)
    b_first = first_group * state
    c_first = group_cols + first_group * state
    take_cols = group_here * state
    bc_here = jnp.concatenate(
        [
            lax.dynamic_slice_in_dim(bc_raw, b_first, take_cols, 1),
            lax.dynamic_slice_in_dim(bc_raw, c_first, take_cols, 1),
        ],
        axis=1,
    )
    weight_bc = jnp.concatenate(
        [
            lax.dynamic_slice_in_dim(conv_bc, b_first, take_cols, 1),
            lax.dynamic_slice_in_dim(conv_bc, c_first, take_cols, 1),
        ],
        axis=1,
    )
    tail_here = jnp.concatenate(
        [
            lax.dynamic_slice_in_dim(tail_bc, b_first, take_cols, 2),
            lax.dynamic_slice_in_dim(tail_bc, c_first, take_cols, 2),
        ],
        axis=2,
    )
    previous_x, previous_bc = passed_along(
        (x_exact[row_count - lag_count :], bc_here[row_count - lag_count :]), "ctx", 1
    )

    def fetch_one(prompt, buffer_set):
        slot_here = lax.dynamic_index_in_dim(cache_slot, prompt, 0, keepdims=False)
        owner_rank = slot_here // slot_count
        local_index = slot_here % slot_count
        pieces = (
            lax.dynamic_index_in_dim(prefix_state, local_index, 0, keepdims=False),
            lax.dynamic_index_in_dim(tail_x, local_index, 0, keepdims=False),
            lax.dynamic_index_in_dim(tail_here, local_index, 0, keepdims=False),
        )
        arrived = (
            from_root(pieces[0], "ctx", owner_rank),
            from_root(pieces[1], "ctx", owner_rank),
            from_root(pieces[2], "ctx", owner_rank),
        )
        return tuple(
            (
                lax.dynamic_update_index_in_dim(holder, piece, prompt, 0)
                for holder, piece in zip(buffer_set, arrived)
            )
        )

    empty_set = (
        jnp.zeros((prompt_count,) + prefix_state.shape[1:], jnp.bfloat16),
        jnp.zeros((prompt_count,) + tail_x.shape[1:], jnp.bfloat16),
        jnp.zeros((prompt_count,) + tail_here.shape[1:], jnp.bfloat16),
    )
    fetched_state, fetched_x, fetched_bc = lax.fori_loop(0, prompt_count, fetch_one, empty_set)
    prefixes = fetched_state.astype(jnp.float32).reshape(prompt_count, head_count, width, state)
    tails_x = fetched_x.astype(jnp.float32)
    tails_bc = fetched_bc.astype(jnp.float32)
    conv_out = causal_conv(
        x_wide, previous_x.astype(jnp.float32), tails_x, conv_x, prompt_id, start_loc
    )
    x_act = jax.nn.silu(conv_out).astype(jnp.bfloat16).reshape(row_count, head_count, width)
    bc_out = causal_conv(
        bc_here.astype(jnp.float32),
        previous_bc.astype(jnp.float32),
        tails_bc,
        weight_bc,
        prompt_id,
        start_loc,
    )
    bc_act = jax.nn.silu(bc_out).astype(jnp.bfloat16)
    b_act = bc_act[:, :take_cols].reshape(row_count, group_here, state)
    c_act = bc_act[:, take_cols:].reshape(row_count, group_here, state)
    delta = jax.nn.softplus(dt_raw)
    log_decay = -jnp.exp(a_log)[None, :] * delta
    intra, ends, through, cumul, before_sum = span_local(
        x_act, b_act, c_act, delta, log_decay, prompt_id, start_loc, prefixes
    )
    identity = (jnp.ones_like(through), jnp.zeros_like(ends))
    _, incoming = entering((through, ends), "ctx", combine_states, identity)
    init = span_init(c_act, incoming, prefixes, prompt_id, start_loc, cumul, before_sum)
    y_full = intra + init + d_skip[None, :, None] * x_act.astype(jnp.float32)
    gated = y_full * jax.nn.silu(gate_z.astype(jnp.float32).reshape(row_count, head_count, width))
    head_squares = jnp.sum(gated * gated, axis=2)
    local_squares = jnp.sum(head_squares.reshape(row_count, group_here, per_group), axis=2)
    all_groups = lax.dynamic_update_slice_in_dim(
        jnp.zeros((row_count, GROUPS), jnp.float32), local_squares, first_group, 1
    )
    summed = lax.psum(all_groups, "head")
    group_totals = lax.dynamic_slice_in_dim(summed, first_group, group_here, 1)
    inverse = lax.rsqrt(group_totals / (heads_group * width) + eps_norm)
    inverse = jnp.repeat(inverse, per_group, axis=1)
    mixed = gated * inverse[:, :, None] * norm_gain.reshape(head_count, width)[None, :, :]
    return mixed.reshape(row_count, head_count * width).astype(jnp.bfloat16)


def solution(mesh):
    in_specs = (
        P("ctx", "head"),
        P("ctx", "head"),
        P("ctx", None),
        P("ctx", "head"),
        P(None, "head"),
        P(),
        P("ctx", "head"),
        P("head"),
        P("head"),
        P("head"),
        P(),
        P(),
        P("ctx", "head", None),
        P("ctx", None, "head"),
        P("ctx", None, None),
    )
    out_specs = P("ctx", "head")
    return jax.shard_map(
        on_device, mesh=mesh, in_specs=in_specs, out_specs=out_specs, check_vma=False
    )
```

profile of v0, /device:TPU:1, one launch (start us, length us, event | category | flops | bytes accessed | tf_op | source)
XLA Modules:
  0.0 824.8 jit_solution(14115373180927704455)
XLA Ops:
  8.2 4.6 collective-permute-start
  15.5 1.9 collective-permute-start.1
  19.0 1.3 and_reduce_fusion
  26.2 1.2 compare_and_fusion.3
  32.4 1.2 slice_bitcast_fusion
  36.6 558.6 %while.44 = (s32[]{:T(128)}, bf16[4,1024,128]{2,1,0:T(8,128)(2,1)S(1)}, bf16[4,3,1024]{2,1,0:T(4,128)(2,1)S(1)}, bf16[4,3,256]{2,1,0:T(4,128)(2,1)S(1)}, s32[4]{...) while((s32[]{:T(128)}, ...), condition=%wide.region_7.8_spmd, body=%wide.region_3.7_spmd.sunk | while | flops 269851 | bytes 2673102 | solution.py:239
  36.6 1.2 dynamic_slice.204
  40.5 1.7 dynamic-slice_select_fusion.6
  42.2 121.7 %all-reduce.2 = (bf16[1,3,1024]{2,1,0:T(4,128)(2,1)S(1)}, bf16[1,3,256]{2,1,0:T(4,128)(2,1)S(1)}) all-reduce(bf16[1,3,1024]{2,1,0:T(4,128)(2,1)S(1)} %dynamic-slice_select_fusion.7, bf16[1,3,256]{2,1,0:T(4,128)(2,1)S(1)} %dynamic-slice_select_fusion.8), channel_id=1, replica_groups=mesh['head'=16,'ctx'=32] {'ctx'}, use_global_device_ids=true, to_apply=%region_5.5 | all-reduce | flops 3840 | bytes 15360 | tf_op jit(solution)/shard_map/while/body/eval_jaxpr/psum | solution.py:21
  164.0 14.4 %all-reduce.5.cloned.1.call-done = bf16[1,1024,128]{2,1,0:T(8,128)(2,1)} async-done(((bf16[1,1024,128]{2,1,0:T(8,128)(2,1)}), bf16[1,1024,128]{2,1,0:T(8,128)(2,1)}) %all-reduce.5.cloned.1.call-update) | async-done | bytes 262160 | tf_op jit(solution)/shard_map/while/body/eval_jaxpr/psum | solution.py:21
  179.4 1.2 dynamic_slice.204
  183.3 1.7 dynamic-slice_select_fusion.6
  185.0 122.3 %all-reduce.2 = (bf16[1,3,1024]{2,1,0:T(4,128)(2,1)S(1)}, bf16[1,3,256]{2,1,0:T(4,128)(2,1)S(1)}) all-reduce(bf16[1,3,1024]{2,1,0:T(4,128)(2,1)S(1)} %dynamic-slice_select_fusion.7, bf16[1,3,256]{2,1,0:T(4,128)(2,1)S(1)} %dynamic-slice_select_fusion.8), channel_id=1, replica_groups=mesh['head'=16,'ctx'=32] {'ctx'}, use_global_device_ids=true, to_apply=%region_5.5 | all-reduce | flops 3840 | bytes 15360 | tf_op jit(solution)/shard_map/while/body/eval_jaxpr/psum | solution.py:21
  307.3 9.7 %all-reduce.5.cloned.1.call-done = bf16[1,1024,128]{2,1,0:T(8,128)(2,1)} async-done(((bf16[1,1024,128]{2,1,0:T(8,128)(2,1)}), bf16[1,1024,128]{2,1,0:T(8,128)(2,1)}) %all-reduce.5.cloned.1.call-update) | async-done | bytes 262160 | tf_op jit(solution)/shard_map/while/body/eval_jaxpr/psum | solution.py:21
  318.1 1.2 dynamic_slice.204
  321.9 1.7 dynamic-slice_select_fusion.6
  323.7 122.3 %all-reduce.2 = (bf16[1,3,1024]{2,1,0:T(4,128)(2,1)S(1)}, bf16[1,3,256]{2,1,0:T(4,128)(2,1)S(1)}) all-reduce(bf16[1,3,1024]{2,1,0:T(4,128)(2,1)S(1)} %dynamic-slice_select_fusion.7, bf16[1,3,256]{2,1,0:T(4,128)(2,1)S(1)} %dynamic-slice_select_fusion.8), channel_id=1, replica_groups=mesh['head'=16,'ctx'=32] {'ctx'}, use_global_device_ids=true, to_apply=%region_5.5 | all-reduce | flops 3840 | bytes 15360 | tf_op jit(solution)/shard_map/while/body/eval_jaxpr/psum | solution.py:21
  446.0 9.7 %all-reduce.5.cloned.1.call-done = bf16[1,1024,128]{2,1,0:T(8,128)(2,1)} async-done(((bf16[1,1024,128]{2,1,0:T(8,128)(2,1)}), bf16[1,1024,128]{2,1,0:T(8,128)(2,1)}) %all-reduce.5.cloned.1.call-update) | async-done | bytes 262160 | tf_op jit(solution)/shard_map/while/body/eval_jaxpr/psum | solution.py:21
  456.7 1.2 dynamic_slice.204
  460.6 1.7 dynamic-slice_select_fusion.6
  462.3 122.3 %all-reduce.2 = (bf16[1,3,1024]{2,1,0:T(4,128)(2,1)S(1)}, bf16[1,3,256]{2,1,0:T(4,128)(2,1)S(1)}) all-reduce(bf16[1,3,1024]{2,1,0:T(4,128)(2,1)S(1)} %dynamic-slice_select_fusion.7, bf16[1,3,256]{2,1,0:T(4,128)(2,1)S(1)} %dynamic-slice_select_fusion.8), channel_id=1, replica_groups=mesh['head'=16,'ctx'=32] {'ctx'}, use_global_device_ids=true, to_apply=%region_5.5 | all-reduce | flops 3840 | bytes 15360 | tf_op jit(solution)/shard_map/while/body/eval_jaxpr/psum | solution.py:21
  584.6 9.7 %all-reduce.5.cloned.1.call-done = bf16[1,1024,128]{2,1,0:T(8,128)(2,1)} async-done(((bf16[1,1024,128]{2,1,0:T(8,128)(2,1)}), bf16[1,1024,128]{2,1,0:T(8,128)(2,1)}) %all-reduce.5.cloned.1.call-update) | async-done | bytes 262160 | tf_op jit(solution)/shard_map/while/body/eval_jaxpr/psum | solution.py:21
  596.9 1.6 gather_fusion.4
  598.5 1.6 gather_fusion.5
  600.1 1.4 gather_fusion.2
  601.5 1.6 gather_fusion.6
  603.1 1.4 gather_fusion.3
  604.5 1.6 gather_fusion.7
  607.4 1.5 multiply_convert_fusion.3
  609.5 3.8 multiply_convert_fusion.1
  613.3 1.8 copy.93
  615.1 2.0 fusion.31
  620.3 1.5 copy.89
  621.8 1.5 copy.94
  623.3 1.5 copy.95
  627.7 1.3 mul.333
  629.1 23.7 %all-gather = f32[32,1,16]{2,1,0:T(1,128)} all-gather(f32[1,1,16]{2,1,0:T(1,128)} %get-tuple-element.529), channel_id=1, replica_groups=mesh['head'=16,'ctx'=32] {'ctx'}, dimensions={0}, use_global_device_ids=true | all-gather | bytes 2112 | tf_op jit(solution)/shard_map/all_gather | solution.py:26
  654.2 73.1 %while.45 = (s32[]{:T(128)}, f32[16,128,64]{1,2,0:T(8,128)}, f32[1,128,128]{2,1,0:T(8,128)S(1)}, s32[16]{0:T(128)S(1)}, f32[128,16]{0,1:T(8,128)}, /*index=5*/f3...) while((s32[]{:T(128)}, f32[16,128,64]{1,2,0:T(8,128)}, ...), condition=%wide.region_10.13_spmd.clone, body=%wide.region_9.12_spmd.clone.sunk | while | flops 2244613 | bytes 119971 | solution.py:100
  657.2 1.6 fusion.107
  661.8 1.6 fusion.107
  666.4 1.6 fusion.107
  670.9 1.6 fusion.107
  675.5 1.6 fusion.107
  680.1 1.6 fusion.107
  684.7 1.6 fusion.107
  689.2 1.6 fusion.107
  693.8 1.6 fusion.107
  698.4 1.6 fusion.107
  702.9 1.6 fusion.107
  707.5 1.6 fusion.107
  712.1 1.6 fusion.107
  716.6 1.6 fusion.107
  721.2 1.6 fusion.107
  725.8 1.6 fusion.107
  727.3 59.8 %while.46 = (s32[]{:T(128)}, f32[16,64,128]{2,1,0:T(8,128)S(1)}, s32[]{:T(128)}, f32[32,16]{1,0:T(8,128)}, f32[32,16,64,128]{3,2,1,0:T(8,128)}, /*index=5*/s32[]{:T(128)}, s32[]{:T(128)}) while((s32[]{:T(128)}, f32[16,64,128]{2,1,0:T(8,128)S(1)}, s32[]{:T(128)}, f32[32,16]{1,0:T(8,128)}, f32[32,16,64,128]{3,2,1,0:T(8,128)}, ...), condition=%wide.region_13.16_spmd.clone, body=%wide.region_12.15_spmd.clone.sunk | while | flops 524292 | bytes 1573161 | solution.py:38
  728.0 1.2 fusion.108
  729.9 1.2 fusion.108
  731.8 1.2 fusion.108
  733.6 1.2 fusion.108
  769.1 1.2 fusion.108
  776.6 1.2 fusion.108
  787.1 1.4 fusion.25
  790.1 1.7 multiply_reduce_fusion
  791.8 24.8 %psum.49 = f32[128,8]{0,1:T(8,128)S(1)} all-reduce(f32[128,8]{0,1:T(8,128)S(1)} %dynamic_update_slice.40), channel_id=1, replica_groups=mesh['head'=16,'ctx'=32] {'head'}, use_global_device_ids=true, to_apply=%region_15.18 | all-reduce | flops 1024 | bytes 8192 | tf_op jit(solution)/shard_map/psum | solution.py:273
  (194 shorter events, 101.5 us)
Async XLA Ops:
  8.2 599.2 %collective-permute-start = (bf16[3,256]{1,0:T(4,128)(2,1)S(1)}, bf16[3,256]{1,0:T(4,128)(2,1)S(1)}, u32[]{:S(2)}, u32[]{:S(2)}) collective-permute-start(bf16[3,256]{1,0:T(4,128)(2,1)S(1)} %fusion.77), channel_id=1, source_target_pairs={{0,1},{1,2},{2,3},{3,4},{4,5},{5,6},{6,7},{7,8},{8,9},{9,10},{10,1... | collective-permute-start | bytes 4616 | tf_op jit(solution)/shard_map/ppermute | solution.py:16
  14.8 0.8 copy-start
  15.5 593.3 %collective-permute-start.1 = (bf16[3,1024]{1,0:T(4,128)(2,1)}, bf16[3,1024]{1,0:T(4,128)(2,1)}, u32[]{:S(2)}, u32[]{:S(2)}) collective-permute-start(bf16[3,1024]{1,0:T(4,128)(2,1)} %slice.281), channel_id=1, source_target_pairs={{0,1},{1,2},{2,3},{3,4},{4,5},{5,6},{6,7},{7,8},{8,9},{9,10},{10,1... | collective-permute-start | bytes 18440 | tf_op jit(solution)/shard_map/ppermute | solution.py:16
  20.4 5.1 copy-start.3
  36.6 141.7 %all-reduce.5.cloned.1.call-start = ((), (), s32[]{:S(2)}) async-start(), calls=%async_computation.1 | async-start | bytes 524288 | tf_op jit(solution)/shard_map/while/body/eval_jaxpr/psum | solution.py:21
  179.4 137.6 %all-reduce.5.cloned.1.call-start = ((), (), s32[]{:S(2)}) async-start(), calls=%async_computation.1 | async-start | bytes 524288 | tf_op jit(solution)/shard_map/while/body/eval_jaxpr/psum | solution.py:21
  318.0 137.6 %all-reduce.5.cloned.1.call-start = ((), (), s32[]{:S(2)}) async-start(), calls=%async_computation.1 | async-start | bytes 524288 | tf_op jit(solution)/shard_map/while/body/eval_jaxpr/psum | solution.py:21
  456.7 137.6 %all-reduce.5.cloned.1.call-start = ((), (), s32[]{:S(2)}) async-start(), calls=%async_computation.1 | async-start | bytes 524288 | tf_op jit(solution)/shard_map/while/body/eval_jaxpr/psum | solution.py:21
  595.3 132.1 %all-gather.3.cloned.1.call-start = ((), (), s32[]{:S(2)}) async-start(), calls=%async_computation | async-start | bytes 17301504 | tf_op jit(solution)/shard_map/all_gather | solution.py:26
  654.2 162.5 %copy-start.2 = (f32[16,64]{1,0:T(8,128)S(1)}, f32[16,64]{1,0:T(8,128)}, u32[]{:S(2)}) copy-start(f32[16,64]{1,0:T(8,128)} %mul.333) | copy-start | bytes 12292
  727.3 62.7 %copy-start.1 = (bf16[128,16,64]{0,2,1:T(8,128)(2,1)}, bf16[128,16,64]{0,2,1:T(8,128)(2,1)S(1)}, u32[]{:S(2)}) copy-start(bf16[128,16,64]{0,2,1:T(8,128)(2,1)S(1)} %get-tuple-element.805) | copy-start | bytes 786436
Sparse Core Ops, SparseCore 0:
  42.3 136.0 all-reduce.4
  185.1 131.8 all-reduce.4
  323.8 131.8 all-reduce.4
  462.4 131.8 all-reduce.4
Sparse Core Ops, SparseCore 1:
  617.2 88.0 all-gather.2
where the time goes:
time: 835 us; the launch traced here: 825 us
  blocking collectives  537 us (64%)
  local copies, waits for them, and re-layouts  83.4 us (10%)
  other arithmetic  60.6 us (7%)
  waiting for transfers between devices  43.6 us (5%)
  loops' own time  38.6 us (5%)
  matrix products  32 us (4%)
  between operations  23 us (3%)
    psum x4, blocking collectives, from_root(): return lax.psum(kept, axis)  489 us
    psum x4, waiting for transfers between devices, from_root(): return lax.psum(kept, axis)  43.5 us
    select_n x32, other arithmetic, hop(): return jax.tree.map(lambda a, b: jnp.where(reached, a, b), new, before)  37.4 us
    another operation x1, loops' own time, span_local(): intra = lax.map(one_head, jnp.arange(head_count, dtype=jnp.int32))  27.3 us
    dot_general x16, matrix products, one_head(): return jnp.dot(weights, values, preferred_element_type=jnp.float32)  25.3 us
    psum x1, blocking collectives, on_device(): summed = lax.psum(all_groups, 'head')  24.8 us
    all_gather x1, blocking collectives, entering(): everything = jax.tree.map(lambda part: lax.all_gather(part, axis), array)  23.7 us
    mul x32, local copies, waits for them, and re-layouts, combine_states(): later[0][:, None, None] * earlier[1] + later[1]  21.8 us
  transfers between devices with their start and end apart: 7, of which 4 were waited for; matrix products, arithmetic and copies ran while one was open for 12% of the time, Pallas kernels for 0%

commit v1 on v0

v1 whole, which is shorter than its diff:
```python
import jax
import jax.numpy as jnp
from jax import lax
from jax.experimental import pallas as pl
from jax.experimental.pallas import tpu as pltpu
from jax.sharding import PartitionSpec as P

BF = jnp.bfloat16
F32 = jnp.float32
HIGH = lax.Precision.HIGHEST
INTERPRET = False

TOK = 128
WIDTH = 64
STATE = 128
MXB = 32
LAGS = 3
PROMPTS = 4
HEADS_GROUP = 32
SLOTS_HERE = 2
EPS = 1e-05
FAR = -1e30

TAIL_AT = 64
PREV_AT = 124
DECAY_AT = 154
ROWS0 = 160


def call(kernel, out_shape, **kw):
    return pl.pallas_call(
        kernel,
        out_shape=out_shape,
        interpret=INTERPRET,
        compiler_params=pltpu.CompilerParams(vmem_limit_bytes=48 * 1024 * 1024),
        **kw,
    )


def vmem():
    return pl.BlockSpec(memory_space=pltpu.VMEM)


def smem():
    return pl.BlockSpec(memory_space=pltpu.SMEM)


def starts_of(len_ref):
    found = [jnp.int32(0)]
    for p in range(PROMPTS - 1):
        found.append(found[-1] + len_ref[p])
    return found


def iota(shape, axis):
    return lax.broadcasted_iota(jnp.int32, shape, axis)


def row_starts(locs, token):
    first = jnp.full(token.shape, locs[0], jnp.int32)
    for p in range(1, PROMPTS):
        first = jnp.where(token >= locs[p], locs[p], first)
    return first


def softplus(v):
    return jnp.maximum(v, 0.0) + jnp.log1p(jnp.exp(-jnp.abs(v)))


def silu(v):
    return v / (1.0 + jnp.exp(-v))


def spread(per, count):
    shape = (count, count * per)
    return (iota(shape, 1) // per == iota(shape, 0)).astype(F32)


def wide_scale(codes):
    scale = jnp.exp2(codes.astype(F32)).astype(BF)
    return jnp.dot(scale, spread(MXB, codes.shape[1]).astype(BF), preferred_element_type=F32)


def group_cols(ref_load, group, groups):
    b_at = pl.multiple_of(group * STATE, STATE)
    c_at = pl.multiple_of((groups + group) * STATE, STATE)
    return jnp.concatenate([ref_load(b_at), ref_load(c_at)], axis=-1).astype(F32)


def pack_kernel(len_ref, dt_ref, alog_ref, prefix_ref, tx_ref, tbc_ref, xm_ref, xc_ref, bc_ref, out_ref):
    ctx = lax.axis_index("ctx")
    group = lax.axis_index("head") * dt_ref.shape[1] // HEADS_GROUP
    groups = bc_ref.shape[1] // (2 * STATE)
    devices, heads = out_ref.shape[0], dt_ref.shape[1]
    per_dev = prefix_ref.shape[1] // devices
    locs = [s - ctx * TOK for s in starts_of(len_ref)]
    last_start = jnp.int32(0)
    for loc in locs:
        last_start = jnp.where((loc >= 0) & (loc < TOK), loc, last_start)
    log_decay = -jnp.exp(alog_ref[...]) * softplus(dt_ref[...])
    rows = iota((TOK, heads), 0)
    decay = jnp.exp(jnp.sum(jnp.where(rows >= last_start, log_decay, 0.0), axis=0, keepdims=True))
    high = decay.astype(BF).astype(F32)
    mid = (decay - high).astype(BF).astype(F32)
    low = decay - high - mid
    tails = jnp.concatenate(
        [
            jnp.concatenate(
                [
                    tx_ref[s].astype(F32),
                    group_cols(lambda at: tbc_ref[s, :, pl.ds(at, STATE)], group, groups),
                ],
                axis=1,
            )
            for s in range(SLOTS_HERE)
        ],
        axis=0,
    )
    skip = xm_ref.shape[0] - LAGS
    x_last = xm_ref[...].astype(F32)[skip:] * wide_scale(xc_ref[...])[xc_ref.shape[0] - LAGS :]
    bc_last = group_cols(lambda at: bc_ref[:, pl.ds(at, STATE)], group, groups)[skip:]
    prev = jnp.concatenate([x_last, bc_last], axis=1)
    lanes = prev.shape[1] // STATE
    pieces = [tails[:, c * STATE : (c + 1) * STATE] for c in range(lanes)]
    pieces += [prev[:, c * STATE : (c + 1) * STATE] for c in range(lanes)]
    pieces.append(jnp.zeros((ROWS0 - DECAY_AT, STATE), F32))
    misc = jnp.concatenate(pieces, axis=0)
    body = misc[: ROWS0 - TAIL_AT - 16].astype(BF)
    foot = misc[ROWS0 - TAIL_AT - 16 :]
    at = iota(foot.shape, 0) + (ROWS0 - 16 - DECAY_AT)
    for k in range(devices):
        h = k * per_dev // WIDTH
        for s in range(SLOTS_HERE):
            out_ref[k, s * per_dev : (s + 1) * per_dev, :] = prefix_ref[s, k * per_dev : (k + 1) * per_dev, :]
        out_ref[k, TAIL_AT : ROWS0 - 16, :] = body
        tile = jnp.where(at == 0, high[:, h : h + 1], foot)
        tile = jnp.where(at == 1, mid[:, h : h + 1], tile)
        tile = jnp.where(at == 2, low[:, h : h + 1], tile)
        out_ref[k, ROWS0 - 16 :, :] = tile.astype(BF)


def block_kernel(
    len_ref,
    slot_ref,
    got_ref,
    xm_ref,
    xc_ref,
    bc_ref,
    wx_ref,
    wbc_ref,
    dt_ref,
    alog_ref,
    skip_ref,
    ends_ref,
    y_ref,
    c_ref,
    cw_ref,
    x_scr,
):
    ctx = lax.axis_index("ctx")
    heads = dt_ref.shape[1]
    chans = heads * WIDTH
    group = lax.axis_index("head") * heads // HEADS_GROUP
    groups = bc_ref.shape[1] // (2 * STATE)
    devices = got_ref.shape[0]
    all_chans = chans + 2 * STATE
    lanes = all_chans // STATE
    locs = [s - ctx * TOK for s in starts_of(len_ref)]

    x_scr[8:, :chans] = xm_ref[...].astype(F32) * wide_scale(xc_ref[...])
    x_scr[8:, chans:] = group_cols(lambda at: bc_ref[:, pl.ds(at, STATE)], group, groups)
    before = got_ref[(ctx + devices - 1) % devices].astype(F32)
    for c in range(lanes):
        x_scr[8 - LAGS : 8, c * STATE : (c + 1) * STATE] = before[PREV_AT + c * LAGS : PREV_AT + (c + 1) * LAGS]

    tails = []
    for p in range(PROMPTS):
        slot = slot_ref[p]
        from_owner = got_ref[slot // SLOTS_HERE].astype(F32)[TAIL_AT:PREV_AT]
        second = (jnp.zeros((LAGS, STATE), jnp.int32) + slot % SLOTS_HERE) == 1
        tails.append(
            jnp.concatenate(
                [
                    jnp.where(
                        second,
                        from_owner[c * 2 * LAGS + LAGS : (c + 1) * 2 * LAGS],
                        from_owner[c * 2 * LAGS : c * 2 * LAGS + LAGS],
                    )
                    for c in range(lanes)
                ],
                axis=1,
            )
        )
    tails.append(jnp.zeros((16 - PROMPTS * LAGS, all_chans), F32))
    tails = jnp.concatenate(tails, axis=0).astype(BF)

    token = iota((TOK, 16), 0)
    first = row_starts(locs, token)
    prompt = sum((token >= loc).astype(jnp.int32) for loc in locs) - 1
    taps = jnp.concatenate(
        [wx_ref[...], group_cols(lambda at: wbc_ref[:, pl.ds(at, STATE)], group, groups)], axis=1
    )
    conv = taps[LAGS : LAGS + 1] * x_scr[8:, :]
    for k in range(1, LAGS + 1):
        outside = token - k < first
        pick = outside & (iota((TOK, 16), 1) == prompt * LAGS + token - k - first + LAGS)
        tail_rows = jnp.dot(pick.astype(BF), tails, preferred_element_type=F32)
        value = jnp.where(outside[:, :1], tail_rows, x_scr[8 - k : 8 + TOK - k, :])
        conv = conv + taps[LAGS - k : LAGS - k + 1] * value
    act = silu(conv).astype(BF)
    x_act = act[:, :chans]
    b_act = act[:, chans : chans + STATE]
    c_act = act[:, chans + STATE :]
    c_ref[...] = c_act

    row, col = iota((TOK, TOK), 0), iota((TOK, TOK), 1)
    live = (col <= row) & (col >= row_starts(locs, row))
    delta = softplus(dt_ref[...])
    log_decay = -jnp.exp(alog_ref[...]) * delta
    within = jnp.dot(live.astype(F32), log_decay, precision=HIGH, preferred_element_type=F32)
    cw_ref[...] = within
    within_t = within.T
    delta_t = delta.T
    scores = lax.dot_general(c_act, b_act, (((1,), (1,)), ((), ())), preferred_element_type=F32)
    skip = jnp.dot(skip_ref[...], spread(WIDTH, heads), precision=HIGH, preferred_element_type=F32)
    left = iota((TOK, 2 * WIDTH), 1) < WIDTH
    for j in range(heads // 2):
        pair = []
        for h in (2 * j, 2 * j + 1):
            fade = jnp.exp(jnp.where(live, within[:, h : h + 1] - within_t[h : h + 1, :], FAR))
            pair.append((scores * fade * delta_t[h : h + 1, :]).astype(BF))
        at = slice(2 * j * WIDTH, 2 * (j + 1) * WIDTH)
        x_pair = x_act[:, at].astype(F32)
        both = jnp.concatenate([jnp.where(left, x_pair, 0.0), jnp.where(left, 0.0, x_pair)], axis=0)
        intra = jnp.dot(jnp.concatenate(pair, axis=1), both.astype(BF), preferred_element_type=F32)
        y_ref[:, at] = intra + skip[:, at] * x_pair

    token_h = iota((TOK, heads), 0)
    keep = token_h >= row_starts(locs, jnp.full((TOK, heads), TOK - 1, jnp.int32))
    to_end = delta * jnp.exp(jnp.where(keep, within[TOK - 1 :, :] - within, FAR))
    to_end = jnp.dot(to_end, spread(WIDTH, heads), precision=HIGH, preferred_element_type=F32)
    inputs = (x_act.astype(F32) * to_end).astype(BF)
    ends = lax.dot_general(inputs, b_act, (((0,), (0,)), ((), ())), preferred_element_type=F32)
    ends_ref[...] = ends.astype(BF)


def scan_kernel(len_ref, slot_ref, got_ref, ends_ref, out_ref):
    devices, rows = ends_ref.shape[0], ends_ref.shape[1]
    starts = starts_of(len_ref)
    blocks = [s // TOK for s in starts]
    prefixes = []
    for p in range(PROMPTS):
        slot = slot_ref[p]
        at = pl.multiple_of((slot % SLOTS_HERE) * rows, rows)
        prefixes.append(got_ref[slot // SLOTS_HERE, pl.ds(at, rows), :])
    wide = [piece.astype(F32) for piece in prefixes]
    state = jnp.zeros((rows, STATE), F32)
    for d in range(devices):
        out_ref[d, :rows, :] = state.astype(BF)
        out_ref[d, rows:, :] = jnp.zeros((out_ref.shape[1] - rows, STATE), BF)
        foot = got_ref[d, ROWS0 - 16 :, :].astype(F32)
        at = DECAY_AT - ROWS0 + 16
        decay = foot[at : at + 1] + foot[at + 1 : at + 2] + foot[at + 2 : at + 3]
        base = state
        for p in range(PROMPTS):
            base = jnp.where(blocks[p] == d, wide[p], base)
        state = decay * base + ends_ref[d].astype(F32)
    for p in range(PROMPTS):
        place = jnp.int32(1)
        for q in range(p):
            place = place + (blocks[q] == blocks[p]).astype(jnp.int32)
        out_ref[blocks[p], pl.ds(pl.multiple_of(place * rows, rows), rows), :] = prefixes[p]


def read_kernel(len_ref, got_ref, c_ref, cw_ref, y_ref, gate_ref, gated_ref, sq_ref):
    ctx = lax.axis_index("ctx")
    devices = got_ref.shape[0]
    heads = cw_ref.shape[1]
    chans = heads * WIDTH
    rows = chans // devices
    locs = [s - ctx * TOK for s in starts_of(len_ref)]
    token = iota((TOK, STATE), 0)
    place = sum(((loc >= 0) & (token >= loc)).astype(jnp.int32) for loc in locs)
    c_act = c_ref[...].astype(F32)
    reads = jnp.zeros((TOK, chans), F32)
    for j in range(got_ref.shape[1] // rows):
        state = got_ref[:, j * rows : (j + 1) * rows, :].reshape(chans, STATE)
        mine = jnp.where(place == j, c_act, 0.0).astype(BF)
        reads = reads + lax.dot_general(mine, state, (((1,), (1,)), ((), ())), preferred_element_type=F32)
    fade = jnp.dot(jnp.exp(cw_ref[...]), spread(WIDTH, heads), precision=HIGH, preferred_element_type=F32)
    gated = (y_ref[...] + fade * reads) * silu(gate_ref[...].astype(F32))
    gated_ref[...] = gated
    square = gated * gated
    part = square[:, :STATE]
    for c in range(1, chans // STATE):
        part = part + square[:, c * STATE : (c + 1) * STATE]
    sq_ref[...] = jnp.sum(part.T, axis=0, keepdims=True)


def norm_kernel(gated_ref, sq_ref, other_ref, gain_ref, out_ref):
    total = sq_ref[...] + other_ref[...]
    inverse = lax.rsqrt(total / (HEADS_GROUP * WIDTH) + EPS)
    inverse = jnp.broadcast_to(inverse, (TOK, TOK)).T
    for c in range(out_ref.shape[1] // TOK):
        at = slice(c * TOK, (c + 1) * TOK)
        out_ref[:, at] = (gated_ref[:, at] * inverse * gain_ref[:, at]).astype(BF)


def on_device(
    x_mant,
    x_codes,
    bc_raw,
    gate_z,
    conv_x,
    conv_bc,
    dt_raw,
    a_log,
    d_skip,
    norm_gain,
    prompt_lengths,
    cache_slot,
    prefix_state,
    tail_x,
    tail_bc,
):
    devices = lax.axis_size("ctx")
    head_devices = lax.axis_size("head")
    heads = a_log.shape[0]
    chans = heads * WIDTH
    rows = chans // devices
    a_row = a_log.reshape(1, heads)
    skip_row = d_skip.reshape(1, heads)
    gain_row = norm_gain.reshape(1, chans)

    def whole(array):
        return pl.BlockSpec(array.shape, lambda i: (0,) * array.ndim)

    last = TOK // 16 - 1
    send0 = call(
        pack_kernel,
        jax.ShapeDtypeStruct((devices, ROWS0, STATE), BF),
        grid=(1,),
        in_specs=[
            smem(),
            whole(dt_raw),
            whole(a_row),
            whole(prefix_state),
            whole(tail_x),
            whole(tail_bc),
            pl.BlockSpec((16, chans), lambda i: (last, 0)),
            pl.BlockSpec((16, x_codes.shape[1]), lambda i: (last, 0)),
            pl.BlockSpec((16, bc_raw.shape[1]), lambda i: (last, 0)),
        ],
        out_specs=pl.BlockSpec((devices, ROWS0, STATE), lambda i: (0, 0, 0)),
    )(prompt_lengths, dt_raw, a_row, prefix_state, tail_x, tail_bc, x_mant, x_codes, bc_raw)
    got0 = lax.all_to_all(send0, "ctx", 0, 0)

    ends, y_part, c_act, within = call(
        block_kernel,
        (
            jax.ShapeDtypeStruct((chans, STATE), BF),
            jax.ShapeDtypeStruct((TOK, chans), F32),
            jax.ShapeDtypeStruct((TOK, STATE), BF),
            jax.ShapeDtypeStruct((TOK, heads), F32),
        ),
        in_specs=[smem(), smem()] + [vmem()] * 9,
        out_specs=(vmem(),) * 4,
        scratch_shapes=[pltpu.VMEM((TOK + 8, chans + 2 * STATE), F32)],
    )(prompt_lengths, cache_slot, got0, x_mant, x_codes, bc_raw, conv_x, conv_bc, dt_raw, a_row, skip_row)
    got1 = lax.all_to_all(ends.reshape(devices, rows, STATE), "ctx", 0, 0)

    send2 = call(
        scan_kernel,
        jax.ShapeDtypeStruct((devices, PROMPTS * rows, STATE), BF),
        in_specs=[smem(), smem(), vmem(), vmem()],
        out_specs=vmem(),
    )(prompt_lengths, cache_slot, got0, got1)
    got2 = lax.all_to_all(send2, "ctx", 0, 0)

    gated, squares = call(
        read_kernel,
        (jax.ShapeDtypeStruct((TOK, chans), F32), jax.ShapeDtypeStruct((1, TOK), F32)),
        in_specs=[smem()] + [vmem()] * 5,
        out_specs=(vmem(), vmem()),
    )(prompt_lengths, got2, c_act, within, y_part, gate_z)
    other = lax.ppermute(squares, "head", [(i, i ^ 1) for i in range(head_devices)])
    return call(
        norm_kernel,
        jax.ShapeDtypeStruct((TOK, chans), BF),
        in_specs=[vmem()] * 4,
        out_specs=vmem(),
    )(gated, squares, other, gain_row)


def solution(mesh):
    in_specs = (
        P("ctx", "head"),
        P("ctx", "head"),
        P("ctx", None),
        P("ctx", "head"),
        P(None, "head"),
        P(),
        P("ctx", "head"),
        P("head"),
        P("head"),
        P("head"),
        P(),
        P(),
        P("ctx", "head", None),
        P("ctx", None, "head"),
        P("ctx", None, None),
    )
    out_specs = P("ctx", "head")
    return jax.shard_map(
        on_device, mesh=mesh, in_specs=in_specs, out_specs=out_specs, check_vma=False
    )
```

time: 835 us -> 82.1 us (0.10); the launches traced: 825 us -> 81.5 us
  blocking collectives: 537 us -> 63 us
  local copies, waits for them, and re-layouts: 83.4 us -> 7.46 us
  other arithmetic: 60.6 us -> 0 us
  waiting for transfers between devices: 43.6 us -> 1.97 us
  loops' own time: 38.6 us -> 0 us
  matrix products: 32 us -> 0 us
  between operations: 23 us -> 0.11 us
    psum x5 -> x0, blocking collectives: 513 us -> none  [the longest x4 489 us: from_root(): return lax.psum(kept, axis)]
    all_to_all x0 -> x3, blocking collectives: none -> 63 us  [the longest x1 30 us: on_device(): got0 = lax.all_to_all(send0, 'ctx', 0, 0)]
    select_n x45 -> x0, other arithmetic: 45.1 us -> none  [the longest x32 37.4 us: hop(): return jax.tree.map(lambda a, b: jnp.where(reached, a, b), new, before)]
    psum x4 -> x0, waiting for transfers between devices: 43.5 us -> none  [from_root(): return lax.psum(kept, axis)]
    another operation x3 -> x0, loops' own time: 38.6 us -> none  [the longest x1 27.3 us: span_local(): intra = lax.map(one_head, jnp.arange(head_count, dtype=jnp.int32))]
    dot_general x22 -> x0, matrix products: 32 us -> none  [the longest x16 25.3 us: one_head(): return jnp.dot(weights, values, preferred_element_type=jnp.float32)]
    mul x38 -> x0, local copies, waits for them, and re-layouts: 24.5 us -> none  [the longest x32 21.8 us: combine_states(): later[0][:, None, None] * earlier[1] + later[1]]
    all_gather x1 -> x0, blocking collectives: 23.7 us -> none  [entering(): everything = jax.tree.map(lambda part: lax.all_gather(part, axis), array)]
  transfers between devices with their start and end apart: 7 -> 1, of which waited for: 4 -> 1; matrix products, arithmetic and copies ran while one was open for 12% -> 0% of each run, Pallas kernels for 0% -> 0%
where the time goes in v1:
time: 82.1 us; the launch traced here: 81.5 us
  blocking collectives  63 us (77%)
  local copies, waits for them, and re-layouts  7.46 us (9%)
  Pallas kernels  6.65 us (8%)
  starting transfers between devices  2.31 us (3%)
  waiting for transfers between devices  1.97 us (2%)
    all_to_all x1, blocking collectives, on_device(): got0 = lax.all_to_all(send0, 'ctx', 0, 0)  30 us
    all_to_all x1, blocking collectives, on_device(): got2 = lax.all_to_all(send2, 'ctx', 0, 0)  20.5 us
    all_to_all x1, blocking collectives, on_device(): got1 = lax.all_to_all(ends.reshape(devices, rows, STATE), 'ctx', 0, 0)  12.5 us
    unnamed x28, local copies, waits for them, and re-layouts  7.46 us
    pallas_call x1, Pallas kernels, on_device(): call(block_kernel, (jax.ShapeDtypeStruct((chans, STATE), BF), jax.ShapeDt...  2.78 us
    ppermute x1, starting transfers between devices, on_device(): lax.ppermute(squares, 'head', [(i, i ^ 1) for i in range(head_devices)])  2.31 us
    ppermute x1, waiting for transfers between devices, on_device(): lax.ppermute(squares, 'head', [(i, i ^ 1) for i in range(head_devices)])  1.97 us
  transfers between devices with their start and end apart: 1, of which 1 were waited for; matrix products, arithmetic and copies ran while one was open for 0% of the time, Pallas kernels for 0%

profile of v1, /device:TPU:1, one launch (start us, length us, event | category | flops | bytes accessed | tf_op | source)
XLA Modules:
  0.0 81.5 jit_solution(13800566520022743445)
XLA Ops:
  0.0 0.7 copy.17.tx_ref
  0.7 0.8 copy.18.tbc_ref
  1.5 0.8 %copy.19.xc_ref = s32[128,32]{1,0:T(8,128)S(1)} copy(s32[128,32]{0,1:T(8,128)} %param.16) | data formatting | bytes 32768 | tf_op args[1]
  2.3 0.8 copy.16.dt_ref
  3.1 0.0 copy-start
  3.1 1.0 %copy-done = bf16[128,2048]{1,0:T(8,128)(2,1)S(1)} copy-done((bf16[128,2048]{1,0:T(8,128)(2,1)S(1)}, bf16[128,2048]{1,0:T(8,128)(2,1)}, u32[]{:S(2)}) %copy-start) | copy-done | bytes 524312
  4.1 0.0 copy-start.1
  4.1 0.9 %copy-done.1 = bf16[128,1024]{1,0:T(8,128)(2,1)S(1)} copy-done((bf16[128,1024]{1,0:T(8,128)(2,1)S(1)}, bf16[128,1024]{1,0:T(8,128)(2,1)}, u32[]{:S(2)}) %copy-start.1) | copy-done | bytes 262168
  5.1 0.0 copy-start.2
  5.1 1.0 %copy-done.2 = bf16[2,1024,128]{2,1,0:T(8,128)(2,1)S(1)} copy-done((bf16[2,1024,128]{2,1,0:T(8,128)(2,1)S(1)}, bf16[2,1024,128]{2,1,0:T(8,128)(2,1)}, u32[]{:S(2)}) %copy-start.2) | copy-done | bytes 524312
  6.1 0.0 copy-start.6
  6.1 0.7 copy-done.6
  6.8 0.0 copy-start.9
  6.8 0.7 copy-done.9
  7.4 0.7 shard_map.145
  8.2 0.0 copy-start.4
  8.2 0.0 copy-start.5
  8.2 0.0 copy-start.10
  8.2 0.0 copy-start.11
  8.2 30.0 %all_to_all.15.got_ref = bf16[32,160,128]{2,1,0:T(8,128)(2,1)S(1)} all-to-all(bf16[32,160,128]{2,1,0:T(8,128)(2,1)S(1)} %shard_map.145), channel_id=1, replica_groups=mesh['head'=16,'ctx'=32] {'ctx'}, dimensions={0} | all-to-all | bytes 2621440 | tf_op jit(solution)/shard_map/all_to_all | solution.py:356
  38.2 0.0 copy-done.4
  38.2 0.0 copy-done.5
  38.2 0.0 copy-done.10
  38.2 0.0 copy-done.11
  38.2 0.0 copy-start.7
  38.2 2.8 %shard_map.146 = (bf16[1024,128]{1,0:T(8,128)(2,1)S(1)}, f32[128,1024]{1,0:T(8,128)S(1)}, bf16[128,128]{1,0:T(8,128)(2,1)S(1)}, f32[128,16]{1,0:T(8,128)S(1)}) custom-call(s32[4]{0:T(128)S(1)} %copy-done.6, s32[4]{0:T(128)S(1)} %copy-done.10, bf16[32,160,128]{2,1,0:T(8,128)(2,1)S(1)} %all_to_all.15.got_ref, bf16[128,1024]{1,0:T(8,128)(2,1)S(1)} %copy-done.1, ...), custom_call_target="tpu_custom_call" | custom-call | tf_op jit(solution)/shard_map/pallas_call | solution.py:358
  41.0 12.5 %all_to_all.16.ends_ref = bf16[32,32,128]{2,1,0:T(8,128)(2,1)S(1)} all-to-all(bf16[32,32,128]{2,1,0:T(8,128)(2,1)S(1)} %bitcast.4), channel_id=1, replica_groups=mesh['head'=16,'ctx'=32] {'ctx'}, dimensions={0} | all-to-all | bytes 524288 | tf_op jit(solution)/shard_map/all_to_all | solution.py:370
  53.5 0.0 copy-done.7
  53.5 0.8 shard_map.147
  54.3 0.0 copy-start.3
  54.3 20.5 %all_to_all.17.got_ref = bf16[32,128,128]{2,1,0:T(8,128)(2,1)S(1)} all-to-all(bf16[32,128,128]{2,1,0:T(8,128)(2,1)S(1)} %shard_map.147), channel_id=1, replica_groups=mesh['head'=16,'ctx'=32] {'ctx'}, dimensions={0} | all-to-all | bytes 2097152 | tf_op jit(solution)/shard_map/all_to_all | solution.py:378
  74.8 0.0 copy-start.8
  74.8 0.0 copy-done.3
  74.8 1.5 %shard_map.148 = (f32[128,1024]{1,0:T(8,128)S(1)}, f32[1,128]{1,0:T(1,128)S(1)}) custom-call(s32[4]{0:T(128)S(1)} %copy-done.7, bf16[32,128,128]{2,1,0:T(8,128)(2,1)S(1)} %all_to_all.17.got_ref, bf16[128,128]{1,0:T(8,128)(2,1)S(1)} %get-tuple-element.12.c_ref, f32[128,16]{1,0:T(8,128)S(1)} %get-tuple-element.13.cw_ref, ...), custom_call_target="tpu_custom_call" | custom-call | tf_op jit(solution)/shard_map/pallas_call | solution.py:380
  76.3 2.3 %collective-permute-start = (f32[1,128]{1,0:T(1,128)S(1)}, f32[1,128]{1,0:T(1,128)S(1)}, u32[]{:S(2)}, u32[]{:S(2)}) collective-permute-start(f32[1,128]{1,0:T(1,128)S(1)} %get-tuple-element.16.sq_ref), channel_id=1, source_target_pairs={{0,32},{32,0},{64,96},{96,64},{128,160},{160,128},{192,224},{224,1... | collective-permute-start | bytes 1544 | tf_op jit(solution)/shard_map/ppermute | solution.py:386
  78.6 2.0 %collective-permute-done.other_ref = f32[1,128]{1,0:T(1,128)S(1)} collective-permute-done((f32[1,128]{1,0:T(1,128)S(1)}, f32[1,128]{1,0:T(1,128)S(1)}, u32[]{:S(2)}, u32[]{:S(2)}) %collective-permute-start) | collective-permute-done | bytes 544 | tf_op jit(solution)/shard_map/ppermute | solution.py:386
  80.6 0.0 copy-done.8
  80.6 0.8 %shard_map.149 = bf16[128,1024]{1,0:T(8,128)(2,1)} custom-call(f32[128,1024]{1,0:T(8,128)S(1)} %get-tuple-element.15.gated_ref, f32[1,128]{1,0:T(1,128)S(1)} %get-tuple-element.16.sq_ref, f32[1,128]{1,0:T(1,128)S(1)} %collective-permute-done.other_ref, f32[1,1024]{1,0:T(1,128)S(1)} %bitcast.5), custom_call_target="tpu_custom_call" | custom-call | tf_op jit(solution)/shard_map/pallas_call | solution.py:387
Async XLA Ops:
  3.1 1.0 %copy-start = (bf16[128,2048]{1,0:T(8,128)(2,1)S(1)}, bf16[128,2048]{1,0:T(8,128)(2,1)}, u32[]{:S(2)}) copy-start(bf16[128,2048]{1,0:T(8,128)(2,1)} %bc_ref.3) | copy-start | bytes 1572868
  4.1 0.9 %copy-start.1 = (bf16[128,1024]{1,0:T(8,128)(2,1)S(1)}, bf16[128,1024]{1,0:T(8,128)(2,1)}, u32[]{:S(2)}) copy-start(bf16[128,1024]{1,0:T(8,128)(2,1)} %xm_ref.3) | copy-start | bytes 786436
  5.1 1.0 %copy-start.2 = (bf16[2,1024,128]{2,1,0:T(8,128)(2,1)S(1)}, bf16[2,1024,128]{2,1,0:T(8,128)(2,1)}, u32[]{:S(2)}) copy-start(bf16[2,1024,128]{2,1,0:T(8,128)(2,1)} %prefix_ref.1) | copy-start | bytes 1572868
  6.1 0.7 copy-start.6
  6.8 0.7 copy-start.9
  8.2 30.0 %copy-start.4 = (f32[4,2048]{1,0:T(4,128)S(1)}, f32[4,2048]{1,0:T(4,128)}, u32[]{:S(2)}) copy-start(f32[4,2048]{1,0:T(4,128)} %wbc_ref.1) | copy-start | bytes 98308
  8.2 30.0 %copy-start.5 = (f32[4,1024]{1,0:T(4,128)S(1)}, f32[4,1024]{1,0:T(4,128)}, u32[]{:S(2)}) copy-start(f32[4,1024]{1,0:T(4,128)} %wx_ref.1) | copy-start | bytes 49156
  8.2 30.0 %copy-start.10 = (s32[4]{0:T(128)S(1)}, s32[4]{0:T(128)}, u32[]{:S(2)}) copy-start(s32[4]{0:T(128)} %slot_ref.3) | copy-start | bytes 52
  8.2 30.0 %copy-start.11 = (f32[16]{0:T(128)S(1)}, f32[16]{0:T(128)}, u32[]{:S(2)}) copy-start(f32[16]{0:T(128)} %param.23) | copy-start | bytes 196
  38.2 15.3 %copy-start.7 = (s32[4]{0:T(128)S(1)}, s32[4]{0:T(128)}, u32[]{:S(2)}) copy-start(s32[4]{0:T(128)} %len_ref.7) | copy-start | bytes 52
  54.3 20.5 %copy-start.3 = (bf16[128,1024]{1,0:T(8,128)(2,1)S(1)}, bf16[128,1024]{1,0:T(8,128)(2,1)}, u32[]{:S(2)}) copy-start(bf16[128,1024]{1,0:T(8,128)(2,1)} %gate_ref.1) | copy-start | bytes 786436
  74.8 5.8 %copy-start.8 = (f32[1024]{0:T(1024)S(1)}, f32[1024]{0:T(1024)}, u32[]{:S(2)}) copy-start(f32[1024]{0:T(1024)} %param.24) | copy-start | bytes 12292
  76.3 4.3 %collective-permute-start = (f32[1,128]{1,0:T(1,128)S(1)}, f32[1,128]{1,0:T(1,128)S(1)}, u32[]{:S(2)}, u32[]{:S(2)}) collective-permute-start(f32[1,128]{1,0:T(1,128)S(1)} %get-tuple-element.16.sq_ref), channel_id=1, source_target_pairs={{0,32},{32,0},{64,96},{96,64},{128,160},{160,128},{192,224},{224,1... | collective-permute-start | bytes 1544 | tf_op jit(solution)/shard_map/ppermute | solution.py:386

commit v2 on v1

v2 whole, which is shorter than its diff:
```python
import jax
import jax.numpy as jnp
from jax import lax
from jax.experimental import pallas as pl
from jax.experimental.pallas import tpu as pltpu
from jax.sharding import PartitionSpec as P

BF = jnp.bfloat16
F32 = jnp.float32
HIGH = lax.Precision.HIGHEST
INTERPRET = False

TOK = 128
WIDTH = 64
STATE = 128
MXB = 32
LAGS = 3
PROMPTS = 4
HEADS_GROUP = 32
SLOTS_HERE = 2
EPS = 1e-05
FAR = -1e30

PREFIX_AT = 32
XB_AT = 96
BB_AT = 104
XP_AT = 112
XT_AT = 124
BP_AT = 130
BT_AT = 142
CT_AT = 148
CP_AT = 154
ROWS1 = 160
DECAY_LANE = LAGS + PROMPTS * LAGS
WINDOWS = 40


def call(kernel, out_shape, **kw):
    return pl.pallas_call(
        kernel,
        out_shape=out_shape,
        interpret=INTERPRET,
        compiler_params=pltpu.CompilerParams(vmem_limit_bytes=48 * 1024 * 1024),
        **kw,
    )


def vmem():
    return pl.BlockSpec(memory_space=pltpu.VMEM)


def hbm():
    return pl.BlockSpec(memory_space=pltpu.HBM)


def smem():
    return pl.BlockSpec(memory_space=pltpu.SMEM)


def starts_of(len_ref):
    found = [jnp.int32(0)]
    for p in range(PROMPTS - 1):
        found.append(found[-1] + len_ref[p])
    return found


def iota(shape, axis):
    return lax.broadcasted_iota(jnp.int32, shape, axis)


def row_starts(locs, token):
    first = jnp.full(token.shape, locs[0], jnp.int32)
    for p in range(1, PROMPTS):
        first = jnp.where(token >= locs[p], locs[p], first)
    return first


def softplus(v):
    return jnp.maximum(v, 0.0) + jnp.log1p(jnp.exp(-jnp.abs(v)))


def silu(v):
    return v / (1.0 + jnp.exp(-v))


def spread(per, count):
    shape = (count, count * per)
    return (iota(shape, 1) // per == iota(shape, 0)).astype(F32)


def group_cols(load, group, groups):
    b_at = pl.multiple_of(group * STATE, STATE)
    c_at = pl.multiple_of((groups + group) * STATE, STATE)
    return load(b_at).astype(F32), load(c_at).astype(F32)


def nt_dot(a, b, **kw):
    return lax.dot_general(a, b, (((1,), (1,)), ((), ())), preferred_element_type=F32, **kw)


def live_matrix(locs):
    row, col = iota((TOK, TOK), 0), iota((TOK, TOK), 1)
    return (col <= row) & (col >= row_starts(locs, row))


def widen(per_head_t, per):
    return jnp.dot(
        per_head_t.T, spread(per, per_head_t.shape[0]), precision=HIGH, preferred_element_type=F32
    )


def block_kernel(*refs):
    (len_hbm, dt_hbm, alog_hbm, xc_hbm, xm_hbm, bc_hbm, tx_hbm, tbc_hbm, wx_hbm, wbc_hbm, prefix_hbm) = refs[:11]
    out_ref, act_ref, within_ref = refs[11:14]
    (len_ref, dt_ref, alog_ref, xc_ref, xm_ref, bc_ref, tx_ref, tbc_ref, wx_ref, wbc_ref) = refs[14:24]
    x_scr, sems = refs[24:]
    rows = PREFIX_AT
    copies = [
        pltpu.make_async_copy(src, dst, sems.at[n])
        for n, (src, dst) in enumerate(
            [
                (len_hbm, len_ref),
                (dt_hbm, dt_ref),
                (alog_hbm, alog_ref),
                (xc_hbm, xc_ref),
                (xm_hbm, xm_ref),
                (bc_hbm, bc_ref),
                (tx_hbm, tx_ref),
                (tbc_hbm, tbc_ref),
                (wx_hbm, wx_ref),
                (wbc_hbm, wbc_ref),
            ]
            + [
                (prefix_hbm.at[s], out_ref.at[:, pl.ds(PREFIX_AT + s * rows, rows), :])
                for s in range(SLOTS_HERE)
            ]
        )
    ]
    for copy in copies:
        copy.start()
    for copy in copies[:10]:
        copy.wait()

    ctx = lax.axis_index("ctx")
    heads = dt_ref.shape[0]
    chans = heads * WIDTH
    group = lax.axis_index("head") * heads // HEADS_GROUP
    groups = bc_ref.shape[1] // (2 * STATE)
    devices = out_ref.shape[0]
    starts = starts_of(len_ref)
    locs = [s - ctx * TOK for s in starts]

    scale = jnp.exp2(xc_ref[...].astype(F32)).T.astype(BF)
    wide = jnp.dot(scale, spread(MXB, xc_ref.shape[0]).astype(BF), preferred_element_type=F32)
    x = xm_ref[...].astype(F32) * wide
    b_raw, c_raw = group_cols(lambda at: bc_ref[:, pl.ds(at, STATE)], group, groups)
    x_scr[8:, :chans] = x
    x_scr[8:, chans:] = b_raw
    x_scr[:8, :] = jnp.zeros((8, chans + STATE), F32)

    live = live_matrix(locs)
    delta = softplus(dt_ref[...])
    log_decay = -jnp.exp(alog_ref[...].T) * delta
    within = nt_dot(log_decay, live.astype(F32), precision=HIGH)
    within_ref[...] = within
    token = iota((heads, TOK), 1)
    first = row_starts(locs, token)
    last_start = row_starts(locs, jnp.full((heads, TOK), TOK - 1, jnp.int32))
    to_end = delta * jnp.exp(jnp.where(token >= last_start, within[:, TOK - 1 :] - within, FAR))
    regular = (token >= LAGS) & (token - first >= LAGS)
    factor = widen(jnp.where(regular, to_end, 0.0), WIDTH)

    w_b, _ = group_cols(lambda at: wbc_ref[:, pl.ds(at, STATE)], group, groups)
    taps = jnp.concatenate([wx_ref[...], w_b], axis=1)
    conv = taps[LAGS : LAGS + 1] * x_scr[8:, :]
    for k in range(1, LAGS + 1):
        conv = conv + taps[LAGS - k : LAGS - k + 1] * x_scr[8 - k : 8 + TOK - k, :]
    act = silu(conv).astype(BF)
    act_ref[...] = act[:, :chans]
    inputs = (act[:, :chans].astype(F32) * factor).astype(BF)
    ends = lax.dot_general(
        inputs, act[:, chans:], (((0,), (0,)), ((), ())), preferred_element_type=F32
    ).astype(BF)

    entry = iota((16, TOK), 0)
    begin = jnp.full((16, TOK), -TOK, jnp.int32)
    for p in range(PROMPTS):
        for i in range(LAGS):
            at = jnp.where(len_ref[p] > i, locs[p] + i, -TOK)
            begin = jnp.where(entry == p * LAGS + i, at, begin)
    chosen = iota((16, TOK), 1) == begin
    raw = jnp.concatenate([x, b_raw], axis=1).astype(BF)
    at_start = jnp.dot(chosen.astype(BF), raw, preferred_element_type=F32)[: PROMPTS * LAGS]
    lane = iota((heads, TOK), 1)
    at_block = jnp.where((token < LAGS) & (token - first >= LAGS), to_end, 0.0)
    vals = nt_dot(to_end, chosen.astype(F32), precision=HIGH)[:, : PROMPTS * LAGS]
    vals = jnp.concatenate(
        [at_block[:, :LAGS], vals, jnp.exp(within[:, TOK - 1 :]), jnp.zeros((heads, TOK - 16), F32)], axis=1
    )
    high = vals.astype(BF).astype(F32)
    low = vals - high

    tails = jnp.concatenate([tx_ref[i].astype(F32) for i in range(LAGS)], axis=0)
    tails = jnp.concatenate(
        [tails[i * SLOTS_HERE + s : i * SLOTS_HERE + s + 1] for s in range(SLOTS_HERE) for i in range(LAGS)], axis=0
    )
    tails_b, tails_c = [], []
    for s in range(SLOTS_HERE):
        for i in range(LAGS):
            b_one, c_one = group_cols(lambda at: tbc_ref[i, :, pl.ds(at, STATE)], group, groups)
            tails_b.append(b_one[s : s + 1])
            tails_c.append(c_one[s : s + 1])
    gap = jnp.zeros((2, STATE), F32)
    b_tile = jnp.concatenate([b_raw[:LAGS], gap, b_raw[TOK - LAGS :]], axis=0)
    foot = jnp.concatenate(
        [at_start[:, chans:]] + tails_b + tails_c + [c_raw[TOK - LAGS :], jnp.zeros((ROWS1 - CP_AT - LAGS, STATE), F32)],
        axis=0,
    )
    for k in range(devices):
        out_ref[k, :rows, :] = ends[k * rows : (k + 1) * rows]
        lanes = slice(k * rows // STATE * STATE, (k * rows // STATE + 1) * STATE)
        h = k * rows // WIDTH
        x_tile = [x[:LAGS, lanes], high[h : h + 1], low[h : h + 1], x[TOK - LAGS :, lanes]]
        part = jnp.concatenate(
            x_tile + [b_tile, at_start[:, lanes], tails[:, lanes], foot], axis=0
        )
        out_ref[k, XB_AT:, :] = part.astype(BF)
    for copy in copies[10:]:
        copy.wait()


def scan_kernel(len_ref, slot_ref, got_ref, wx_ref, wbc_ref, out_ref, x_scr, b_scr, in_scr, mix_scr):
    devices = got_ref.shape[0]
    rows = PREFIX_AT
    ctx = lax.axis_index("ctx")
    chans = wx_ref.shape[1]
    group = lax.axis_index("head") * (chans // WIDTH) // HEADS_GROUP
    groups = wbc_ref.shape[1] // (2 * STATE)
    at = ctx * rows % STATE
    starts = starts_of(len_ref)
    blocks = [s // TOK for s in starts]

    x_scr[...] = got_ref[:, XB_AT : XB_AT + 8, :].astype(F32).reshape(devices * 8, STATE)
    b_scr[...] = got_ref[:, BB_AT : BB_AT + 8, :].astype(F32).reshape(devices * 8, STATE)
    factors = x_scr[pl.ds(LAGS, devices, stride=8), :] + x_scr[pl.ds(LAGS + 1, devices, stride=8), :]
    prompt_factors = jnp.sum(factors, axis=0, keepdims=True)

    def windows(scr, start_at, tail_at):
        before, now = [], []
        for p in range(PROMPTS):
            slot = slot_ref[p]
            own = got_ref[blocks[p], XB_AT:, :].astype(F32)
            after = got_ref[jnp.minimum(blocks[p] + 1, devices - 1), XB_AT:, :].astype(F32)
            after = jnp.where(blocks[p] + 1 < devices, after, 0.0)
            place = start_at - XB_AT + p * LAGS
            now.append((own + after)[place : place + LAGS])
            owner = got_ref[slot // SLOTS_HERE, XB_AT:, :].astype(F32)
            place = tail_at - XB_AT
            before.append(
                jnp.where(
                    slot % SLOTS_HERE == 1, owner[place + LAGS : place + 2 * LAGS], owner[place : place + LAGS]
                )
            )
        pad = jnp.zeros((WINDOWS - devices - PROMPTS, STATE), F32)
        found = []
        for i in range(LAGS):
            last = scr[pl.ds(8 - LAGS + i, devices, stride=8), :]
            last = jnp.concatenate([last[devices - 1 :], last[: devices - 1]], axis=0)
            found.append(jnp.concatenate([last] + [b[i : i + 1] for b in before] + [pad], axis=0))
        for i in range(LAGS):
            fresh = scr[pl.ds(i, devices, stride=8), :]
            found.append(jnp.concatenate([fresh] + [n[i : i + 1] for n in now] + [pad], axis=0))
        return found

    def activation(rows6, taps, i):
        conv = taps[LAGS : LAGS + 1] * rows6[LAGS + i]
        for k in range(1, LAGS + 1):
            conv = conv + taps[LAGS - k : LAGS - k + 1] * rows6[LAGS + i - k]
        return silu(conv).astype(BF).astype(F32)

    x_taps = wx_ref[:, pl.ds(pl.multiple_of(ctx * rows // STATE * STATE, STATE), STATE)]
    b_taps, _ = group_cols(lambda at: wbc_ref[:, pl.ds(at, STATE)], group, groups)
    x_rows = windows(x_scr, XP_AT, XT_AT)
    b_rows = windows(b_scr, BP_AT, BT_AT)
    x_act = [activation(x_rows, x_taps, i) for i in range(LAGS)]
    b_act = [activation(b_rows, b_taps, i) for i in range(LAGS)]
    scaled = []
    for i in range(LAGS):
        column = [factors[:, i : i + 1]]
        for p in range(PROMPTS):
            lane = LAGS + p * LAGS + i
            column.append(prompt_factors[:, lane : lane + 1])
        column.append(jnp.zeros((WINDOWS - devices - PROMPTS, 1), F32))
        scaled.append(x_act[i] * jnp.concatenate(column, axis=0))
    spare = jnp.zeros((STATE - LAGS * WINDOWS, STATE), F32)
    in_scr[...] = jnp.concatenate(scaled + [spare], axis=0).T
    mine = in_scr[pl.ds(pl.multiple_of(at, rows), rows), :]
    lane = iota((rows, STATE), 1)
    target = lane % WINDOWS
    for p in range(PROMPTS):
        for i in range(LAGS):
            target = jnp.where(lane == i * WINDOWS + devices + p, (starts[p] + i) // TOK, target)
    for d in range(devices):
        mix_scr[d * rows : (d + 1) * rows, :] = jnp.where(target == d, mine, 0.0).astype(BF)
    b_all = jnp.concatenate(b_act + [spare], axis=0).astype(BF)
    extra = jnp.dot(mix_scr[...], b_all, preferred_element_type=F32)

    turn = at // rows
    from_prompts = jnp.where(
        turn == 0, x_act[0][devices:], jnp.where(turn == 1, x_act[1][devices:], x_act[2][devices:])
    )
    pad = jnp.zeros((8 - LAGS, STATE), F32)

    prefixes = []
    for p in range(PROMPTS):
        slot = slot_ref[p]
        place = pl.multiple_of(PREFIX_AT + (slot % SLOTS_HERE) * rows, rows)
        prefixes.append(got_ref[slot // SLOTS_HERE, pl.ds(place, rows), :])
    wide = [piece.astype(F32) for piece in prefixes]
    state = jnp.zeros((rows, STATE), F32)
    states = PROMPTS * rows
    for d in range(devices):
        out_ref[d, :rows, :] = state.astype(BF)
        out_ref[d, rows:states, :] = jnp.zeros((states - rows, STATE), BF)
        from_block = jnp.concatenate([x_act[i][d : d + 1] for i in range(LAGS)] + [pad], axis=0)
        out_ref[d, states:, :] = jnp.where(turn == LAGS, from_block, from_prompts).astype(BF)
        base = state
        for p in range(PROMPTS):
            base = jnp.where(blocks[p] == d, wide[p], base)
        decay = factors[d : d + 1, DECAY_LANE : DECAY_LANE + 1]
        state = decay * base + (got_ref[d, :rows, :].astype(F32) + extra[d * rows : (d + 1) * rows])
    for p in range(PROMPTS):
        place = jnp.int32(1)
        for q in range(p):
            place = place + (blocks[q] == blocks[p]).astype(jnp.int32)
        out_ref[blocks[p], pl.ds(pl.multiple_of(place * rows, rows), rows), :] = prefixes[p]


def read_kernel(
    len_ref,
    slot_ref,
    sent_ref,
    got_ref,
    act_ref,
    bc_ref,
    wbc_ref,
    within_ref,
    dt_ref,
    skip_ref,
    gate_ref,
    gated_ref,
    sq_ref,
    bc_scr,
):
    ctx = lax.axis_index("ctx")
    devices = got_ref.shape[0]
    heads = dt_ref.shape[0]
    chans = heads * WIDTH
    rows = chans // devices
    group = lax.axis_index("head") * heads // HEADS_GROUP
    groups = bc_ref.shape[1] // (2 * STATE)
    locs = [s - ctx * TOK for s in starts_of(len_ref)]

    token = iota((TOK, 16), 0)
    entry = iota((TOK, 16), 1)
    first = row_starts(locs, token)
    prompt = sum((token >= loc).astype(jnp.int32) for loc in locs) - 1

    bc_scr[8:, :] = jnp.concatenate(group_cols(lambda at: bc_ref[:, pl.ds(at, STATE)], group, groups), axis=1)
    before = sent_ref[(ctx + devices - 1) % devices, XB_AT:, :].astype(F32)
    bc_scr[8 - LAGS : 8, :STATE] = before[BB_AT - XB_AT + 8 - LAGS : BB_AT - XB_AT + 8]
    bc_scr[8 - LAGS : 8, STATE:] = before[CP_AT - XB_AT : CP_AT - XB_AT + LAGS]
    tails = []
    for p in range(PROMPTS):
        owner = sent_ref[slot_ref[p] // SLOTS_HERE, XB_AT:, :].astype(F32)
        pair = []
        for place in (BT_AT - XB_AT, CT_AT - XB_AT):
            pair.append(
                jnp.where(
                    slot_ref[p] % SLOTS_HERE == 1,
                    owner[place + LAGS : place + 2 * LAGS],
                    owner[place : place + LAGS],
                )
            )
        tails.append(jnp.concatenate(pair, axis=1))
    tails.append(jnp.zeros((16 - PROMPTS * LAGS, 2 * STATE), F32))
    tails = jnp.concatenate(tails, axis=0).astype(BF)
    taps = jnp.concatenate(group_cols(lambda at: wbc_ref[:, pl.ds(at, STATE)], group, groups), axis=1)
    conv = taps[LAGS : LAGS + 1] * bc_scr[8:, :]
    for k in range(1, LAGS + 1):
        outside = token - k < first
        pick = outside & (entry == prompt * LAGS + token - k - first + LAGS)
        tail_rows = jnp.dot(pick.astype(BF), tails, preferred_element_type=F32)
        value = jnp.where(outside[:, :1], tail_rows, bc_scr[8 - k : 8 + TOK - k, :])
        conv = conv + taps[LAGS - k : LAGS - k + 1] * value
    bc_act = silu(conv).astype(BF)
    b_act, c_act = bc_act[:, :STATE], bc_act[:, STATE:]

    near = token - first < LAGS
    by_prompt = (prompt == entry % PROMPTS) & (token - first == entry // PROMPTS) & near
    by_block = (token == entry - LAGS * PROMPTS) & (token < LAGS) & jnp.logical_not(near)
    pick = by_prompt | by_block
    other = (near | (token < LAGS))[:, :1]
    per = STATE // rows
    states = PROMPTS * rows
    spec = []
    for c in range(chans // STATE):
        spec.append(
            jnp.concatenate(
                [got_ref[c * per + j, states:, :].astype(F32)[:PROMPTS] for j in range(per)], axis=0
            )
        )
    spec = jnp.concatenate(spec, axis=1).astype(BF)
    patch = jnp.dot(pick.astype(BF), spec, preferred_element_type=F32)
    x_wide = jnp.where(other, patch, act_ref[...].astype(F32))

    live = live_matrix(locs)
    delta = softplus(dt_ref[...])
    within = within_ref[...]
    within_c = within.T
    scores = nt_dot(c_act, b_act)
    place = iota((TOK, STATE), 0)
    place = sum(((loc >= 0) & (place >= loc)).astype(jnp.int32) for loc in locs)
    c_wide = c_act.astype(F32)
    reads = jnp.zeros((TOK, chans), F32)
    for j in range(PROMPTS):
        state = got_ref[:, j * rows : (j + 1) * rows, :].reshape(chans, STATE)
        reads = reads + nt_dot(jnp.where(place == j, c_wide, 0.0).astype(BF), state)
    y = widen(jnp.exp(within), WIDTH) * reads
    skip = jnp.dot(skip_ref[...], spread(WIDTH, heads), precision=HIGH, preferred_element_type=F32)
    left = iota((TOK, 2 * WIDTH), 1) < WIDTH
    part = jnp.zeros((TOK, TOK), F32)
    for j in range(heads // 2):
        pair = []
        for h in (2 * j, 2 * j + 1):
            fade = jnp.exp(jnp.where(live, within_c[:, h : h + 1] - within[h : h + 1, :], FAR))
            pair.append((scores * fade * delta[h : h + 1, :]).astype(BF))
        at = slice(2 * j * WIDTH, 2 * (j + 1) * WIDTH)
        x_pair = x_wide[:, at]
        both = jnp.concatenate([jnp.where(left, x_pair, 0.0), jnp.where(left, 0.0, x_pair)], axis=0)
        intra = jnp.dot(jnp.concatenate(pair, axis=1), both.astype(BF), preferred_element_type=F32)
        total = y[:, at] + (intra + skip[:, at] * x_pair)
        gated = total * silu(gate_ref[:, at].astype(F32))
        gated_ref[:, at] = gated
        part = part + gated * gated
    sq_ref[...] = jnp.sum(part.T, axis=0, keepdims=True)


def norm_kernel(gated_ref, sq_ref, other_ref, gain_ref, out_ref):
    total = sq_ref[...] + other_ref[...]
    inverse = lax.rsqrt(total / (HEADS_GROUP * WIDTH) + EPS)
    inverse = jnp.broadcast_to(inverse, (TOK, TOK)).T
    for c in range(out_ref.shape[1] // TOK):
        at = slice(c * TOK, (c + 1) * TOK)
        out_ref[:, at] = (gated_ref[:, at] * inverse * gain_ref[:, at]).astype(BF)


def on_device(
    x_mant,
    x_codes,
    bc_raw,
    gate_z,
    conv_x,
    conv_bc,
    dt_raw,
    a_log,
    d_skip,
    norm_gain,
    prompt_lengths,
    cache_slot,
    prefix_state,
    tail_x,
    tail_bc,
):
    devices = lax.axis_size("ctx")
    head_devices = lax.axis_size("head")
    heads = a_log.shape[0]
    chans = heads * WIDTH
    rows = chans // devices
    dt_t = dt_raw.T
    sources = [
        prompt_lengths,
        dt_t,
        a_log.reshape(1, heads),
        x_codes.T,
        x_mant,
        bc_raw,
        jnp.transpose(tail_x, (1, 0, 2)),
        jnp.transpose(tail_bc, (1, 0, 2)),
        conv_x,
        conv_bc,
    ]
    prefixes = prefix_state.reshape(SLOTS_HERE, devices, rows, STATE)
    send1, act, within = call(
        block_kernel,
        (
            jax.ShapeDtypeStruct((devices, ROWS1, STATE), BF),
            jax.ShapeDtypeStruct((TOK, chans), BF),
            jax.ShapeDtypeStruct((heads, TOK), F32),
        ),
        in_specs=[hbm()] * 11,
        out_specs=(vmem(),) * 3,
        scratch_shapes=[pltpu.SMEM((PROMPTS,), jnp.int32)]
        + [pltpu.VMEM(source.shape, source.dtype) for source in sources[1:]]
        + [pltpu.VMEM((TOK + 8, chans + STATE), F32), pltpu.SemaphoreType.DMA((12,))],
    )(*sources, prefixes)
    got1 = lax.all_to_all(send1, "ctx", 0, 0)

    send2 = call(
        scan_kernel,
        jax.ShapeDtypeStruct((devices, PROMPTS * rows + 8, STATE), BF),
        in_specs=[smem(), smem()] + [vmem()] * 3,
        out_specs=vmem(),
        scratch_shapes=[
            pltpu.VMEM((devices * 8, STATE), F32),
            pltpu.VMEM((devices * 8, STATE), F32),
            pltpu.VMEM((STATE, STATE), F32),
            pltpu.VMEM((chans, STATE), BF),
        ],
    )(prompt_lengths, cache_slot, got1, conv_x, conv_bc)
    got2 = lax.all_to_all(send2, "ctx", 0, 0)

    gated, squares = call(
        read_kernel,
        (jax.ShapeDtypeStruct((TOK, chans), F32), jax.ShapeDtypeStruct((1, TOK), F32)),
        in_specs=[smem(), smem()] + [vmem()] * 9,
        out_specs=(vmem(), vmem()),
        scratch_shapes=[pltpu.VMEM((TOK + 8, 2 * STATE), F32)],
    )(
        prompt_lengths,
        cache_slot,
        got1,
        got2,
        act,
        bc_raw,
        conv_bc,
        within,
        dt_t,
        d_skip.reshape(1, heads),
        gate_z,
    )
    other = lax.ppermute(squares, "head", [(i, i ^ 1) for i in range(head_devices)])
    return call(
        norm_kernel,
        jax.ShapeDtypeStruct((TOK, chans), BF),
        in_specs=[vmem()] * 4,
        out_specs=vmem(),
    )(gated, squares, other, norm_gain.reshape(1, chans))


def solution(mesh):
    in_specs = (
        P("ctx", "head"),
        P("ctx", "head"),
        P("ctx", None),
        P("ctx", "head"),
        P(None, "head"),
        P(),
        P("ctx", "head"),
        P("head"),
        P("head"),
        P("head"),
        P(),
        P(),
        P("ctx", "head", None),
        P("ctx", None, "head"),
        P("ctx", None, None),
    )
    out_specs = P("ctx", "head")
    return jax.shard_map(
        on_device, mesh=mesh, in_specs=in_specs, out_specs=out_specs, check_vma=False
    )
```

time: 82.1 us -> 72 us (0.88)
  blocking collectives: 63 us -> 51.9 us
  local copies, waits for them, and re-layouts: 7.46 us -> 8.71 us
    all_to_all x2 -> x1, blocking collectives: 42.4 us -> 29.9 us  [on_device(): got1 = lax.all_to_all(send1, 'ctx', 0, 0)]
    all_to_all x1, blocking collectives: 20.5 us -> 22 us  [on_device(): got2 = lax.all_to_all(send2, 'ctx', 0, 0)]
    unnamed x28 -> x34, local copies, waits for them, and re-layouts: 7.46 us -> 8.71 us
    pallas_call x3 -> x2, Pallas kernels: 4.32 us -> 3.28 us  [the longest x1 2.08 us: on_device(): call(block_kernel, (jax.ShapeDtypeStruct((devices, ROWS1, STATE), BF), ja...]
where the time goes in v2:
time: 72 us; the launch traced here: 71.3 us
  blocking collectives  51.9 us (72%)
  local copies, waits for them, and re-layouts  8.71 us (12%)
  Pallas kernels  6.36 us (9%)
  starting transfers between devices  2.3 us (3%)
  waiting for transfers between devices  1.98 us (3%)
    all_to_all x1, blocking collectives, on_device(): got1 = lax.all_to_all(send1, 'ctx', 0, 0)  29.9 us
    all_to_all x1, blocking collectives, on_device(): got2 = lax.all_to_all(send2, 'ctx', 0, 0)  22 us
    unnamed x34, local copies, waits for them, and re-layouts  8.71 us
    ppermute x1, starting transfers between devices, on_device(): lax.ppermute(squares, 'head', [(i, i ^ 1) for i in range(head_devices)])  2.3 us
    pallas_call x1, Pallas kernels, on_device(): call(read_kernel, (jax.ShapeDtypeStruct((TOK, chans), F32), jax.ShapeDtyp...  2.24 us
    pallas_call x1, Pallas kernels, on_device(): call(block_kernel, (jax.ShapeDtypeStruct((devices, ROWS1, STATE), BF), ja...  2.08 us
    ppermute x1, waiting for transfers between devices, on_device(): lax.ppermute(squares, 'head', [(i, i ^ 1) for i in range(head_devices)])  1.98 us
  transfers between devices with their start and end apart: 1, of which 1 were waited for; matrix products, arithmetic and copies ran while one was open for 0% of the time, Pallas kernels for 0%

profile of v2, /device:TPU:1, one launch (start us, length us, event | category | flops | bytes accessed | tf_op | source)
XLA Modules:
  0.0 71.3 jit_solution(7656922754189947378)
XLA Ops:
  0.0 0.0 copy-start
  0.0 1.0 %copy-done = bf16[128,2048]{1,0:T(8,128)(2,1)S(1)} copy-done((bf16[128,2048]{1,0:T(8,128)(2,1)S(1)}, bf16[128,2048]{1,0:T(8,128)(2,1)}, u32[]{:S(2)}) %copy-start) | copy-done | bytes 524312
  1.0 0.0 copy-start.2
  1.0 1.0 %copy-done.2 = bf16[2,1024,128]{2,1,0:T(8,128)(2,1)S(1)} copy-done((bf16[2,1024,128]{2,1,0:T(8,128)(2,1)S(1)}, bf16[2,1024,128]{2,1,0:T(8,128)(2,1)}, u32[]{:S(2)}) %copy-start.2) | copy-done | bytes 524312
  2.1 0.0 copy-start.3
  2.1 0.8 %copy-done.3 = f32[4,2048]{1,0:T(4,128)S(1)} copy-done((f32[4,2048]{1,0:T(4,128)S(1)}, f32[4,2048]{1,0:T(4,128)}, u32[]{:S(2)}) %copy-start.3) | copy-done | bytes 32792
  2.8 0.0 copy-start.5
  2.8 0.9 %copy-done.5 = bf16[128,1024]{1,0:T(8,128)(2,1)S(1)} copy-done((bf16[128,1024]{1,0:T(8,128)(2,1)S(1)}, bf16[128,1024]{1,0:T(8,128)(2,1)}, u32[]{:S(2)}) %copy-start.5) | copy-done | bytes 262168
  3.8 0.0 copy-start.7
  3.8 0.7 %copy-done.7 = f32[4,1024]{1,0:T(4,128)S(1)} copy-done((f32[4,1024]{1,0:T(4,128)S(1)}, f32[4,1024]{1,0:T(4,128)}, u32[]{:S(2)}) %copy-start.7) | copy-done | bytes 16408
  4.5 0.0 copy-start.8
  4.5 0.7 copy-done.8
  5.2 0.0 copy-start.9
  5.2 0.7 %copy-done.9 = bf16[2,3,2048]{2,0,1:T(2,128)(2,1)S(1)} copy-done((bf16[2,3,2048]{2,0,1:T(2,128)(2,1)S(1)}, bf16[2,3,2048]{2,0,1:T(2,128)(2,1)}, u32[]{:S(2)}) %copy-start.9) | copy-done | bytes 24600
  5.9 0.0 copy-start.10
  5.9 0.7 %copy-done.10 = s32[128,32]{0,1:T(8,128)S(1)} copy-done((s32[128,32]{0,1:T(8,128)S(1)}, s32[128,32]{0,1:T(8,128)}, u32[]{:S(2)}) %copy-start.10) | copy-done | bytes 16408
  6.7 0.0 copy-start.11
  6.7 0.7 copy-done.11
  7.4 0.0 copy-start.12
  7.4 0.7 copy-done.12
  8.0 0.0 copy-start.15
  8.0 0.7 copy-done.15
  8.7 2.1 %shard_map.145 = (bf16[32,160,128]{2,1,0:T(8,128)(2,1)S(1)}, bf16[128,1024]{1,0:T(8,128)(2,1)S(1)}, f32[16,128]{1,0:T(8,128)S(1)}) custom-call(s32[4]{0:T(128)S(1)} %copy-done.12, f32[16,128]{1,0:T(8,128)S(1)} %bitcast.9, f32[1,16]{1,0:T(1,128)S(1)} %bitcast.15, s32[32,128]{1,0:T(8,128)S(1)} %bitcast.12, bf16[128,1024]{1,0:T(8,128)(2,1)S(1)} %copy-done.5, ...), custom_call_target="tpu_custom_call" | custom-call | tf_op jit(solution)/shard_map/pallas_call | solution.py:494
  10.8 0.0 copy-start.14
  10.8 29.9 %all_to_all.10.got_ref.sent_ref = bf16[32,160,128]{2,1,0:T(8,128)(2,1)S(1)} all-to-all(bf16[32,160,128]{2,1,0:T(8,128)(2,1)S(1)} %get-tuple-element.10), channel_id=1, replica_groups=mesh['head'=16,'ctx'=32] {'ctx'}, dimensions={0} | all-to-all | bytes 2621440 | tf_op jit(solution)/shard_map/all_to_all | solution.py:507
  40.6 0.0 copy-done.14
  40.6 1.2 %shard_map.146 = bf16[32,136,128]{2,1,0:T(8,128)(2,1)S(1)} custom-call(s32[4]{0:T(128)S(1)} %copy-done.12, s32[4]{0:T(128)S(1)} %copy-done.14, bf16[32,160,128]{2,1,0:T(8,128)(2,1)S(1)} %all_to_all.10.got_ref.sent_ref, f32[4,1024]{1,0:T(4,128)S(1)} %copy-done.7, f32[4,2048]{1,0:T(4,128)S(1)} %copy-done.3), custom_call_target="tpu_custom_call" | custom-call | tf_op jit(solution)/shard_map/pallas_call | solution.py:509
  41.8 0.0 copy-start.1
  41.9 0.0 copy-start.4
  41.9 0.0 copy-start.6
  41.9 0.0 copy-start.16
  41.9 22.0 %all_to_all.11.got_ref = bf16[32,136,128]{2,1,0:T(8,128)(2,1)S(1)} all-to-all(bf16[32,136,128]{2,1,0:T(8,128)(2,1)S(1)} %shard_map.146), channel_id=1, replica_groups=mesh['head'=16,'ctx'=32] {'ctx'}, dimensions={0} | all-to-all | bytes 2228224 | tf_op jit(solution)/shard_map/all_to_all | solution.py:521
  63.9 0.0 copy-done.1
  63.9 0.0 copy-done.4
  63.9 0.0 copy-done.6
  63.9 0.0 copy-done.16
  63.9 0.0 copy-start.13
  63.9 2.2 %shard_map.147 = (f32[128,1024]{1,0:T(8,128)S(1)}, f32[1,128]{1,0:T(1,128)S(1)}) custom-call(s32[4]{0:T(128)S(1)} %copy-done.12, s32[4]{0:T(128)S(1)} %copy-done.14, bf16[32,160,128]{2,1,0:T(8,128)(2,1)S(1)} %all_to_all.10.got_ref.sent_ref, bf16[32,136,128]{2,1,0:T(8,128)(2,1)S(1)} %all_to_all.11.got_ref, bf16[128,1024]{1,0:T(8,128)(2,1)S(1)} %get-tuple-element.11.act_ref, ...), custom_call_target="tpu_custom_call" | custom-call | tf_op jit(solution)/shard_map/pallas_call | solution.py:523
  66.2 2.3 %collective-permute-start = (f32[1,128]{1,0:T(1,128)S(1)}, f32[1,128]{1,0:T(1,128)S(1)}, u32[]{:S(2)}, u32[]{:S(2)}) collective-permute-start(f32[1,128]{1,0:T(1,128)S(1)} %get-tuple-element.14.sq_ref), channel_id=1, source_target_pairs={{0,32},{32,0},{64,96},{96,64},{128,160},{160,128},{192,224},{224,1... | collective-permute-start | bytes 1544 | tf_op jit(solution)/shard_map/ppermute | solution.py:542
  68.5 2.0 %collective-permute-done.other_ref = f32[1,128]{1,0:T(1,128)S(1)} collective-permute-done((f32[1,128]{1,0:T(1,128)S(1)}, f32[1,128]{1,0:T(1,128)S(1)}, u32[]{:S(2)}, u32[]{:S(2)}) %collective-permute-start) | collective-permute-done | bytes 544 | tf_op jit(solution)/shard_map/ppermute | solution.py:542
  70.5 0.0 copy-done.13
  70.5 0.8 %shard_map.148 = bf16[128,1024]{1,0:T(8,128)(2,1)} custom-call(f32[128,1024]{1,0:T(8,128)S(1)} %get-tuple-element.13.gated_ref, f32[1,128]{1,0:T(1,128)S(1)} %get-tuple-element.14.sq_ref, f32[1,128]{1,0:T(1,128)S(1)} %collective-permute-done.other_ref, f32[1,1024]{1,0:T(1,128)S(1)} %bitcast.14), custom_call_target="tpu_custom_call" | custom-call | tf_op jit(solution)/shard_map/pallas_call | solution.py:543
Async XLA Ops:
  0.0 1.0 %copy-start = (bf16[128,2048]{1,0:T(8,128)(2,1)S(1)}, bf16[128,2048]{1,0:T(8,128)(2,1)}, u32[]{:S(2)}) copy-start(bf16[128,2048]{1,0:T(8,128)(2,1)} %bc_ref.1) | copy-start | bytes 1572868
  1.0 1.0 %copy-start.2 = (bf16[2,1024,128]{2,1,0:T(8,128)(2,1)S(1)}, bf16[2,1024,128]{2,1,0:T(8,128)(2,1)}, u32[]{:S(2)}) copy-start(bf16[2,1024,128]{2,1,0:T(8,128)(2,1)} %param.27) | copy-start | bytes 1572868
  2.1 0.8 %copy-start.3 = (f32[4,2048]{1,0:T(4,128)S(1)}, f32[4,2048]{1,0:T(4,128)}, u32[]{:S(2)}) copy-start(f32[4,2048]{1,0:T(4,128)} %wbc_ref.3) | copy-start | bytes 98308
  2.8 0.9 %copy-start.5 = (bf16[128,1024]{1,0:T(8,128)(2,1)S(1)}, bf16[128,1024]{1,0:T(8,128)(2,1)}, u32[]{:S(2)}) copy-start(bf16[128,1024]{1,0:T(8,128)(2,1)} %refs_4_.1) | copy-start | bytes 786436
  3.8 0.7 %copy-start.7 = (f32[4,1024]{1,0:T(4,128)S(1)}, f32[4,1024]{1,0:T(4,128)}, u32[]{:S(2)}) copy-start(f32[4,1024]{1,0:T(4,128)} %wx_ref.1) | copy-start | bytes 49156
  4.5 0.7 copy-start.8
  5.2 0.7 %copy-start.9 = (bf16[2,3,2048]{2,0,1:T(2,128)(2,1)S(1)}, bf16[2,3,2048]{2,0,1:T(2,128)(2,1)}, u32[]{:S(2)}) copy-start(bf16[2,3,2048]{2,0,1:T(2,128)(2,1)} %param.29) | copy-start | bytes 73732
  5.9 0.7 %copy-start.10 = (s32[128,32]{0,1:T(8,128)S(1)}, s32[128,32]{0,1:T(8,128)}, u32[]{:S(2)}) copy-start(s32[128,32]{0,1:T(8,128)} %param.16) | copy-start | bytes 49156
  6.7 0.7 copy-start.11
  7.4 0.7 copy-start.12
  8.0 0.7 copy-start.15
  10.8 29.9 %copy-start.14 = (s32[4]{0:T(128)S(1)}, s32[4]{0:T(128)}, u32[]{:S(2)}) copy-start(s32[4]{0:T(128)} %slot_ref.3) | copy-start | bytes 52
  41.8 22.1 %copy-start.1 = (bf16[128,2048]{1,0:T(8,128)(2,1)S(1)}, bf16[128,2048]{1,0:T(8,128)(2,1)}, u32[]{:S(2)}) copy-start(bf16[128,2048]{1,0:T(8,128)(2,1)} %bc_ref.1) | copy-start | bytes 1572868
  41.9 22.1 %copy-start.4 = (f32[4,2048]{1,0:T(4,128)S(1)}, f32[4,2048]{1,0:T(4,128)}, u32[]{:S(2)}) copy-start(f32[4,2048]{1,0:T(4,128)} %wbc_ref.3) | copy-start | bytes 98308
  41.9 22.0 %copy-start.6 = (bf16[128,1024]{1,0:T(8,128)(2,1)S(1)}, bf16[128,1024]{1,0:T(8,128)(2,1)}, u32[]{:S(2)}) copy-start(bf16[128,1024]{1,0:T(8,128)(2,1)} %gate_ref.1) | copy-start | bytes 786436
  41.9 22.0 %copy-start.16 = (f32[16]{0:T(128)S(1)}, f32[16]{0:T(128)}, u32[]{:S(2)}) copy-start(f32[16]{0:T(128)} %param.23) | copy-start | bytes 196
  63.9 6.5 %copy-start.13 = (f32[1024]{0:T(1024)S(1)}, f32[1024]{0:T(1024)}, u32[]{:S(2)}) copy-start(f32[1024]{0:T(1024)} %param.24) | copy-start | bytes 12292
  66.2 4.3 %collective-permute-start = (f32[1,128]{1,0:T(1,128)S(1)}, f32[1,128]{1,0:T(1,128)S(1)}, u32[]{:S(2)}, u32[]{:S(2)}) collective-permute-start(f32[1,128]{1,0:T(1,128)S(1)} %get-tuple-element.14.sq_ref), channel_id=1, source_target_pairs={{0,32},{32,0},{64,96},{96,64},{128,160},{160,128},{192,224},{224,1... | collective-permute-start | bytes 1544 | tf_op jit(solution)/shard_map/ppermute | solution.py:542

commit v3 on v2

--- a/solution.py
+++ b/solution.py
@@ -1,3 +1,5 @@
+import functools
+
 import jax
 import jax.numpy as jnp
 from jax import lax
@@ -21,16 +23,26 @@
 EPS = 1e-05
 FAR = -1e30
 
-PREFIX_AT = 32
-XB_AT = 96
-BB_AT = 104
-XP_AT = 112
-XT_AT = 124
-BP_AT = 130
-BT_AT = 142
-CT_AT = 148
-CP_AT = 154
-ROWS1 = 160
+
+class Plan:
+    def __init__(self, slots, prompts):
+        self.slots, self.prompts = slots, prompts
+        at = 32
+        self.prefix, at = at, at + 32 * slots
+        self.xb, at = at, at + 8
+        self.bb, at = at, at + 8
+        self.xp, at = at, at + LAGS * prompts
+        self.xt, at = at, at + LAGS * slots
+        self.bp, at = at, at + LAGS * prompts
+        self.bt, at = at, at + LAGS * slots
+        self.ct, at = at, at + LAGS * slots
+        self.cp, at = at, at + LAGS
+        self.used = at
+        self.rows = (at + 7) // 8 * 8
+
+
+SMALL = Plan(1, 2)
+FULL = Plan(SLOTS_HERE, PROMPTS)
 DECAY_LANE = LAGS + PROMPTS * LAGS
 WINDOWS = 40
 
@@ -53,6 +65,10 @@
     return pl.BlockSpec(memory_space=pltpu.HBM)
 
 
+def pinned(array):
+    return array if INTERPRET else pltpu.with_memory_space_constraint(array, pltpu.HBM)
+
+
 def smem():
     return pl.BlockSpec(memory_space=pltpu.SMEM)
 
@@ -109,45 +125,85 @@
     )
 
 
-def block_kernel(*refs):
-    (len_hbm, dt_hbm, alog_hbm, xc_hbm, xm_hbm, bc_hbm, tx_hbm, tbc_hbm, wx_hbm, wbc_hbm, prefix_hbm) = refs[:11]
-    out_ref, act_ref, within_ref = refs[11:14]
-    (len_ref, dt_ref, alog_ref, xc_ref, xm_ref, bc_ref, tx_ref, tbc_ref, wx_ref, wbc_ref) = refs[14:24]
-    x_scr, sems = refs[24:]
-    rows = PREFIX_AT
+def small_enough(starts, slot_ref):
+    fits = jnp.int32(1)
+    for p in range(PROMPTS - 2):
+        crowded = (starts[p + 1] - 1) // TOK == starts[p + 2] // TOK
+        fits = jnp.where(crowded, 0, fits)
+    for p in range(PROMPTS):
+        for q in range(p):
+            one, two = slot_ref[p], slot_ref[q]
+            shared = (one // SLOTS_HERE == two // SLOTS_HERE) & (one != two)
+            fits = jnp.where(shared, 0, fits)
+    return fits
+
+
+def block_kernel(plan, *refs):
+    (
+        len_hbm,
+        slot_hbm,
+        dt_hbm,
+        alog_hbm,
+        xc_hbm,
+        xm_hbm,
+        bc_hbm,
+        tx_hbm,
+        tbc_hbm,
+        wx_hbm,
+        wbc_hbm,
+        prefix_hbm,
+    ) = refs[:12]
+    out_ref, act_ref, within_ref, fits_ref = refs[12:16]
+    (len_ref, slot_ref, dt_ref, alog_ref, xc_ref, xm_ref, bc_ref, tx_ref, tbc_ref, wx_ref, wbc_ref) = refs[16:27]
+    x_scr, sems = refs[27:]
+    rows = plan.prefix
+    small = plan.slots == 1
+    ctx = lax.axis_index("ctx")
     copies = [
         pltpu.make_async_copy(src, dst, sems.at[n])
         for n, (src, dst) in enumerate(
             [
                 (len_hbm, len_ref),
+                (slot_hbm, slot_ref),
                 (dt_hbm, dt_ref),
                 (alog_hbm, alog_ref),
                 (xc_hbm, xc_ref),
                 (xm_hbm, xm_ref),
                 (bc_hbm, bc_ref),
+                (wx_hbm, wx_ref),
+                (wbc_hbm, wbc_ref),
                 (tx_hbm, tx_ref),
                 (tbc_hbm, tbc_ref),
-                (wx_hbm, wx_ref),
-                (wbc_hbm, wbc_ref),
-            ]
-            + [
-                (prefix_hbm.at[s], out_ref.at[:, pl.ds(PREFIX_AT + s * rows, rows), :])
-                for s in range(SLOTS_HERE)
             ]
         )
     ]
     for copy in copies:
         copy.start()
-    for copy in copies[:10]:
+    copies[0].wait()
+    copies[1].wait()
+    used = jnp.int32(0)
+    for p in range(PROMPTS):
+        used = jnp.where(slot_ref[p] // SLOTS_HERE == ctx, slot_ref[p] % SLOTS_HERE, used)
+    states = [
+        pltpu.make_async_copy(
+            prefix_hbm.at[used if small else s],
+            out_ref.at[:, pl.ds(plan.prefix + s * rows, rows), :],
+            sems.at[len(copies) + s],
+        )
+        for s in range(plan.slots)
+    ]
+    for copy in states:
+        copy.start()
+    for copy in copies[2:]:
         copy.wait()
 
-    ctx = lax.axis_index("ctx")
     heads = dt_ref.shape[0]
     chans = heads * WIDTH
     group = lax.axis_index("head") * heads // HEADS_GROUP
     groups = bc_ref.shape[1] // (2 * STATE)
     devices = out_ref.shape[0]
     starts = starts_of(len_ref)
+    fits_ref[0] = small_enough(starts, slot_ref)
     locs = [s - ctx * TOK for s in starts]
 
     scale = jnp.exp2(xc_ref[...].astype(F32)).T.astype(BF)
@@ -182,40 +238,42 @@
         inputs, act[:, chans:], (((0,), (0,)), ((), ())), preferred_element_type=F32
     ).astype(BF)
 
-    entry = iota((16, TOK), 0)
-    begin = jnp.full((16, TOK), -TOK, jnp.int32)
-    for p in range(PROMPTS):
-        for i in range(LAGS):
-            at = jnp.where(len_ref[p] > i, locs[p] + i, -TOK)
-            begin = jnp.where(entry == p * LAGS + i, at, begin)
-    chosen = iota((16, TOK), 1) == begin
+    def chosen_rows(modulus):
+        entry = iota((16, TOK), 0)
+        begin = jnp.full((16, TOK), -TOK, jnp.int32)
+        for p in range(PROMPTS):
+            for i in range(LAGS):
+                at = locs[p] + i
+                inside = (len_ref[p] > i) & (at >= 0) & (at < TOK)
+                begin = jnp.where((entry == p % modulus * LAGS + i) & inside, at, begin)
+        return iota((16, TOK), 1) == begin
+
     raw = jnp.concatenate([x, b_raw], axis=1).astype(BF)
-    at_start = jnp.dot(chosen.astype(BF), raw, preferred_element_type=F32)[: PROMPTS * LAGS]
-    lane = iota((heads, TOK), 1)
+    at_start = jnp.dot(chosen_rows(plan.prompts).astype(BF), raw, preferred_element_type=F32)
+    at_start = at_start[: plan.prompts * LAGS]
     at_block = jnp.where((token < LAGS) & (token - first >= LAGS), to_end, 0.0)
-    vals = nt_dot(to_end, chosen.astype(F32), precision=HIGH)[:, : PROMPTS * LAGS]
+    vals = nt_dot(to_end, chosen_rows(PROMPTS).astype(F32), precision=HIGH)[:, : PROMPTS * LAGS]
     vals = jnp.concatenate(
         [at_block[:, :LAGS], vals, jnp.exp(within[:, TOK - 1 :]), jnp.zeros((heads, TOK - 16), F32)], axis=1
     )
     high = vals.astype(BF).astype(F32)
     low = vals - high
 
-    tails = jnp.concatenate([tx_ref[i].astype(F32) for i in range(LAGS)], axis=0)
-    tails = jnp.concatenate(
-        [tails[i * SLOTS_HERE + s : i * SLOTS_HERE + s + 1] for s in range(SLOTS_HERE) for i in range(LAGS)], axis=0
-    )
-    tails_b, tails_c = [], []
-    for s in range(SLOTS_HERE):
+    tails_x, tails_b, tails_c = [], [], []
+    for s in range(plan.slots):
         for i in range(LAGS):
-            b_one, c_one = group_cols(lambda at: tbc_ref[i, :, pl.ds(at, STATE)], group, groups)
-            tails_b.append(b_one[s : s + 1])
-            tails_c.append(c_one[s : s + 1])
+            b_two, c_two = group_cols(lambda at: tbc_ref[i, :, pl.ds(at, STATE)], group, groups)
+            for found, two in ((tails_x, tx_ref[i].astype(F32)), (tails_b, b_two), (tails_c, c_two)):
+                found.append(jnp.where(used == 1, two[1:], two[:1]) if small else two[s : s + 1])
+    tails = jnp.concatenate(tails_x, axis=0)
     gap = jnp.zeros((2, STATE), F32)
     b_tile = jnp.concatenate([b_raw[:LAGS], gap, b_raw[TOK - LAGS :]], axis=0)
     foot = jnp.concatenate(
-        [at_start[:, chans:]] + tails_b + tails_c + [c_raw[TOK - LAGS :], jnp.zeros((ROWS1 - CP_AT - LAGS, STATE), F32)],
+        [at_start[:, chans:]] + tails_b + tails_c + [c_raw[TOK - LAGS :]],
         axis=0,
     )
+    if plan.rows > plan.used:
+        foot = jnp.concatenate([foot, jnp.zeros((plan.rows - plan.used, STATE), F32)], axis=0)
     for k in range(devices):
         out_ref[k, :rows, :] = ends[k * rows : (k + 1) * rows]
         lanes = slice(k * rows // STATE * STATE, (k * rows // STATE + 1) * STATE)
@@ -224,14 +282,23 @@
         part = jnp.concatenate(
             x_tile + [b_tile, at_start[:, lanes], tails[:, lanes], foot], axis=0
         )
-        out_ref[k, XB_AT:, :] = part.astype(BF)
-    for copy in copies[10:]:
+        out_ref[k, plan.xb :, :] = part.astype(BF)
+    for copy in states:
         copy.wait()
 
 
-def scan_kernel(len_ref, slot_ref, got_ref, wx_ref, wbc_ref, out_ref, x_scr, b_scr, in_scr, mix_scr):
+def tail_of(plan, got_ref, slot, tail_at):
+    owner = got_ref[slot // SLOTS_HERE, plan.xb :, :].astype(F32)
+    place = tail_at - plan.xb
+    tail = owner[place : place + LAGS]
+    if plan.slots > 1:
+        tail = jnp.where(slot % SLOTS_HERE == 1, owner[place + LAGS : place + 2 * LAGS], tail)
+    return tail
+
+
+def scan_kernel(plan, len_ref, slot_ref, got_ref, wx_ref, wbc_ref, out_ref, x_scr, b_scr, in_scr, mix_scr):
     devices = got_ref.shape[0]
-    rows = PREFIX_AT
+    rows = plan.prefix
     ctx = lax.axis_index("ctx")
     chans = wx_ref.shape[1]
     group = lax.axis_index("head") * (chans // WIDTH) // HEADS_GROUP
@@ -240,27 +307,28 @@
     starts = starts_of(len_ref)
     blocks = [s // TOK for s in starts]
 
-    x_scr[...] = got_ref[:, XB_AT : XB_AT + 8, :].astype(F32).reshape(devices * 8, STATE)
-    b_scr[...] = got_ref[:, BB_AT : BB_AT + 8, :].astype(F32).reshape(devices * 8, STATE)
+    x_scr[...] = got_ref[:, plan.xb : plan.xb + 8, :].astype(F32).reshape(devices * 8, STATE)
+    b_scr[...] = got_ref[:, plan.bb : plan.bb + 8, :].astype(F32).reshape(devices * 8, STATE)
     factors = x_scr[pl.ds(LAGS, devices, stride=8), :] + x_scr[pl.ds(LAGS + 1, devices, stride=8), :]
     prompt_factors = jnp.sum(factors, axis=0, keepdims=True)
 
     def windows(scr, start_at, tail_at):
         before, now = [], []
         for p in range(PROMPTS):
-            slot = slot_ref[p]
-            own = got_ref[blocks[p], XB_AT:, :].astype(F32)
-            after = got_ref[jnp.minimum(blocks[p] + 1, devices - 1), XB_AT:, :].astype(F32)
-            after = jnp.where(blocks[p] + 1 < devices, after, 0.0)
-            place = start_at - XB_AT + p * LAGS
-            now.append((own + after)[place : place + LAGS])
-            owner = got_ref[slot // SLOTS_HERE, XB_AT:, :].astype(F32)
-            place = tail_at - XB_AT
-            before.append(
-                jnp.where(
-                    slot % SLOTS_HERE == 1, owner[place + LAGS : place + 2 * LAGS], owner[place : place + LAGS]
-                )
+            own = got_ref[blocks[p], plan.xb :, :].astype(F32)
+            after = got_ref[jnp.minimum(blocks[p] + 1, devices - 1), plan.xb :, :].astype(F32)
+            place = start_at - plan.xb + p % plan.prompts * LAGS
+            now.append(
+                [
+                    jnp.where(
+                        (starts[p] + i) // TOK == blocks[p],
+                        own[place + i : place + i + 1],
+                        after[place + i : place + i + 1],
+                    )
+                    for i in range(LAGS)
+                ]
             )
+            before.append(tail_of(plan, got_ref, slot_ref[p], tail_at))
         pad = jnp.zeros((WINDOWS - devices - PROMPTS, STATE), F32)
         found = []
         for i in range(LAGS):
@@ -269,7 +337,7 @@
             found.append(jnp.concatenate([last] + [b[i : i + 1] for b in before] + [pad], axis=0))
         for i in range(LAGS):
             fresh = scr[pl.ds(i, devices, stride=8), :]
-            found.append(jnp.concatenate([fresh] + [n[i : i + 1] for n in now] + [pad], axis=0))
+            found.append(jnp.concatenate([fresh] + [n[i] for n in now] + [pad], axis=0))
         return found
 
     def activation(rows6, taps, i):
@@ -280,8 +348,8 @@
 
     x_taps = wx_ref[:, pl.ds(pl.multiple_of(ctx * rows // STATE * STATE, STATE), STATE)]
     b_taps, _ = group_cols(lambda at: wbc_ref[:, pl.ds(at, STATE)], group, groups)
-    x_rows = windows(x_scr, XP_AT, XT_AT)
-    b_rows = windows(b_scr, BP_AT, BT_AT)
+    x_rows = windows(x_scr, plan.xp, plan.xt)
+    b_rows = windows(b_scr, plan.bp, plan.bt)
     x_act = [activation(x_rows, x_taps, i) for i in range(LAGS)]
     b_act = [activation(b_rows, b_taps, i) for i in range(LAGS)]
     scaled = []
@@ -314,11 +382,13 @@
     prefixes = []
     for p in range(PROMPTS):
         slot = slot_ref[p]
-        place = pl.multiple_of(PREFIX_AT + (slot % SLOTS_HERE) * rows, rows)
+        place = plan.prefix
+        if plan.slots > 1:
+            place = pl.multiple_of(place + (slot % SLOTS_HERE) * rows, rows)
         prefixes.append(got_ref[slot // SLOTS_HERE, pl.ds(place, rows), :])
     wide = [piece.astype(F32) for piece in prefixes]
     state = jnp.zeros((rows, STATE), F32)
-    states = PROMPTS * rows
+    states = plan.prompts * rows
     for d in range(devices):
         out_ref[d, :rows, :] = state.astype(BF)
         out_ref[d, rows:states, :] = jnp.zeros((states - rows, STATE), BF)
@@ -330,13 +400,15 @@
         decay = factors[d : d + 1, DECAY_LANE : DECAY_LANE + 1]
         state = decay * base + (got_ref[d, :rows, :].astype(F32) + extra[d * rows : (d + 1) * rows])
     for p in range(PROMPTS):
-        place = jnp.int32(1)
-        for q in range(p):
-            place = place + (blocks[q] == blocks[p]).astype(jnp.int32)
+        place = jnp.int32(0)
+        for q in range(p + 1):
+            place = place + (starts[q] > blocks[p] * TOK).astype(jnp.int32)
+        place = jnp.minimum(place, plan.prompts - 1)
         out_ref[blocks[p], pl.ds(pl.multiple_of(place * rows, rows), rows), :] = prefixes[p]
 
 
 def read_kernel(
+    plan,
     len_ref,
     slot_ref,
     sent_ref,
@@ -367,21 +439,12 @@
     prompt = sum((token >= loc).astype(jnp.int32) for loc in locs) - 1
 
     bc_scr[8:, :] = jnp.concatenate(group_cols(lambda at: bc_ref[:, pl.ds(at, STATE)], group, groups), axis=1)
-    before = sent_ref[(ctx + devices - 1) % devices, XB_AT:, :].astype(F32)
-    bc_scr[8 - LAGS : 8, :STATE] = before[BB_AT - XB_AT + 8 - LAGS : BB_AT - XB_AT + 8]
-    bc_scr[8 - LAGS : 8, STATE:] = before[CP_AT - XB_AT : CP_AT - XB_AT + LAGS]
+    before = sent_ref[(ctx + devices - 1) % devices, plan.bb :, :].astype(F32)
+    bc_scr[8 - LAGS : 8, :STATE] = before[8 - LAGS : 8]
+    bc_scr[8 - LAGS : 8, STATE:] = before[plan.cp - plan.bb : plan.cp - plan.bb + LAGS]
     tails = []
     for p in range(PROMPTS):
-        owner = sent_ref[slot_ref[p] // SLOTS_HERE, XB_AT:, :].astype(F32)
-        pair = []
-        for place in (BT_AT - XB_AT, CT_AT - XB_AT):
-            pair.append(
-                jnp.where(
-                    slot_ref[p] % SLOTS_HERE == 1,
-                    owner[place + LAGS : place + 2 * LAGS],
-                    owner[place : place + LAGS],
-                )
-            )
+        pair = [tail_of(plan, sent_ref, slot_ref[p], at) for at in (plan.bt, plan.ct)]
         tails.append(jnp.concatenate(pair, axis=1))
     tails.append(jnp.zeros((16 - PROMPTS * LAGS, 2 * STATE), F32))
     tails = jnp.concatenate(tails, axis=0).astype(BF)
@@ -402,7 +465,7 @@
     pick = by_prompt | by_block
     other = (near | (token < LAGS))[:, :1]
     per = STATE // rows
-    states = PROMPTS * rows
+    states = plan.prompts * rows
     spec = []
     for c in range(chans // STATE):
         spec.append(
@@ -420,10 +483,10 @@
     within_c = within.T
     scores = nt_dot(c_act, b_act)
     place = iota((TOK, STATE), 0)
-    place = sum(((loc >= 0) & (place >= loc)).astype(jnp.int32) for loc in locs)
+    place = sum(((loc > 0) & (place >= loc)).astype(jnp.int32) for loc in locs)
     c_wide = c_act.astype(F32)
     reads = jnp.zeros((TOK, chans), F32)
-    for j in range(PROMPTS):
+    for j in range(plan.prompts):
         state = got_ref[:, j * rows : (j + 1) * rows, :].reshape(chans, STATE)
         reads = reads + nt_dot(jnp.where(place == j, c_wide, 0.0).astype(BF), state)
     y = widen(jnp.exp(within), WIDTH) * reads
@@ -446,9 +509,8 @@
     sq_ref[...] = jnp.sum(part.T, axis=0, keepdims=True)
 
 
-def norm_kernel(gated_ref, sq_ref, other_ref, gain_ref, out_ref):
-    total = sq_ref[...] + other_ref[...]
-    inverse = lax.rsqrt(total / (HEADS_GROUP * WIDTH) + EPS)
+def norm_kernel(gated_ref, sq_ref, gain_ref, out_ref):
+    inverse = lax.rsqrt(sq_ref[...] / (HEADS_GROUP * WIDTH) + EPS)
     inverse = jnp.broadcast_to(inverse, (TOK, TOK)).T
     for c in range(out_ref.shape[1] // TOK):
         at = slice(c * TOK, (c + 1) * TOK)
@@ -478,74 +540,90 @@
     chans = heads * WIDTH
     rows = chans // devices
     dt_t = dt_raw.T
-    sources = [
-        prompt_lengths,
-        dt_t,
-        a_log.reshape(1, heads),
-        x_codes.T,
-        x_mant,
-        bc_raw,
-        jnp.transpose(tail_x, (1, 0, 2)),
-        jnp.transpose(tail_bc, (1, 0, 2)),
-        conv_x,
-        conv_bc,
-    ]
+    a_row = a_log.reshape(1, heads)
+    skip_row = d_skip.reshape(1, heads)
+    tail_x = jnp.transpose(tail_x, (1, 0, 2))
+    tail_bc = jnp.transpose(tail_bc, (1, 0, 2))
     prefixes = prefix_state.reshape(SLOTS_HERE, devices, rows, STATE)
-    send1, act, within = call(
-        block_kernel,
-        (
-            jax.ShapeDtypeStruct((devices, ROWS1, STATE), BF),
-            jax.ShapeDtypeStruct((TOK, chans), BF),
-            jax.ShapeDtypeStruct((heads, TOK), F32),
-        ),
-        in_specs=[hbm()] * 11,
-        out_specs=(vmem(),) * 3,
-        scratch_shapes=[pltpu.SMEM((PROMPTS,), jnp.int32)]
-        + [pltpu.VMEM(source.shape, source.dtype) for source in sources[1:]]
-        + [pltpu.VMEM((TOK + 8, chans + STATE), F32), pltpu.SemaphoreType.DMA((12,))],
-    )(*sources, prefixes)
-    got1 = lax.all_to_all(send1, "ctx", 0, 0)
-
-    send2 = call(
-        scan_kernel,
-        jax.ShapeDtypeStruct((devices, PROMPTS * rows + 8, STATE), BF),
-        in_specs=[smem(), smem()] + [vmem()] * 3,
-        out_specs=vmem(),
-        scratch_shapes=[
-            pltpu.VMEM((devices * 8, STATE), F32),
-            pltpu.VMEM((devices * 8, STATE), F32),
-            pltpu.VMEM((STATE, STATE), F32),
-            pltpu.VMEM((chans, STATE), BF),
-        ],
-    )(prompt_lengths, cache_slot, got1, conv_x, conv_bc)
-    got2 = lax.all_to_all(send2, "ctx", 0, 0)
-
-    gated, squares = call(
-        read_kernel,
-        (jax.ShapeDtypeStruct((TOK, chans), F32), jax.ShapeDtypeStruct((1, TOK), F32)),
-        in_specs=[smem(), smem()] + [vmem()] * 9,
-        out_specs=(vmem(), vmem()),
-        scratch_shapes=[pltpu.VMEM((TOK + 8, 2 * STATE), F32)],
-    )(
-        prompt_lengths,
-        cache_slot,
-        got1,
-        got2,
-        act,
-        bc_raw,
-        conv_bc,
-        within,
-        dt_t,
-        d_skip.reshape(1, heads),
-        gate_z,
-    )
-    other = lax.ppermute(squares, "head", [(i, i ^ 1) for i in range(head_devices)])
+
+    def first_part(plan):
+        sources = [
+            prompt_lengths,
+            cache_slot,
+            dt_t,
+            a_row,
+            x_codes.T,
+            x_mant,
+            bc_raw,
+            tail_x,
+            tail_bc,
+            conv_x,
+            conv_bc,
+        ]
+        return call(
+            functools.partial(block_kernel, plan),
+            (
+                jax.ShapeDtypeStruct((devices, plan.rows, STATE), BF),
+                jax.ShapeDtypeStruct((TOK, chans), BF),
+                jax.ShapeDtypeStruct((heads, TOK), F32),
+                jax.ShapeDtypeStruct((1,), jnp.int32),
+            ),
+            in_specs=[hbm()] * 12,
+            out_specs=(vmem(), vmem(), vmem(), smem()),
+            scratch_shapes=[pltpu.SMEM((PROMPTS,), jnp.int32)] * 2
+            + [pltpu.VMEM(source.shape, source.dtype) for source in sources[2:]]
+            + [pltpu.VMEM((TOK + 8, chans + STATE), F32), pltpu.SemaphoreType.DMA((11 + plan.slots,))],
+        )(*[pinned(source) for source in sources + [prefixes]])
+
+    def second_part(plan, send1, act, within):
+        got1 = lax.all_to_all(send1, "ctx", 0, 0)
+        send2 = call(
+            functools.partial(scan_kernel, plan),
+            jax.ShapeDtypeStruct((devices, plan.prompts * rows + 8, STATE), BF),
+            in_specs=[smem(), smem()] + [vmem()] * 3,
+            out_specs=vmem(),
+            scratch_shapes=[
+                pltpu.VMEM((devices * 8, STATE), F32),
+                pltpu.VMEM((devices * 8, STATE), F32),
+                pltpu.VMEM((STATE, STATE), F32),
+                pltpu.VMEM((chans, STATE), BF),
+            ],
+        )(prompt_lengths, cache_slot, got1, conv_x, conv_bc)
+        got2 = lax.all_to_all(send2, "ctx", 0, 0)
+        return call(
+            functools.partial(read_kernel, plan),
+            (jax.ShapeDtypeStruct((TOK, chans), F32), jax.ShapeDtypeStruct((1, TOK), F32)),
+            in_specs=[smem(), smem()] + [vmem()] * 9,
+            out_specs=(vmem(), vmem()),
+            scratch_shapes=[pltpu.VMEM((TOK + 8, 2 * STATE), F32)],
+        )(
+            prompt_lengths,
+            cache_slot,
+            got1,
+            got2,
+            act,
+            bc_raw,
+            conv_bc,
+            within,
+            dt_t,
+            skip_row,
+            gate_z,
+        )
+
+    send1, act, within, fits = first_part(SMALL)
+    gated, squares = lax.cond(
+        fits[0] == 1,
+        lambda: second_part(SMALL, send1, act, within),
+        lambda: second_part(FULL, *first_part(FULL)[:3]),
+    )
+    pairs = [[i, i + 1] for i in range(0, head_devices, 2)]
+    total = lax.psum(squares, "head", axis_index_groups=pairs)
     return call(
         norm_kernel,
         jax.ShapeDtypeStruct((TOK, chans), BF),
-        in_specs=[vmem()] * 4,
+        in_specs=[vmem()] * 3,
         out_specs=vmem(),
-    )(gated, squares, other, norm_gain.reshape(1, chans))
+    )(gated, total, norm_gain.reshape(1, chans))
 
 
 def solution(mesh):

time: 72 us -> 68.5 us (0.951)
  local copies, waits for them, and re-layouts: 8.71 us -> 0.84 us
  Pallas kernels: 6.36 us -> 10.8 us
  blocking collectives: 51.9 us -> 55.6 us
  starting transfers between devices: 2.3 us -> 0 us
  waiting for transfers between devices: 1.98 us -> 0 us
    unnamed x34 -> x18, local copies, waits for them, and re-layouts: 8.71 us -> 0.04 us
    pallas_call x3 -> x4, Pallas kernels: 5.51 us -> 9.99 us  [the longest x2 6.54 us: first_part(): call(functools.partial(block_kernel, plan), (jax.ShapeDtypeStruct((device...]
    psum x0 -> x1, blocking collectives: none -> 3.79 us  [on_device(): total = lax.psum(squares, 'head', axis_index_groups=pairs)]
    ppermute x1 -> x0, starting transfers between devices: 2.3 us -> none  [on_device(): lax.ppermute(squares, 'head', [(i, i ^ 1) for i in range(head_devices)])]
    ppermute x1 -> x0, waiting for transfers between devices: 1.98 us -> none  [on_device(): lax.ppermute(squares, 'head', [(i, i ^ 1) for i in range(head_devices)])]
    cond x0 -> x24, local copies, waits for them, and re-layouts: none -> 0.8 us
  transfers between devices with their start and end apart: 1 -> 0, of which waited for: 1 -> 0; matrix products, arithmetic and copies ran while one was open for 0% -> 0% of each run, Pallas kernels for 0% -> 0%
where the time goes in v3:
time: 68.5 us; the launch traced here: 68.2 us
  blocking collectives  55.6 us (81%)
  Pallas kernels  10.8 us (16%)
  local copies, waits for them, and re-layouts  0.84 us (1%)
  between operations  0.78 us (1%)
    all_to_all x1, blocking collectives, second_part(): got1 = lax.all_to_all(send1, 'ctx', 0, 0)  29.8 us
    all_to_all x1, blocking collectives, second_part(): got2 = lax.all_to_all(send2, 'ctx', 0, 0)  22 us
    pallas_call x2, Pallas kernels, first_part(): call(functools.partial(block_kernel, plan), (jax.ShapeDtypeStruct((device...  6.54 us
    psum x1, blocking collectives, on_device(): total = lax.psum(squares, 'head', axis_index_groups=pairs)  3.79 us
    pallas_call x1, Pallas kernels, second_part(): call(functools.partial(read_kernel, plan), (jax.ShapeDtypeStruct((TOK, ch...  2.24 us

profile of v3, /device:TPU:1, one launch (start us, length us, event | category | flops | bytes accessed | tf_op | source)
XLA Modules:
  0.0 68.2 jit_solution(17874574220534198186)
XLA Ops:
  0.0 0.0 copy-start.17
  0.0 0.0 copy-start.14
  0.0 0.0 copy-start.4
  0.0 0.0 copy-start.8
  0.0 0.0 copy-start.1
  0.0 0.0 copy-start.7
  0.0 0.0 copy-start.20
  0.0 0.0 copy-start.11
  0.1 3.3 %shard_map.145 = (bf16[32,104,128]{2,1,0:T(8,128)(2,1)S(1)}, bf16[128,1024]{1,0:T(8,128)(2,1)S(1)}, f32[16,128]{1,0:T(8,128)S(1)}, s32[1]{0:T(128)}) custom-call(s32[4]{0:T(128)} %refs_0_.1, s32[4]{0:T(128)} %refs_1_.1, f32[16,128]{1,0:T(8,128)} %bitcast.13, f32[1,16]{1,0:T(1,128)} %bitcast.22, s32[32,128]{1,0:T(8,128)} %bitcast.18, ...), custom_call_target="tpu_custom_call" | custom-call | tf_op jit(solution)/shard_map/pallas_call | solution.py:563
  4.0 0.0 copy-done.17
  4.0 0.0 copy-done.14
  4.0 0.0 copy-done.4
  4.0 0.0 copy-done.8
  4.1 0.0 copy-done.1
  4.1 0.0 copy-done.7
  4.1 0.0 copy-done.20
  4.1 0.0 copy-done.11
  4.1 0.0 copy-start
  4.1 59.5 %conditional.1 = ((f32[128,1024]{1,0:T(8,128)S(1)}, f32[1,128]{1,0:T(1,128)S(1)})) conditional(s32[]{:T(128)} %bitcast.7, (s32[128,32]{0,1:T(8,128)}, s32[4]{0:T(128)S(1)}, s32[4]{0:T(128)S(1)}, f32[16,128]{1,0:T(8,128)S(1)}, f32[1,16]{1,0:T(1,128)}, /*index=5*/bf16[128,1024]{1,0:T(8,128)(2,1)}, bf16[128,2048]{1,0:T(8,128)(2,1)S(1)}, ...), branch_computations={%region_0.0_spmd, %region_1.0_spmd} | conditional | bytes 9503320 | solution.py:614
  4.1 0.0 copy-start.2
  4.1 0.0 copy-start.5
  4.1 0.0 copy-start.9
  4.2 0.0 copy-start.12
  4.2 0.0 copy-start.15
  4.2 0.0 copy-start.18
  4.2 0.7 %copy-done.2 = bf16[128,2048]{1,0:T(8,128)(2,1)} copy-done((bf16[128,2048]{1,0:T(8,128)(2,1)}, bf16[128,2048]{1,0:T(8,128)(2,1)S(1)}, u32[]{:S(2)}) %copy-start.2) | copy-done | bytes 524312 | tf_op jit(solution)/shard_map/cond
  4.9 0.0 copy-done.5
  4.9 0.0 copy-done.9
  4.9 0.0 copy-done.12
  4.9 0.0 copy-done.15
  4.9 0.0 copy-done.18
  5.0 3.2 %branch_0_fun.3 = (bf16[32,160,128]{2,1,0:T(8,128)(2,1)S(1)}, bf16[128,1024]{1,0:T(8,128)(2,1)S(1)}, f32[16,128]{1,0:T(8,128)S(1)}, s32[1]{0:T(128)}) custom-call(s32[4]{0:T(128)} %copy-done.15, s32[4]{0:T(128)} %copy-done.18, f32[16,128]{1,0:T(8,128)} %copy-done.12, f32[1,16]{1,0:T(1,128)} %get-tuple-element.58.refs_3_, s32[32,128]{1,0:T(8,128)} %bitcast.19, ...), custom_call_target="tpu_custom_call" | custom-call | tf_op jit(solution)/shard_map/cond/branch_0_fun/pallas_call | solution.py:563
  8.2 0.0 copy-start.6
  8.2 0.0 copy-start.10
  8.2 0.0 copy-start.16
  8.2 0.0 copy-start.19
  8.2 29.8 %all_to_all.16.got_ref.sent_ref = bf16[32,160,128]{2,1,0:T(8,128)(2,1)S(1)} all-to-all(bf16[32,160,128]{2,1,0:T(8,128)(2,1)S(1)} %get-tuple-element.67), channel_id=1, replica_groups=mesh['head'=16,'ctx'=32] {'ctx'}, dimensions={0} | all-to-all | bytes 2621440 | tf_op jit(solution)/shard_map/cond/branch_0_fun/all_to_all | solution.py:579
  38.1 0.0 copy-done.6
  38.1 0.0 copy-done.10
  38.1 0.0 copy-done.16
  38.1 0.0 copy-done.19
  38.1 1.2 %branch_0_fun.4 = bf16[32,136,128]{2,1,0:T(8,128)(2,1)S(1)} custom-call(s32[4]{0:T(128)S(1)} %copy-done.16, s32[4]{0:T(128)S(1)} %copy-done.19, bf16[32,160,128]{2,1,0:T(8,128)(2,1)S(1)} %all_to_all.16.got_ref.sent_ref, f32[4,1024]{1,0:T(4,128)S(1)} %copy-done.10, f32[4,2048]{1,0:T(4,128)S(1)} %copy-done.6), custom_call_target="tpu_custom_call" | custom-call | tf_op jit(solution)/shard_map/cond/branch_0_fun/pallas_call | solution.py:580
  39.3 0.0 copy-start.3
  39.3 0.0 copy-start.13
  39.3 22.0 %all_to_all.17.got_ref = bf16[32,136,128]{2,1,0:T(8,128)(2,1)S(1)} all-to-all(bf16[32,136,128]{2,1,0:T(8,128)(2,1)S(1)} %branch_0_fun.4), channel_id=1, replica_groups=mesh['head'=16,'ctx'=32] {'ctx'}, dimensions={0} | all-to-all | bytes 2228224 | tf_op jit(solution)/shard_map/cond/branch_0_fun/all_to_all | solution.py:592
  61.4 0.0 copy-done.3
  61.4 0.0 copy-done.13
  61.4 2.2 %branch_0_fun.5 = (f32[128,1024]{1,0:T(8,128)S(1)}, f32[1,128]{1,0:T(1,128)S(1)}) custom-call(s32[4]{0:T(128)S(1)} %copy-done.16, s32[4]{0:T(128)S(1)} %copy-done.19, bf16[32,160,128]{2,1,0:T(8,128)(2,1)S(1)} %all_to_all.16.got_ref.sent_ref, bf16[32,136,128]{2,1,0:T(8,128)(2,1)S(1)} %all_to_all.17.got_ref, bf16[128,1024]{1,0:T(8,128)(2,1)S(1)} %get-tuple-element.68.act_ref, ...), custom_call_target="tpu_custom_call" | custom-call | tf_op jit(solution)/shard_map/cond/branch_0_fun/pallas_call | solution.py:593
  63.6 3.8 %psum.7.sq_ref = f32[1,128]{1,0:T(1,128)S(1)} all-reduce(f32[1,128]{1,0:T(1,128)S(1)} %get-tuple-element.94), channel_id=1, replica_groups={{0,32},{64,96},{128,160},{192,224},{256,288},{320,352},{384,416},{448,4..., use_global_device_ids=true, to_apply=%region_2.0 | all-reduce | flops 128 | bytes 1024 | tf_op jit(solution)/shard_map/psum | solution.py:620
  67.4 0.0 copy-done
  67.4 0.8 %shard_map.146 = bf16[128,1024]{1,0:T(8,128)(2,1)} custom-call(f32[128,1024]{1,0:T(8,128)S(1)} %get-tuple-element.93.gated_ref, f32[1,128]{1,0:T(1,128)S(1)} %psum.7.sq_ref, f32[1,1024]{1,0:T(1,128)S(1)} %bitcast.10), custom_call_target="tpu_custom_call" | custom-call | tf_op jit(solution)/shard_map/pallas_call | solution.py:621
Async XLA Ops:
  0.0 4.0 %copy-start.17 = (s32[4]{0:T(128)S(1)}, s32[4]{0:T(128)}, u32[]{:S(2)}) copy-start(s32[4]{0:T(128)} %refs_1_.1) | copy-start | bytes 52
  0.0 4.0 %copy-start.14 = (s32[4]{0:T(128)S(1)}, s32[4]{0:T(128)}, u32[]{:S(2)}) copy-start(s32[4]{0:T(128)} %refs_0_.1) | copy-start | bytes 52
  0.0 4.0 %copy-start.4 = (f32[4,2048]{1,0:T(4,128)S(1)}, f32[4,2048]{1,0:T(4,128)}, u32[]{:S(2)}) copy-start(f32[4,2048]{1,0:T(4,128)} %refs_10_.1) | copy-start | bytes 98308
  0.0 4.0 %copy-start.8 = (f32[4,1024]{1,0:T(4,128)S(1)}, f32[4,1024]{1,0:T(4,128)}, u32[]{:S(2)}) copy-start(f32[4,1024]{1,0:T(4,128)} %refs_9_.1) | copy-start | bytes 49156
  0.0 4.0 %copy-start.1 = (bf16[128,2048]{1,0:T(8,128)(2,1)S(1)}, bf16[128,2048]{1,0:T(8,128)(2,1)}, u32[]{:S(2)}) copy-start(bf16[128,2048]{1,0:T(8,128)(2,1)} %refs_6_.1) | copy-start | bytes 1572868
  0.0 4.0 %copy-start.7 = (bf16[128,1024]{1,0:T(8,128)(2,1)S(1)}, bf16[128,1024]{1,0:T(8,128)(2,1)}, u32[]{:S(2)}) copy-start(bf16[128,1024]{1,0:T(8,128)(2,1)} %param.20) | copy-start | bytes 786436
  0.0 4.0 %copy-start.20 = (f32[16]{0:T(128)S(1)}, f32[16]{0:T(128)}, u32[]{:S(2)}) copy-start(f32[16]{0:T(128)} %param.25) | copy-start | bytes 196
  0.0 4.0 %copy-start.11 = (f32[128,16]{0,1:T(8,128)S(1)}, f32[128,16]{0,1:T(8,128)}, u32[]{:S(2)}) copy-start(f32[128,16]{0,1:T(8,128)} %param.23) | copy-start | bytes 24580
  4.1 63.3 %copy-start = (f32[1024]{0:T(1024)S(1)}, f32[1024]{0:T(1024)}, u32[]{:S(2)}) copy-start(f32[1024]{0:T(1024)} %param.26) | copy-start | bytes 12292
  4.1 0.8 %copy-start.2 = (bf16[128,2048]{1,0:T(8,128)(2,1)}, bf16[128,2048]{1,0:T(8,128)(2,1)S(1)}, u32[]{:S(2)}) copy-start(bf16[128,2048]{1,0:T(8,128)(2,1)S(1)} %get-tuple-element.61.refs_6_.bc_ref) | copy-start | bytes 1572868 | tf_op jit(solution)/shard_map/cond
  4.1 0.8 %copy-start.5 = (f32[4,2048]{1,0:T(4,128)}, f32[4,2048]{1,0:T(4,128)S(1)}, u32[]{:S(2)}) copy-start(f32[4,2048]{1,0:T(4,128)S(1)} %get-tuple-element.65.refs_10_.wbc_ref) | copy-start | bytes 98308 | tf_op jit(solution)/shard_map/cond
  4.1 0.8 %copy-start.9 = (f32[4,1024]{1,0:T(4,128)}, f32[4,1024]{1,0:T(4,128)S(1)}, u32[]{:S(2)}) copy-start(f32[4,1024]{1,0:T(4,128)S(1)} %get-tuple-element.64.refs_9_.wx_ref) | copy-start | bytes 49156 | tf_op jit(solution)/shard_map/cond
  4.2 0.8 %copy-start.12 = (f32[16,128]{1,0:T(8,128)}, f32[16,128]{1,0:T(8,128)S(1)}, u32[]{:S(2)}) copy-start(f32[16,128]{1,0:T(8,128)S(1)} %get-tuple-element.57.refs_2_.dt_ref) | copy-start | bytes 24580 | tf_op jit(solution)/shard_map/cond
  4.2 0.8 %copy-start.15 = (s32[4]{0:T(128)}, s32[4]{0:T(128)S(1)}, u32[]{:S(2)}) copy-start(s32[4]{0:T(128)S(1)} %get-tuple-element.55.refs_0_.len_ref) | copy-start | bytes 52 | tf_op jit(solution)/shard_map/cond
  4.2 0.8 %copy-start.18 = (s32[4]{0:T(128)}, s32[4]{0:T(128)S(1)}, u32[]{:S(2)}) copy-start(s32[4]{0:T(128)S(1)} %get-tuple-element.56.refs_1_.slot_ref) | copy-start | bytes 52 | tf_op jit(solution)/shard_map/cond
  8.2 29.9 %copy-start.6 = (f32[4,2048]{1,0:T(4,128)S(1)}, f32[4,2048]{1,0:T(4,128)}, u32[]{:S(2)}) copy-start(f32[4,2048]{1,0:T(4,128)} %copy-done.5) | copy-start | bytes 98308 | tf_op jit(solution)/shard_map/cond
  8.2 29.9 %copy-start.10 = (f32[4,1024]{1,0:T(4,128)S(1)}, f32[4,1024]{1,0:T(4,128)}, u32[]{:S(2)}) copy-start(f32[4,1024]{1,0:T(4,128)} %copy-done.9) | copy-start | bytes 49156 | tf_op jit(solution)/shard_map/cond
  8.2 29.9 %copy-start.16 = (s32[4]{0:T(128)S(1)}, s32[4]{0:T(128)}, u32[]{:S(2)}) copy-start(s32[4]{0:T(128)} %copy-done.15) | copy-start | bytes 52 | tf_op jit(solution)/shard_map/cond
  8.2 29.9 %copy-start.19 = (s32[4]{0:T(128)S(1)}, s32[4]{0:T(128)}, u32[]{:S(2)}) copy-start(s32[4]{0:T(128)} %copy-done.18) | copy-start | bytes 52 | tf_op jit(solution)/shard_map/cond
  39.3 22.0 %copy-start.3 = (bf16[128,2048]{1,0:T(8,128)(2,1)S(1)}, bf16[128,2048]{1,0:T(8,128)(2,1)}, u32[]{:S(2)}) copy-start(bf16[128,2048]{1,0:T(8,128)(2,1)} %copy-done.2) | copy-start | bytes 1572868 | tf_op jit(solution)/shard_map/cond
  39.3 22.0 %copy-start.13 = (f32[16,128]{1,0:T(8,128)S(1)}, f32[16,128]{1,0:T(8,128)}, u32[]{:S(2)}) copy-start(f32[16,128]{1,0:T(8,128)} %copy-done.12) | copy-start | bytes 24580 | tf_op jit(solution)/shard_map/cond

commit v4 on v3

--- a/solution.py
+++ b/solution.py
@@ -9,7 +9,6 @@
 
 BF = jnp.bfloat16
 F32 = jnp.float32
-HIGH = lax.Precision.HIGHEST
 INTERPRET = False
 
 TOK = 128
@@ -22,27 +21,28 @@
 SLOTS_HERE = 2
 EPS = 1e-05
 FAR = -1e30
+NORM_PARTS = 4
 
 
 class Plan:
     def __init__(self, slots, prompts):
         self.slots, self.prompts = slots, prompts
+        self.begun = 1 if prompts == 2 else PROMPTS
         at = 32
         self.prefix, at = at, at + 32 * slots
         self.xb, at = at, at + 8
         self.bb, at = at, at + 8
-        self.xp, at = at, at + LAGS * prompts
+        self.xp, at = at, at + LAGS * self.begun
         self.xt, at = at, at + LAGS * slots
-        self.bp, at = at, at + LAGS * prompts
+        self.bp, at = at, at + LAGS * self.begun
         self.bt, at = at, at + LAGS * slots
         self.ct, at = at, at + LAGS * slots
-        self.cp, at = at, at + LAGS
+        self.cp, at = at, at + 1
         self.used = at
         self.rows = (at + 7) // 8 * 8
 
 
-SMALL = Plan(1, 2)
-FULL = Plan(SLOTS_HERE, PROMPTS)
+PLANS = (Plan(1, 2), Plan(SLOTS_HERE, 2), Plan(1, 3), Plan(SLOTS_HERE, PROMPTS))
 DECAY_LANE = LAGS + PROMPTS * LAGS
 WINDOWS = 40
 
@@ -96,18 +96,19 @@
 
 
 def silu(v):
-    return v / (1.0 + jnp.exp(-v))
+    half = 0.5 * v
+    return half + half * jnp.tanh(half)
+
+
+def terms(v, axis):
+    high = v.astype(BF).astype(F32)
+    mid = (v - high).astype(BF).astype(F32)
+    return jnp.concatenate([high, mid, v - high - mid], axis=axis)
 
 
 def spread(per, count):
     shape = (count, count * per)
-    return (iota(shape, 1) // per == iota(shape, 0)).astype(F32)
-
-
-def group_cols(load, group, groups):
-    b_at = pl.multiple_of(group * STATE, STATE)
-    c_at = pl.multiple_of((groups + group) * STATE, STATE)
-    return load(b_at).astype(F32), load(c_at).astype(F32)
+    return (iota(shape, 1) // per == iota(shape, 0)).astype(BF)
 
 
 def nt_dot(a, b, **kw):
@@ -119,23 +120,34 @@
     return (col <= row) & (col >= row_starts(locs, row))
 
 
-def widen(per_head_t, per):
-    return jnp.dot(
-        per_head_t.T, spread(per, per_head_t.shape[0]), precision=HIGH, preferred_element_type=F32
-    )
-
-
-def small_enough(starts, slot_ref):
-    fits = jnp.int32(1)
+def spread_terms(heads):
+    shape = (3 * heads, heads * WIDTH)
+    return (iota(shape, 1) // WIDTH == iota(shape, 0) % heads).astype(BF)
+
+
+def widen(per_head_t):
+    columns = terms(per_head_t, 0).T.astype(BF)
+    return jnp.dot(columns, spread_terms(per_head_t.shape[0]), preferred_element_type=F32)
+
+
+def exact_nt(v, zero_one):
+    rows = v.shape[0]
+    parts = nt_dot(terms(v, 0).astype(BF), zero_one.astype(BF))
+    return parts[:rows] + parts[rows : 2 * rows] + parts[2 * rows :]
+
+
+def plan_number(starts, slot_ref):
+    crowd = jnp.int32(2)
     for p in range(PROMPTS - 2):
-        crowded = (starts[p + 1] - 1) // TOK == starts[p + 2] // TOK
-        fits = jnp.where(crowded, 0, fits)
+        crowd = jnp.where((starts[p + 1] - 1) // TOK == starts[p + 2] // TOK, 3, crowd)
+    crowd = jnp.where((starts[1] - 1) // TOK == starts[3] // TOK, 4, crowd)
+    shared = jnp.int32(0)
     for p in range(PROMPTS):
         for q in range(p):
             one, two = slot_ref[p], slot_ref[q]
-            shared = (one // SLOTS_HERE == two // SLOTS_HERE) & (one != two)
-            fits = jnp.where(shared, 0, fits)
-    return fits
+            both = (one // SLOTS_HERE == two // SLOTS_HERE) & (one != two)
+            shared = jnp.where(both, 1, shared)
+    return jnp.where(crowd == 2, shared, jnp.where((crowd == 3) & (shared == 0), 2, 3))
 
 
 def block_kernel(plan, *refs):
@@ -153,12 +165,19 @@
         wbc_hbm,
         prefix_hbm,
     ) = refs[:12]
-    out_ref, act_ref, within_ref, fits_ref = refs[12:16]
-    (len_ref, slot_ref, dt_ref, alog_ref, xc_ref, xm_ref, bc_ref, tx_ref, tbc_ref, wx_ref, wbc_ref) = refs[16:27]
-    x_scr, sems = refs[27:]
+    out_ref, act_ref, within_ref, delta_ref, bc_ref, taps_ref, number_ref = refs[12:19]
+    (len_ref, slot_ref, dt_ref, alog_ref, xc_ref, xm_ref, tx_ref, tbc_ref, wx_ref) = refs[19:28]
+    x_scr, sems = refs[28:]
     rows = plan.prefix
     small = plan.slots == 1
     ctx = lax.axis_index("ctx")
+    heads = dt_ref.shape[0]
+    chans = heads * WIDTH
+    group = lax.axis_index("head") * heads // HEADS_GROUP
+    groups = bc_hbm.shape[1] // (2 * STATE)
+    b_cols = pl.ds(pl.multiple_of(group * STATE, STATE), STATE)
+    x_cols = pl.ds(pl.multiple_of(ctx * rows // STATE * STATE, STATE), STATE)
+    c_cols = pl.ds(pl.multiple_of((groups + group) * STATE, STATE), STATE)
     copies = [
         pltpu.make_async_copy(src, dst, sems.at[n])
         for n, (src, dst) in enumerate(
@@ -169,11 +188,15 @@
                 (alog_hbm, alog_ref),
                 (xc_hbm, xc_ref),
                 (xm_hbm, xm_ref),
-                (bc_hbm, bc_ref),
+                (bc_hbm.at[:, b_cols], bc_ref.at[0]),
+                (bc_hbm.at[:, c_cols], bc_ref.at[1]),
                 (wx_hbm, wx_ref),
-                (wbc_hbm, wbc_ref),
+                (wbc_hbm.at[:, b_cols], taps_ref.at[1]),
+                (wx_hbm.at[:, x_cols], taps_ref.at[0]),
+                (wbc_hbm.at[:, c_cols], taps_ref.at[2]),
                 (tx_hbm, tx_ref),
-                (tbc_hbm, tbc_ref),
+                (tbc_hbm.at[:, :, b_cols], tbc_ref.at[0]),
+                (tbc_hbm.at[:, :, c_cols], tbc_ref.at[1]),
             ]
         )
     ]
@@ -197,37 +220,33 @@
     for copy in copies[2:]:
         copy.wait()
 
-    heads = dt_ref.shape[0]
-    chans = heads * WIDTH
-    group = lax.axis_index("head") * heads // HEADS_GROUP
-    groups = bc_ref.shape[1] // (2 * STATE)
     devices = out_ref.shape[0]
     starts = starts_of(len_ref)
-    fits_ref[0] = small_enough(starts, slot_ref)
+    number_ref[0] = plan_number(starts, slot_ref)
     locs = [s - ctx * TOK for s in starts]
 
     scale = jnp.exp2(xc_ref[...].astype(F32)).T.astype(BF)
-    wide = jnp.dot(scale, spread(MXB, xc_ref.shape[0]).astype(BF), preferred_element_type=F32)
+    wide = jnp.dot(scale, spread(MXB, xc_ref.shape[0]), preferred_element_type=F32)
     x = xm_ref[...].astype(F32) * wide
-    b_raw, c_raw = group_cols(lambda at: bc_ref[:, pl.ds(at, STATE)], group, groups)
+    b_raw, c_raw = bc_ref[0].astype(F32), bc_ref[1].astype(F32)
     x_scr[8:, :chans] = x
     x_scr[8:, chans:] = b_raw
     x_scr[:8, :] = jnp.zeros((8, chans + STATE), F32)
 
     live = live_matrix(locs)
     delta = softplus(dt_ref[...])
+    delta_ref[...] = delta
     log_decay = -jnp.exp(alog_ref[...].T) * delta
-    within = nt_dot(log_decay, live.astype(F32), precision=HIGH)
+    within = exact_nt(log_decay, live)
     within_ref[...] = within
     token = iota((heads, TOK), 1)
     first = row_starts(locs, token)
     last_start = row_starts(locs, jnp.full((heads, TOK), TOK - 1, jnp.int32))
     to_end = delta * jnp.exp(jnp.where(token >= last_start, within[:, TOK - 1 :] - within, FAR))
     regular = (token >= LAGS) & (token - first >= LAGS)
-    factor = widen(jnp.where(regular, to_end, 0.0), WIDTH)
-
-    w_b, _ = group_cols(lambda at: wbc_ref[:, pl.ds(at, STATE)], group, groups)
-    taps = jnp.concatenate([wx_ref[...], w_b], axis=1)
+    factor = widen(jnp.where(regular, to_end, 0.0))
+
+    taps = jnp.concatenate([wx_ref[...], taps_ref[1]], axis=1)
     conv = taps[LAGS : LAGS + 1] * x_scr[8:, :]
     for k in range(1, LAGS + 1):
         conv = conv + taps[LAGS - k : LAGS - k + 1] * x_scr[8 - k : 8 + TOK - k, :]
@@ -238,21 +257,21 @@
         inputs, act[:, chans:], (((0,), (0,)), ((), ())), preferred_element_type=F32
     ).astype(BF)
 
-    def chosen_rows(modulus):
+    def chosen_rows(modulus, lowest):
         entry = iota((16, TOK), 0)
         begin = jnp.full((16, TOK), -TOK, jnp.int32)
         for p in range(PROMPTS):
             for i in range(LAGS):
                 at = locs[p] + i
-                inside = (len_ref[p] > i) & (at >= 0) & (at < TOK)
+                inside = (len_ref[p] > i) & (at >= lowest) & (at < TOK)
                 begin = jnp.where((entry == p % modulus * LAGS + i) & inside, at, begin)
         return iota((16, TOK), 1) == begin
 
     raw = jnp.concatenate([x, b_raw], axis=1).astype(BF)
-    at_start = jnp.dot(chosen_rows(plan.prompts).astype(BF), raw, preferred_element_type=F32)
-    at_start = at_start[: plan.prompts * LAGS]
+    at_start = jnp.dot(chosen_rows(plan.begun, LAGS).astype(BF), raw, preferred_element_type=F32)
+    at_start = at_start[: plan.begun * LAGS]
     at_block = jnp.where((token < LAGS) & (token - first >= LAGS), to_end, 0.0)
-    vals = nt_dot(to_end, chosen_rows(PROMPTS).astype(F32), precision=HIGH)[:, : PROMPTS * LAGS]
+    vals = exact_nt(to_end, chosen_rows(PROMPTS, 0))[:, : PROMPTS * LAGS]
     vals = jnp.concatenate(
         [at_block[:, :LAGS], vals, jnp.exp(within[:, TOK - 1 :]), jnp.zeros((heads, TOK - 16), F32)], axis=1
     )
@@ -262,27 +281,31 @@
     tails_x, tails_b, tails_c = [], [], []
     for s in range(plan.slots):
         for i in range(LAGS):
-            b_two, c_two = group_cols(lambda at: tbc_ref[i, :, pl.ds(at, STATE)], group, groups)
-            for found, two in ((tails_x, tx_ref[i].astype(F32)), (tails_b, b_two), (tails_c, c_two)):
+            for found, two in ((tails_x, tx_ref[i]), (tails_b, tbc_ref[0, i]), (tails_c, tbc_ref[1, i])):
+                two = two.astype(F32)
                 found.append(jnp.where(used == 1, two[1:], two[:1]) if small else two[s : s + 1])
     tails = jnp.concatenate(tails_x, axis=0)
     gap = jnp.zeros((2, STATE), F32)
-    b_tile = jnp.concatenate([b_raw[:LAGS], gap, b_raw[TOK - LAGS :]], axis=0)
+    c_last = c_raw[TOK - LAGS :]
+    b_tile = jnp.concatenate([b_raw[:LAGS], c_last[:2], b_raw[TOK - LAGS :]], axis=0)
     foot = jnp.concatenate(
-        [at_start[:, chans:]] + tails_b + tails_c + [c_raw[TOK - LAGS :]],
+        [at_start[:, chans:]] + tails_b + tails_c + [c_last[2:]],
         axis=0,
     )
     if plan.rows > plan.used:
         foot = jnp.concatenate([foot, jnp.zeros((plan.rows - plan.used, STATE), F32)], axis=0)
-    for k in range(devices):
-        out_ref[k, :rows, :] = ends[k * rows : (k + 1) * rows]
-        lanes = slice(k * rows // STATE * STATE, (k * rows // STATE + 1) * STATE)
-        h = k * rows // WIDTH
-        x_tile = [x[:LAGS, lanes], high[h : h + 1], low[h : h + 1], x[TOK - LAGS :, lanes]]
-        part = jnp.concatenate(
-            x_tile + [b_tile, at_start[:, lanes], tails[:, lanes], foot], axis=0
-        )
-        out_ref[k, plan.xb :, :] = part.astype(BF)
+    tile_row = iota((8, STATE), 0)
+    for c in range(chans // STATE):
+        lanes = slice(c * STATE, (c + 1) * STATE)
+        x_tile = jnp.concatenate([x[:LAGS, lanes], gap, x[TOK - LAGS :, lanes]], axis=0)
+        part = jnp.concatenate([b_tile, at_start[:, lanes], tails[:, lanes], foot], axis=0).astype(BF)
+        for k in range(c * STATE // rows, (c + 1) * STATE // rows):
+            h = k * rows // WIDTH
+            out_ref[k, :rows, :] = ends[k * rows : (k + 1) * rows]
+            tile = jnp.where(tile_row == LAGS, high[h : h + 1], x_tile)
+            tile = jnp.where(tile_row == LAGS + 1, low[h : h + 1], tile)
+            out_ref[k, plan.xb : plan.bb, :] = tile.astype(BF)
+            out_ref[k, plan.bb :, :] = part
     for copy in states:
         copy.wait()
 
@@ -296,13 +319,10 @@
     return tail
 
 
-def scan_kernel(plan, len_ref, slot_ref, got_ref, wx_ref, wbc_ref, out_ref, x_scr, b_scr, in_scr, mix_scr):
+def scan_kernel(plan, len_ref, slot_ref, got_ref, taps_ref, out_ref, x_scr, b_scr, in_scr, mix_scr):
     devices = got_ref.shape[0]
     rows = plan.prefix
     ctx = lax.axis_index("ctx")
-    chans = wx_ref.shape[1]
-    group = lax.axis_index("head") * (chans // WIDTH) // HEADS_GROUP
-    groups = wbc_ref.shape[1] // (2 * STATE)
     at = ctx * rows % STATE
     starts = starts_of(len_ref)
     blocks = [s // TOK for s in starts]
@@ -316,18 +336,14 @@
         before, now = [], []
         for p in range(PROMPTS):
             own = got_ref[blocks[p], plan.xb :, :].astype(F32)
-            after = got_ref[jnp.minimum(blocks[p] + 1, devices - 1), plan.xb :, :].astype(F32)
-            place = start_at - plan.xb + p % plan.prompts * LAGS
-            now.append(
-                [
-                    jnp.where(
-                        (starts[p] + i) // TOK == blocks[p],
-                        own[place + i : place + i + 1],
-                        after[place + i : place + i + 1],
-                    )
-                    for i in range(LAGS)
-                ]
-            )
+            place = start_at - plan.xb + p % plan.begun * LAGS
+            found = []
+            for i in range(LAGS):
+                row = (starts[p] + i) % TOK
+                block = jnp.minimum((starts[p] + i) // TOK, devices - 1)
+                early = scr[pl.ds(8 * block + jnp.minimum(row, LAGS - 1), 1), :]
+                found.append(jnp.where(row < LAGS, early, own[place + i : place + i + 1]))
+            now.append(found)
             before.append(tail_of(plan, got_ref, slot_ref[p], tail_at))
         pad = jnp.zeros((WINDOWS - devices - PROMPTS, STATE), F32)
         found = []
@@ -346,12 +362,10 @@
             conv = conv + taps[LAGS - k : LAGS - k + 1] * rows6[LAGS + i - k]
         return silu(conv).astype(BF).astype(F32)
 
-    x_taps = wx_ref[:, pl.ds(pl.multiple_of(ctx * rows // STATE * STATE, STATE), STATE)]
-    b_taps, _ = group_cols(lambda at: wbc_ref[:, pl.ds(at, STATE)], group, groups)
     x_rows = windows(x_scr, plan.xp, plan.xt)
     b_rows = windows(b_scr, plan.bp, plan.bt)
-    x_act = [activation(x_rows, x_taps, i) for i in range(LAGS)]
-    b_act = [activation(b_rows, b_taps, i) for i in range(LAGS)]
+    x_act = [activation(x_rows, taps_ref[0], i) for i in range(LAGS)]
+    b_act = [activation(b_rows, taps_ref[1], i) for i in range(LAGS)]
     scaled = []
     for i in range(LAGS):
         column = [factors[:, i : i + 1]]
@@ -415,9 +429,9 @@
     got_ref,
     act_ref,
     bc_ref,
-    wbc_ref,
+    taps_ref,
     within_ref,
-    dt_ref,
+    delta_ref,
     skip_ref,
     gate_ref,
     gated_ref,
@@ -426,11 +440,9 @@
 ):
     ctx = lax.axis_index("ctx")
     devices = got_ref.shape[0]
-    heads = dt_ref.shape[0]
+    heads = delta_ref.shape[0]
     chans = heads * WIDTH
     rows = chans // devices
-    group = lax.axis_index("head") * heads // HEADS_GROUP
-    groups = bc_ref.shape[1] // (2 * STATE)
     locs = [s - ctx * TOK for s in starts_of(len_ref)]
 
     token = iota((TOK, 16), 0)
@@ -438,17 +450,18 @@
     first = row_starts(locs, token)
     prompt = sum((token >= loc).astype(jnp.int32) for loc in locs) - 1
 
-    bc_scr[8:, :] = jnp.concatenate(group_cols(lambda at: bc_ref[:, pl.ds(at, STATE)], group, groups), axis=1)
+    bc_scr[8:, :] = jnp.concatenate([bc_ref[0], bc_ref[1]], axis=1).astype(F32)
     before = sent_ref[(ctx + devices - 1) % devices, plan.bb :, :].astype(F32)
     bc_scr[8 - LAGS : 8, :STATE] = before[8 - LAGS : 8]
-    bc_scr[8 - LAGS : 8, STATE:] = before[plan.cp - plan.bb : plan.cp - plan.bb + LAGS]
+    c_last = plan.cp - plan.bb
+    bc_scr[8 - LAGS : 8, STATE:] = jnp.concatenate([before[LAGS : LAGS + 2], before[c_last : c_last + 1]], axis=0)
     tails = []
     for p in range(PROMPTS):
         pair = [tail_of(plan, sent_ref, slot_ref[p], at) for at in (plan.bt, plan.ct)]
         tails.append(jnp.concatenate(pair, axis=1))
     tails.append(jnp.zeros((16 - PROMPTS * LAGS, 2 * STATE), F32))
     tails = jnp.concatenate(tails, axis=0).astype(BF)
-    taps = jnp.concatenate(group_cols(lambda at: wbc_ref[:, pl.ds(at, STATE)], group, groups), axis=1)
+    taps = jnp.concatenate([taps_ref[1], taps_ref[2]], axis=1)
     conv = taps[LAGS : LAGS + 1] * bc_scr[8:, :]
     for k in range(1, LAGS + 1):
         outside = token - k < first
@@ -478,7 +491,7 @@
     x_wide = jnp.where(other, patch, act_ref[...].astype(F32))
 
     live = live_matrix(locs)
-    delta = softplus(dt_ref[...])
+    delta = delta_ref[...]
     within = within_ref[...]
     within_c = within.T
     scores = nt_dot(c_act, b_act)
@@ -489,8 +502,8 @@
     for j in range(plan.prompts):
         state = got_ref[:, j * rows : (j + 1) * rows, :].reshape(chans, STATE)
         reads = reads + nt_dot(jnp.where(place == j, c_wide, 0.0).astype(BF), state)
-    y = widen(jnp.exp(within), WIDTH) * reads
-    skip = jnp.dot(skip_ref[...], spread(WIDTH, heads), precision=HIGH, preferred_element_type=F32)
+    y = widen(jnp.exp(within)) * reads
+    skip = jnp.dot(terms(skip_ref[...], 1).astype(BF), spread_terms(heads), preferred_element_type=F32)
     left = iota((TOK, 2 * WIDTH), 1) < WIDTH
     part = jnp.zeros((TOK, TOK), F32)
     for j in range(heads // 2):
@@ -509,12 +522,20 @@
     sq_ref[...] = jnp.sum(part.T, axis=0, keepdims=True)
 
 
-def norm_kernel(gated_ref, sq_ref, gain_ref, out_ref):
+def norm_kernel(gated_ref, sq_ref, gain_ref, out_hbm, out_scr, sems):
     inverse = lax.rsqrt(sq_ref[...] / (HEADS_GROUP * WIDTH) + EPS)
     inverse = jnp.broadcast_to(inverse, (TOK, TOK)).T
-    for c in range(out_ref.shape[1] // TOK):
-        at = slice(c * TOK, (c + 1) * TOK)
-        out_ref[:, at] = (gated_ref[:, at] * inverse * gain_ref[:, at]).astype(BF)
+    rows = TOK // NORM_PARTS
+    copies = []
+    for part in range(NORM_PARTS):
+        at = slice(part * rows, (part + 1) * rows)
+        for c in range(out_scr.shape[1] // TOK):
+            cols = slice(c * TOK, (c + 1) * TOK)
+            out_scr[at, cols] = (gated_ref[at, cols] * inverse[at] * gain_ref[:, cols]).astype(BF)
+        copies.append(pltpu.make_async_copy(out_scr.at[at], out_hbm.at[at], sems.at[part]))
+        copies[-1].start()
+    for copy in copies:
+        copy.wait()
 
 
 def on_device(
@@ -566,21 +587,30 @@
                 jax.ShapeDtypeStruct((devices, plan.rows, STATE), BF),
                 jax.ShapeDtypeStruct((TOK, chans), BF),
                 jax.ShapeDtypeStruct((heads, TOK), F32),
+                jax.ShapeDtypeStruct((heads, TOK), F32),
+                jax.ShapeDtypeStruct((2, TOK, STATE), BF),
+                jax.ShapeDtypeStruct((3, conv_x.shape[0], STATE), F32),
                 jax.ShapeDtypeStruct((1,), jnp.int32),
             ),
             in_specs=[hbm()] * 12,
-            out_specs=(vmem(), vmem(), vmem(), smem()),
+            out_specs=(vmem(),) * 6 + (smem(),),
             scratch_shapes=[pltpu.SMEM((PROMPTS,), jnp.int32)] * 2
-            + [pltpu.VMEM(source.shape, source.dtype) for source in sources[2:]]
-            + [pltpu.VMEM((TOK + 8, chans + STATE), F32), pltpu.SemaphoreType.DMA((11 + plan.slots,))],
+            + [pltpu.VMEM(source.shape, source.dtype) for source in sources[2:6]]
+            + [
+                pltpu.VMEM(tail_x.shape, BF),
+                pltpu.VMEM((2,) + tail_x.shape[:2] + (STATE,), BF),
+                pltpu.VMEM(conv_x.shape, F32),
+                pltpu.VMEM((TOK + 8, chans + STATE), F32),
+                pltpu.SemaphoreType.DMA((15 + plan.slots,)),
+            ],
         )(*[pinned(source) for source in sources + [prefixes]])
 
-    def second_part(plan, send1, act, within):
+    def second_part(plan, send1, act, within, delta, bc_here, taps):
         got1 = lax.all_to_all(send1, "ctx", 0, 0)
         send2 = call(
             functools.partial(scan_kernel, plan),
             jax.ShapeDtypeStruct((devices, plan.prompts * rows + 8, STATE), BF),
-            in_specs=[smem(), smem()] + [vmem()] * 3,
+            in_specs=[smem(), smem()] + [vmem()] * 2,
             out_specs=vmem(),
             scratch_shapes=[
                 pltpu.VMEM((devices * 8, STATE), F32),
@@ -588,7 +618,7 @@
                 pltpu.VMEM((STATE, STATE), F32),
                 pltpu.VMEM((chans, STATE), BF),
             ],
-        )(prompt_lengths, cache_slot, got1, conv_x, conv_bc)
+        )(prompt_lengths, cache_slot, got1, taps)
         got2 = lax.all_to_all(send2, "ctx", 0, 0)
         return call(
             functools.partial(read_kernel, plan),
@@ -602,19 +632,19 @@
             got1,
             got2,
             act,
-            bc_raw,
-            conv_bc,
+            bc_here,
+            taps,
             within,
-            dt_t,
+            delta,
             skip_row,
             gate_z,
         )
 
-    send1, act, within, fits = first_part(SMALL)
-    gated, squares = lax.cond(
-        fits[0] == 1,
-        lambda: second_part(SMALL, send1, act, within),
-        lambda: second_part(FULL, *first_part(FULL)[:3]),
+    *first, number = first_part(PLANS[0])
+    gated, squares = lax.switch(
+        number[0],
+        [lambda: second_part(PLANS[0], *first)]
+        + [lambda plan=plan: second_part(plan, *first_part(plan)[:-1]) for plan in PLANS[1:]],
     )
     pairs = [[i, i + 1] for i in range(0, head_devices, 2)]
     total = lax.psum(squares, "head", axis_index_groups=pairs)
@@ -622,7 +652,8 @@
         norm_kernel,
         jax.ShapeDtypeStruct((TOK, chans), BF),
         in_specs=[vmem()] * 3,
-        out_specs=vmem(),
+        out_specs=hbm(),
+        scratch_shapes=[pltpu.VMEM((TOK, chans), BF), pltpu.SemaphoreType.DMA((NORM_PARTS,))],
     )(gated, total, norm_gain.reshape(1, chans))
 
 

time: 68.5 us -> 51.3 us (0.75)
  blocking collectives: 55.6 us -> 43.5 us
  Pallas kernels: 10.8 us -> 6.39 us
  local copies, waits for them, and re-layouts: 0.84 us -> 0.02 us
    all_to_all x1, blocking collectives: 22 us -> 15.9 us  [second_part(): got2 = lax.all_to_all(send2, 'ctx', 0, 0)]
    all_to_all x1, blocking collectives: 29.8 us -> 23.9 us  [second_part(): got1 = lax.all_to_all(send1, 'ctx', 0, 0)]
    pallas_call x2 -> x1, Pallas kernels: 6.54 us -> 2.76 us  [first_part(): call(functools.partial(block_kernel, plan), (jax.ShapeDtypeStruct((device...]
    cond x24 -> x0, local copies, waits for them, and re-layouts: 0.8 us -> none
where the time goes in v4:
time: 51.3 us; the launch traced here: 51.1 us
  blocking collectives  43.5 us (85%)
  Pallas kernels  6.39 us (12%)
  between operations  0.9 us (2%)
    all_to_all x1, blocking collectives, second_part(): got1 = lax.all_to_all(send1, 'ctx', 0, 0)  23.9 us
    all_to_all x1, blocking collectives, second_part(): got2 = lax.all_to_all(send2, 'ctx', 0, 0)  15.9 us
    psum x1, blocking collectives, on_device(): total = lax.psum(squares, 'head', axis_index_groups=pairs)  3.79 us
    pallas_call x1, Pallas kernels, first_part(): call(functools.partial(block_kernel, plan), (jax.ShapeDtypeStruct((device...  2.76 us
    pallas_call x1, Pallas kernels, second_part(): call(functools.partial(read_kernel, plan), (jax.ShapeDtypeStruct((TOK, ch...  1.66 us
    pallas_call x1, Pallas kernels, second_part(): call(functools.partial(scan_kernel, plan), jax.ShapeDtypeStruct((devices,...  1.15 us

profile of v4, /device:TPU:1, one launch (start us, length us, event | category | flops | bytes accessed | tf_op | source)
XLA Modules:
  0.0 51.1 jit_solution(5714875660775478325)
XLA Ops:
  0.0 0.0 copy-start.9
  0.0 0.0 copy-start.2
  0.0 0.0 copy-start.1
  0.0 0.0 copy-start.16
  0.0 2.8 %shard_map.145 = (bf16[32,96,128]{2,1,0:T(8,128)(2,1)S(1)}, bf16[128,1024]{1,0:T(8,128)(2,1)S(1)}, f32[16,128]{1,0:T(8,128)S(1)}, f32[16,128]{1,0:T(8,128)S(1)},...) custom-call(s32[4]{0:T(128)} %refs_0_.1, s32[4]{0:T(128)} %refs_1_.1, f32[16,128]{1,0:T(8,128)} %bitcast.29, ...), custom_call_target="tpu_custom_call" | custom-call | tf_op jit(solution)/shard_map/pallas_call | solution.py:584
  3.4 0.0 copy-done.9
  3.4 0.0 copy-done.2
  3.5 0.0 copy-done.1
  3.5 0.0 copy-done.16
  3.5 0.0 copy-start
  3.5 42.8 %conditional.1 = ((f32[128,1024]{1,0:T(8,128)S(1)}, f32[1,128]{1,0:T(1,128)S(1)})) conditional(s32[]{:T(128)} %bitcast.9, (bf16[32,96,128]{2,1,0:T(8,128)(2,1)S(1)}, s32[4]{0:T(128)S(1)}, s32[4]{0:T(128)S(1)}, f32[3,4,128]{2,1,0:T(4,128)S(1)}, bf16[128,1024]{1,0:T(8,128)(2,1)S(1)}, ...), branch_computations={%region_0.0_spmd, %region_1.0_spmd, %region_2.0_spmd, %region_3.0_... | conditional | bytes 4850040 | solution.py:644
  3.5 23.9 %all_to_all.32.got_ref.sent_ref = bf16[32,96,128]{2,1,0:T(8,128)(2,1)S(1)} all-to-all(bf16[32,96,128]{2,1,0:T(8,128)(2,1)S(1)} %get-tuple-element.111), channel_id=1, replica_groups=mesh['head'=16,'ctx'=32] {'ctx'}, dimensions={0} | all-to-all | bytes 1572864 | tf_op jit(solution)/shard_map/cond/branch_0_fun/all_to_all | solution.py:609
  27.4 1.1 %branch_0_fun.2 = bf16[32,72,128]{2,1,0:T(8,128)(2,1)S(1)} custom-call(s32[4]{0:T(128)S(1)} %get-tuple-element.109.len_ref, s32[4]{0:T(128)S(1)} %get-tuple-element.110.slot_ref, bf16[32,96,128]{2,1,0:T(8,128)(2,1)S(1)} %all_to_all.32.got_ref.sent_ref, f32[3,4,128]{2,1,0:T(4,128)S(1)} %get-tuple-element.112.taps_ref), custom_call_target="tpu_custom_call" | custom-call | tf_op jit(solution)/shard_map/cond/branch_0_fun/pallas_call | solution.py:610
  28.5 15.9 %all_to_all.33.got_ref = bf16[32,72,128]{2,1,0:T(8,128)(2,1)S(1)} all-to-all(bf16[32,72,128]{2,1,0:T(8,128)(2,1)S(1)} %branch_0_fun.2), channel_id=1, replica_groups=mesh['head'=16,'ctx'=32] {'ctx'}, dimensions={0} | all-to-all | bytes 1179648 | tf_op jit(solution)/shard_map/cond/branch_0_fun/all_to_all | solution.py:622
  44.4 1.7 %branch_0_fun.3 = (f32[128,1024]{1,0:T(8,128)S(1)}, f32[1,128]{1,0:T(1,128)S(1)}) custom-call(s32[4]{0:T(128)S(1)} %get-tuple-element.109.len_ref, s32[4]{0:T(128)S(1)} %get-tuple-element.110.slot_ref, bf16[32,96,128]{2,1,0:T(8,128)(2,1)S(1)} %all_to_all.32.got_ref.sent_ref, bf16[32,72,128]{2,1,0:T(8,128)(2,1)S(1)} %all_to_all.33.got_ref, ...), custom_call_target="tpu_custom_call" | custom-call | tf_op jit(solution)/shard_map/cond/branch_0_fun/pallas_call | solution.py:623
  46.3 3.8 %psum.7.sq_ref = f32[1,128]{1,0:T(1,128)S(1)} all-reduce(f32[1,128]{1,0:T(1,128)S(1)} %get-tuple-element.196), channel_id=1, replica_groups={{0,32},{64,96},{128,160},{192,224},{256,288},{320,352},{384,416},{448,4..., use_global_device_ids=true, to_apply=%region_4.0 | all-reduce | flops 128 | bytes 1024 | tf_op jit(solution)/shard_map/psum | solution.py:650
  50.1 0.0 copy-done
  50.1 0.8 %shard_map.146 = bf16[128,1024]{1,0:T(8,128)(2,1)} custom-call(f32[128,1024]{1,0:T(8,128)S(1)} %get-tuple-element.195.gated_ref, f32[1,128]{1,0:T(1,128)S(1)} %psum.7.sq_ref, f32[1,1024]{1,0:T(1,128)S(1)} %bitcast.12), custom_call_target="tpu_custom_call" | custom-call | tf_op jit(solution)/shard_map/pallas_call | solution.py:651
Async XLA Ops:
  0.0 3.4 %copy-start.9 = (s32[4]{0:T(128)S(1)}, s32[4]{0:T(128)}, u32[]{:S(2)}) copy-start(s32[4]{0:T(128)} %refs_1_.1) | copy-start | bytes 52
  0.0 3.4 %copy-start.2 = (s32[4]{0:T(128)S(1)}, s32[4]{0:T(128)}, u32[]{:S(2)}) copy-start(s32[4]{0:T(128)} %refs_0_.1) | copy-start | bytes 52
  0.0 3.5 %copy-start.1 = (bf16[128,1024]{1,0:T(8,128)(2,1)S(1)}, bf16[128,1024]{1,0:T(8,128)(2,1)}, u32[]{:S(2)}) copy-start(bf16[128,1024]{1,0:T(8,128)(2,1)} %param.22) | copy-start | bytes 786436
  0.0 3.5 %copy-start.16 = (f32[16]{0:T(128)S(1)}, f32[16]{0:T(128)}, u32[]{:S(2)}) copy-start(f32[16]{0:T(128)} %param.27) | copy-start | bytes 196
  3.5 46.6 %copy-start = (f32[1024]{0:T(1024)S(1)}, f32[1024]{0:T(1024)}, u32[]{:S(2)}) copy-start(f32[1024]{0:T(1024)} %param.28) | copy-start | bytes 12292

commit v5 on v4

--- a/solution.py
+++ b/solution.py
@@ -27,7 +27,7 @@
 class Plan:
     def __init__(self, slots, prompts):
         self.slots, self.prompts = slots, prompts
-        self.begun = 1 if prompts == 2 else PROMPTS
+        self.begun = prompts - 1
         at = 32
         self.prefix, at = at, at + 32 * slots
         self.xb, at = at, at + 8
@@ -150,7 +150,7 @@
     return jnp.where(crowd == 2, shared, jnp.where((crowd == 3) & (shared == 0), 2, 3))
 
 
-def block_kernel(plan, *refs):
+def block_kernel(*refs):
     (
         len_hbm,
         slot_hbm,
@@ -165,19 +165,20 @@
         wbc_hbm,
         prefix_hbm,
     ) = refs[:12]
-    out_ref, act_ref, within_ref, delta_ref, bc_ref, taps_ref, number_ref = refs[12:19]
-    (len_ref, slot_ref, dt_ref, alog_ref, xc_ref, xm_ref, tx_ref, tbc_ref, wx_ref) = refs[19:28]
-    x_scr, sems = refs[28:]
-    rows = plan.prefix
-    small = plan.slots == 1
+    out_refs, refs = refs[12 : 12 + len(PLANS)], refs[12 + len(PLANS) :]
+    act_ref, within_ref, delta_ref, bc_ref, taps_ref, number_ref = refs[:6]
+    (len_ref, slot_ref, dt_ref, alog_ref, xc_ref, xm_ref, tx_ref, tbc_ref, wx_ref) = refs[6:15]
+    x_scr, vals_scr, sems = refs[15:]
+    rows = PLANS[0].prefix
     ctx = lax.axis_index("ctx")
     heads = dt_ref.shape[0]
     chans = heads * WIDTH
+    devices = out_refs[0].shape[0]
     group = lax.axis_index("head") * heads // HEADS_GROUP
     groups = bc_hbm.shape[1] // (2 * STATE)
     b_cols = pl.ds(pl.multiple_of(group * STATE, STATE), STATE)
+    c_cols = pl.ds(pl.multiple_of((groups + group) * STATE, STATE), STATE)
     x_cols = pl.ds(pl.multiple_of(ctx * rows // STATE * STATE, STATE), STATE)
-    c_cols = pl.ds(pl.multiple_of((groups + group) * STATE, STATE), STATE)
     copies = [
         pltpu.make_async_copy(src, dst, sems.at[n])
         for n, (src, dst) in enumerate(
@@ -207,28 +208,30 @@
     used = jnp.int32(0)
     for p in range(PROMPTS):
         used = jnp.where(slot_ref[p] // SLOTS_HERE == ctx, slot_ref[p] % SLOTS_HERE, used)
-    states = [
-        pltpu.make_async_copy(
-            prefix_hbm.at[used if small else s],
-            out_ref.at[:, pl.ds(plan.prefix + s * rows, rows), :],
-            sems.at[len(copies) + s],
-        )
-        for s in range(plan.slots)
-    ]
+    starts = starts_of(len_ref)
+    locs = [s - ctx * TOK for s in starts]
+    number = plan_number(starts, slot_ref)
+    number_ref[0] = number
+
+    def state_copies(plan, out_ref):
+        return [
+            pltpu.make_async_copy(
+                prefix_hbm.at[used if plan.slots == 1 else s],
+                out_ref.at[:, pl.ds(plan.prefix + s * rows, rows), :],
+                sems.at[len(copies) + s],
+            )
+            for s in range(plan.slots)
+        ]
+
+    states = state_copies(PLANS[0], out_refs[0])
     for copy in states:
         copy.start()
     for copy in copies[2:]:
         copy.wait()
-
-    devices = out_ref.shape[0]
-    starts = starts_of(len_ref)
-    number_ref[0] = plan_number(starts, slot_ref)
-    locs = [s - ctx * TOK for s in starts]
-
     scale = jnp.exp2(xc_ref[...].astype(F32)).T.astype(BF)
     wide = jnp.dot(scale, spread(MXB, xc_ref.shape[0]), preferred_element_type=F32)
     x = xm_ref[...].astype(F32) * wide
-    b_raw, c_raw = bc_ref[0].astype(F32), bc_ref[1].astype(F32)
+    b_raw = bc_ref[0].astype(F32)
     x_scr[8:, :chans] = x
     x_scr[8:, chans:] = b_raw
     x_scr[:8, :] = jnp.zeros((8, chans + STATE), F32)
@@ -246,6 +249,26 @@
     regular = (token >= LAGS) & (token - first >= LAGS)
     factor = widen(jnp.where(regular, to_end, 0.0))
 
+    def chosen_rows(modulus, lowest):
+        entry = iota((16, TOK), 0)
+        begin = jnp.full((16, TOK), -TOK, jnp.int32)
+        for p in range(PROMPTS):
+            for i in range(LAGS):
+                at = locs[p] + i
+                inside = (len_ref[p] > i) & (at >= lowest) & (at < TOK)
+                begin = jnp.where((entry == p % modulus * LAGS + i) & inside, at, begin)
+        return iota((16, TOK), 1) == begin
+
+    at_block = jnp.where((token < LAGS) & (token - first >= LAGS), to_end, 0.0)
+    vals = exact_nt(to_end, chosen_rows(PROMPTS, 0))[:, : PROMPTS * LAGS]
+    vals = jnp.concatenate(
+        [at_block[:, :LAGS], vals, jnp.exp(within[:, TOK - 1 :]), jnp.zeros((heads, TOK - 16), F32)], axis=1
+    )
+    high = vals.astype(BF).astype(F32)
+    low = vals - high
+    vals_scr[0] = high
+    vals_scr[1] = low
+
     taps = jnp.concatenate([wx_ref[...], taps_ref[1]], axis=1)
     conv = taps[LAGS : LAGS + 1] * x_scr[8:, :]
     for k in range(1, LAGS + 1):
@@ -256,58 +279,56 @@
     ends = lax.dot_general(
         inputs, act[:, chans:], (((0,), (0,)), ((), ())), preferred_element_type=F32
     ).astype(BF)
-
-    def chosen_rows(modulus, lowest):
-        entry = iota((16, TOK), 0)
-        begin = jnp.full((16, TOK), -TOK, jnp.int32)
-        for p in range(PROMPTS):
+    for k in range(devices):
+        out_refs[0][k, :rows, :] = ends[k * rows : (k + 1) * rows]
+
+    def finish(plan, out_ref, x, b_raw, high, low):
+        raw = jnp.concatenate([x, b_raw], axis=1).astype(BF)
+        at_start = jnp.dot(chosen_rows(plan.begun, LAGS).astype(BF), raw, preferred_element_type=F32)
+        at_start = at_start[: plan.begun * LAGS]
+        tails_x, tails_b, tails_c = [], [], []
+        for s in range(plan.slots):
             for i in range(LAGS):
-                at = locs[p] + i
-                inside = (len_ref[p] > i) & (at >= lowest) & (at < TOK)
-                begin = jnp.where((entry == p % modulus * LAGS + i) & inside, at, begin)
-        return iota((16, TOK), 1) == begin
-
-    raw = jnp.concatenate([x, b_raw], axis=1).astype(BF)
-    at_start = jnp.dot(chosen_rows(plan.begun, LAGS).astype(BF), raw, preferred_element_type=F32)
-    at_start = at_start[: plan.begun * LAGS]
-    at_block = jnp.where((token < LAGS) & (token - first >= LAGS), to_end, 0.0)
-    vals = exact_nt(to_end, chosen_rows(PROMPTS, 0))[:, : PROMPTS * LAGS]
-    vals = jnp.concatenate(
-        [at_block[:, :LAGS], vals, jnp.exp(within[:, TOK - 1 :]), jnp.zeros((heads, TOK - 16), F32)], axis=1
-    )
-    high = vals.astype(BF).astype(F32)
-    low = vals - high
-
-    tails_x, tails_b, tails_c = [], [], []
-    for s in range(plan.slots):
-        for i in range(LAGS):
-            for found, two in ((tails_x, tx_ref[i]), (tails_b, tbc_ref[0, i]), (tails_c, tbc_ref[1, i])):
-                two = two.astype(F32)
-                found.append(jnp.where(used == 1, two[1:], two[:1]) if small else two[s : s + 1])
-    tails = jnp.concatenate(tails_x, axis=0)
-    gap = jnp.zeros((2, STATE), F32)
-    c_last = c_raw[TOK - LAGS :]
-    b_tile = jnp.concatenate([b_raw[:LAGS], c_last[:2], b_raw[TOK - LAGS :]], axis=0)
-    foot = jnp.concatenate(
-        [at_start[:, chans:]] + tails_b + tails_c + [c_last[2:]],
-        axis=0,
-    )
-    if plan.rows > plan.used:
-        foot = jnp.concatenate([foot, jnp.zeros((plan.rows - plan.used, STATE), F32)], axis=0)
-    tile_row = iota((8, STATE), 0)
-    for c in range(chans // STATE):
-        lanes = slice(c * STATE, (c + 1) * STATE)
-        x_tile = jnp.concatenate([x[:LAGS, lanes], gap, x[TOK - LAGS :, lanes]], axis=0)
-        part = jnp.concatenate([b_tile, at_start[:, lanes], tails[:, lanes], foot], axis=0).astype(BF)
-        for k in range(c * STATE // rows, (c + 1) * STATE // rows):
-            h = k * rows // WIDTH
-            out_ref[k, :rows, :] = ends[k * rows : (k + 1) * rows]
-            tile = jnp.where(tile_row == LAGS, high[h : h + 1], x_tile)
-            tile = jnp.where(tile_row == LAGS + 1, low[h : h + 1], tile)
-            out_ref[k, plan.xb : plan.bb, :] = tile.astype(BF)
-            out_ref[k, plan.bb :, :] = part
+                for found, two in ((tails_x, tx_ref[i]), (tails_b, tbc_ref[0, i]), (tails_c, tbc_ref[1, i])):
+                    two = two.astype(F32)
+                    found.append(jnp.where(used == 1, two[1:], two[:1]) if plan.slots == 1 else two[s : s + 1])
+        tails = jnp.concatenate(tails_x, axis=0)
+        c_last = bc_ref[1].astype(F32)[TOK - LAGS :]
+        b_tile = jnp.concatenate([b_raw[:LAGS], c_last[:2], b_raw[TOK - LAGS :]], axis=0)
+        foot = [at_start[:, chans:]] + tails_b + tails_c + [c_last[2:]]
+        if plan.rows > plan.used:
+            foot.append(jnp.zeros((plan.rows - plan.used, STATE), F32))
+        foot = jnp.concatenate(foot, axis=0)
+        gap = jnp.zeros((2, STATE), F32)
+        tile_row = iota((8, STATE), 0)
+        for c in range(chans // STATE):
+            lanes = slice(c * STATE, (c + 1) * STATE)
+            x_tile = jnp.concatenate([x[:LAGS, lanes], gap, x[TOK - LAGS :, lanes]], axis=0)
+            part = jnp.concatenate([b_tile, at_start[:, lanes], tails[:, lanes], foot], axis=0).astype(BF)
+            for k in range(c * STATE // rows, (c + 1) * STATE // rows):
+                h = k * rows // WIDTH
+                tile = jnp.where(tile_row == LAGS, high[h : h + 1], x_tile)
+                tile = jnp.where(tile_row == LAGS + 1, low[h : h + 1], tile)
+                out_ref[k, plan.xb : plan.bb, :] = tile.astype(BF)
+                out_ref[k, plan.bb :, :] = part
+
+    finish(PLANS[0], out_refs[0], x, b_raw, high, low)
     for copy in states:
         copy.wait()
+
+    @pl.when(number > 0)
+    def _():
+        for n, plan in list(enumerate(PLANS))[1:]:
+
+            @pl.when(number == n)
+            def _():
+                own = state_copies(plan, out_refs[n])
+                for copy in own:
+                    copy.start()
+                out_refs[n][:, :rows, :] = out_refs[0][:, :rows, :]
+                finish(plan, out_refs[n], x_scr[8:, :chans], x_scr[8:, chans:], vals_scr[0], vals_scr[1])
+                for copy in own:
+                    copy.wait()
 
 
 def tail_of(plan, got_ref, slot, tail_at):
@@ -567,43 +588,44 @@
     tail_bc = jnp.transpose(tail_bc, (1, 0, 2))
     prefixes = prefix_state.reshape(SLOTS_HERE, devices, rows, STATE)
 
-    def first_part(plan):
-        sources = [
-            prompt_lengths,
-            cache_slot,
-            dt_t,
-            a_row,
-            x_codes.T,
-            x_mant,
-            bc_raw,
-            tail_x,
-            tail_bc,
-            conv_x,
-            conv_bc,
-        ]
-        return call(
-            functools.partial(block_kernel, plan),
-            (
-                jax.ShapeDtypeStruct((devices, plan.rows, STATE), BF),
-                jax.ShapeDtypeStruct((TOK, chans), BF),
-                jax.ShapeDtypeStruct((heads, TOK), F32),
-                jax.ShapeDtypeStruct((heads, TOK), F32),
-                jax.ShapeDtypeStruct((2, TOK, STATE), BF),
-                jax.ShapeDtypeStruct((3, conv_x.shape[0], STATE), F32),
-                jax.ShapeDtypeStruct((1,), jnp.int32),
-            ),
-            in_specs=[hbm()] * 12,
-            out_specs=(vmem(),) * 6 + (smem(),),
-            scratch_shapes=[pltpu.SMEM((PROMPTS,), jnp.int32)] * 2
-            + [pltpu.VMEM(source.shape, source.dtype) for source in sources[2:6]]
-            + [
-                pltpu.VMEM(tail_x.shape, BF),
-                pltpu.VMEM((2,) + tail_x.shape[:2] + (STATE,), BF),
-                pltpu.VMEM(conv_x.shape, F32),
-                pltpu.VMEM((TOK + 8, chans + STATE), F32),
-                pltpu.SemaphoreType.DMA((15 + plan.slots,)),
-            ],
-        )(*[pinned(source) for source in sources + [prefixes]])
+    sources = [
+        prompt_lengths,
+        cache_slot,
+        dt_t,
+        a_row,
+        x_codes.T,
+        x_mant,
+        bc_raw,
+        tail_x,
+        tail_bc,
+        conv_x,
+        conv_bc,
+    ]
+    found = call(
+        block_kernel,
+        tuple(jax.ShapeDtypeStruct((devices, plan.rows, STATE), BF) for plan in PLANS)
+        + (
+            jax.ShapeDtypeStruct((TOK, chans), BF),
+            jax.ShapeDtypeStruct((heads, TOK), F32),
+            jax.ShapeDtypeStruct((heads, TOK), F32),
+            jax.ShapeDtypeStruct((2, TOK, STATE), BF),
+            jax.ShapeDtypeStruct((3, conv_x.shape[0], STATE), F32),
+            jax.ShapeDtypeStruct((1,), jnp.int32),
+        ),
+        in_specs=[hbm()] * 12,
+        out_specs=(vmem(),) * (5 + len(PLANS)) + (smem(),),
+        scratch_shapes=[pltpu.SMEM((PROMPTS,), jnp.int32)] * 2
+        + [pltpu.VMEM(source.shape, source.dtype) for source in sources[2:6]]
+        + [
+            pltpu.VMEM(tail_x.shape, BF),
+            pltpu.VMEM((2,) + tail_x.shape[:2] + (STATE,), BF),
+            pltpu.VMEM(conv_x.shape, F32),
+            pltpu.VMEM((TOK + 8, chans + STATE), F32),
+            pltpu.VMEM((2, heads, STATE), F32),
+            pltpu.SemaphoreType.DMA((15 + SLOTS_HERE,)),
+        ],
+    )(*[pinned(source) for source in sources + [prefixes]])
+    messages, rest, number = found[: len(PLANS)], found[len(PLANS) : -1], found[-1]
 
     def second_part(plan, send1, act, within, delta, bc_here, taps):
         got1 = lax.all_to_all(send1, "ctx", 0, 0)
@@ -640,11 +662,12 @@
             gate_z,
         )
 
-    *first, number = first_part(PLANS[0])
     gated, squares = lax.switch(
         number[0],
-        [lambda: second_part(PLANS[0], *first)]
-        + [lambda plan=plan: second_part(plan, *first_part(plan)[:-1]) for plan in PLANS[1:]],
+        [
+            lambda plan=plan, message=message: second_part(plan, message, *rest)
+            for plan, message in zip(PLANS, messages)
+        ],
     )
     pairs = [[i, i + 1] for i in range(0, head_devices, 2)]
     total = lax.psum(squares, "head", axis_index_groups=pairs)

time: 51.3 us -> 50.9 us (level)
  no operation moved by 1% of the time
where the time goes in v5:
time: 50.9 us; the launch traced here: 50.7 us
  blocking collectives  43.5 us (85%)
  Pallas kernels  6.37 us (13%)
  between operations  0.72 us (1%)
    all_to_all x1, blocking collectives, second_part(): got1 = lax.all_to_all(send1, 'ctx', 0, 0)  23.9 us
    all_to_all x1, blocking collectives, second_part(): got2 = lax.all_to_all(send2, 'ctx', 0, 0)  15.9 us
    psum x1, blocking collectives, on_device(): total = lax.psum(squares, 'head', axis_index_groups=pairs)  3.79 us
    pallas_call x1, Pallas kernels, on_device(): call(block_kernel, tuple((jax.ShapeDtypeStruct((devices, plan.rows, STATE...  2.76 us
    pallas_call x1, Pallas kernels, second_part(): call(functools.partial(read_kernel, plan), (jax.ShapeDtypeStruct((TOK, ch...  1.64 us
    pallas_call x1, Pallas kernels, second_part(): call(functools.partial(scan_kernel, plan), jax.ShapeDtypeStruct((devices,...  1.15 us

profile of v5, /device:TPU:1, one launch (start us, length us, event | category | flops | bytes accessed | tf_op | source)
XLA Modules:
  0.0 50.7 jit_solution(11143186080023255137)
XLA Ops:
  0.0 0.0 copy-start.3
  0.0 0.0 copy-start.2
  0.0 0.0 copy-start.1
  0.0 0.0 copy-start.4
  0.0 2.8 %shard_map.145 = (bf16[32,96,128]{2,1,0:T(8,128)(2,1)S(1)}, bf16[32,144,128]{2,1,0:T(8,128)(2,1)S(1)}, bf16[32,104,128]{2,1,0:T(8,128)(2,1)S(1)}, bf16[32,152,12...) custom-call(s32[4]{0:T(128)} %refs_0_.1, ...), custom_call_target="tpu_custom_call" | custom-call | tf_op jit(solution)/shard_map/pallas_call | solution.py:604
  3.4 0.0 copy-done.3
  3.4 0.0 copy-done.2
  3.5 0.0 copy-done.1
  3.5 0.0 copy-done.4
  3.5 0.0 copy-start
  3.5 42.5 %conditional.1 = ((f32[128,1024]{1,0:T(8,128)S(1)}, f32[1,128]{1,0:T(1,128)S(1)})) conditional(s32[]{:T(128)} %bitcast.6, (bf16[32,96,128]{2,1,0:T(8,128)(2,1)S(1)}, s32[4]{0:T(128)S(1)}, s32[4]{0:T(128)S(1)}, f32[3,4,128]{2,1,0:T(4,128)S(1)}, bf16[128,1024]{1,0:T(8,128)(2,1)S(1)}, ...), branch_computations={%region_0.0_spmd, %region_1.0_spmd, %region_2.0_spmd, %region_3.0_... | conditional | bytes 4718600 | solution.py:665
  3.5 23.9 %all_to_all.32.got_ref.sent_ref = bf16[32,96,128]{2,1,0:T(8,128)(2,1)S(1)} all-to-all(bf16[32,96,128]{2,1,0:T(8,128)(2,1)S(1)} %get-tuple-element.87), channel_id=1, replica_groups=mesh['head'=16,'ctx'=32] {'ctx'}, dimensions={0} | all-to-all | bytes 1572864 | tf_op jit(solution)/shard_map/cond/branch_0_fun/all_to_all | solution.py:631
  27.4 1.1 %branch_0_fun.2 = bf16[32,72,128]{2,1,0:T(8,128)(2,1)S(1)} custom-call(s32[4]{0:T(128)S(1)} %get-tuple-element.85.len_ref, s32[4]{0:T(128)S(1)} %get-tuple-element.86.slot_ref, bf16[32,96,128]{2,1,0:T(8,128)(2,1)S(1)} %all_to_all.32.got_ref.sent_ref, f32[3,4,128]{2,1,0:T(4,128)S(1)} %get-tuple-element.88.taps_ref), custom_call_target="tpu_custom_call" | custom-call | tf_op jit(solution)/shard_map/cond/branch_0_fun/pallas_call | solution.py:632
  28.5 15.9 %all_to_all.33.got_ref = bf16[32,72,128]{2,1,0:T(8,128)(2,1)S(1)} all-to-all(bf16[32,72,128]{2,1,0:T(8,128)(2,1)S(1)} %branch_0_fun.2), channel_id=1, replica_groups=mesh['head'=16,'ctx'=32] {'ctx'}, dimensions={0} | all-to-all | bytes 1179648 | tf_op jit(solution)/shard_map/cond/branch_0_fun/all_to_all | solution.py:644
  44.4 1.6 %branch_0_fun.3 = (f32[128,1024]{1,0:T(8,128)S(1)}, f32[1,128]{1,0:T(1,128)S(1)}) custom-call(s32[4]{0:T(128)S(1)} %get-tuple-element.85.len_ref, s32[4]{0:T(128)S(1)} %get-tuple-element.86.slot_ref, bf16[32,96,128]{2,1,0:T(8,128)(2,1)S(1)} %all_to_all.32.got_ref.sent_ref, bf16[32,72,128]{2,1,0:T(8,128)(2,1)S(1)} %all_to_all.33.got_ref, ...), custom_call_target="tpu_custom_call" | custom-call | tf_op jit(solution)/shard_map/cond/branch_0_fun/pallas_call | solution.py:645
  46.0 3.8 %psum.7.sq_ref = f32[1,128]{1,0:T(1,128)S(1)} all-reduce(f32[1,128]{1,0:T(1,128)S(1)} %get-tuple-element.148), channel_id=1, replica_groups={{0,32},{64,96},{128,160},{192,224},{256,288},{320,352},{384,416},{448,4..., use_global_device_ids=true, to_apply=%region_4.0 | all-reduce | flops 128 | bytes 1024 | tf_op jit(solution)/shard_map/psum | solution.py:673
  49.8 0.0 copy-done
  49.8 0.8 %shard_map.146 = bf16[128,1024]{1,0:T(8,128)(2,1)} custom-call(f32[128,1024]{1,0:T(8,128)S(1)} %get-tuple-element.147.gated_ref, f32[1,128]{1,0:T(1,128)S(1)} %psum.7.sq_ref, f32[1,1024]{1,0:T(1,128)S(1)} %bitcast.9), custom_call_target="tpu_custom_call" | custom-call | tf_op jit(solution)/shard_map/pallas_call | solution.py:674
Async XLA Ops:
  0.0 3.4 %copy-start.3 = (s32[4]{0:T(128)S(1)}, s32[4]{0:T(128)}, u32[]{:S(2)}) copy-start(s32[4]{0:T(128)} %refs_1_.1) | copy-start | bytes 52
  0.0 3.4 %copy-start.2 = (s32[4]{0:T(128)S(1)}, s32[4]{0:T(128)}, u32[]{:S(2)}) copy-start(s32[4]{0:T(128)} %refs_0_.1) | copy-start | bytes 52
  0.0 3.5 %copy-start.1 = (bf16[128,1024]{1,0:T(8,128)(2,1)S(1)}, bf16[128,1024]{1,0:T(8,128)(2,1)}, u32[]{:S(2)}) copy-start(bf16[128,1024]{1,0:T(8,128)(2,1)} %param.22) | copy-start | bytes 786436
  0.0 3.5 %copy-start.4 = (f32[16]{0:T(128)S(1)}, f32[16]{0:T(128)}, u32[]{:S(2)}) copy-start(f32[16]{0:T(128)} %param.27) | copy-start | bytes 196
  3.5 46.4 %copy-start = (f32[1024]{0:T(1024)S(1)}, f32[1024]{0:T(1024)}, u32[]{:S(2)}) copy-start(f32[1024]{0:T(1024)} %param.28) | copy-start | bytes 12292

commit v6 on v5

--- a/solution.py
+++ b/solution.py
@@ -166,9 +166,9 @@
         prefix_hbm,
     ) = refs[:12]
     out_refs, refs = refs[12 : 12 + len(PLANS)], refs[12 + len(PLANS) :]
-    act_ref, within_ref, delta_ref, bc_ref, taps_ref, number_ref = refs[:6]
+    act_ref, within_ref, delta_ref, bc_ref, taps_ref, number_hbm = refs[:6]
     (len_ref, slot_ref, dt_ref, alog_ref, xc_ref, xm_ref, tx_ref, tbc_ref, wx_ref) = refs[6:15]
-    x_scr, vals_scr, sems = refs[15:]
+    prefix_ref, x_scr, vals_scr, number_ref, sems = refs[15:]
     rows = PLANS[0].prefix
     ctx = lax.axis_index("ctx")
     heads = dt_ref.shape[0]
@@ -198,6 +198,7 @@
                 (tx_hbm, tx_ref),
                 (tbc_hbm.at[:, :, b_cols], tbc_ref.at[0]),
                 (tbc_hbm.at[:, :, c_cols], tbc_ref.at[1]),
+                (prefix_hbm, prefix_ref),
             ]
         )
     ]
@@ -212,21 +213,10 @@
     locs = [s - ctx * TOK for s in starts]
     number = plan_number(starts, slot_ref)
     number_ref[0] = number
-
-    def state_copies(plan, out_ref):
-        return [
-            pltpu.make_async_copy(
-                prefix_hbm.at[used if plan.slots == 1 else s],
-                out_ref.at[:, pl.ds(plan.prefix + s * rows, rows), :],
-                sems.at[len(copies) + s],
-            )
-            for s in range(plan.slots)
-        ]
-
-    states = state_copies(PLANS[0], out_refs[0])
-    for copy in states:
-        copy.start()
-    for copy in copies[2:]:
+    tell = pltpu.make_async_copy(number_ref, number_hbm, sems.at[len(copies)])
+    tell.start()
+
+    for copy in copies[2:-1]:
         copy.wait()
     scale = jnp.exp2(xc_ref[...].astype(F32)).T.astype(BF)
     wide = jnp.dot(scale, spread(MXB, xc_ref.shape[0]), preferred_element_type=F32)
@@ -313,8 +303,10 @@
                 out_ref[k, plan.bb :, :] = part
 
     finish(PLANS[0], out_refs[0], x, b_raw, high, low)
-    for copy in states:
-        copy.wait()
+    copies[-1].wait()
+    out_refs[0][:, rows : 2 * rows, :] = prefix_ref[used]
+
+    tell.wait()
 
     @pl.when(number > 0)
     def _():
@@ -322,13 +314,11 @@
 
             @pl.when(number == n)
             def _():
-                own = state_copies(plan, out_refs[n])
-                for copy in own:
-                    copy.start()
                 out_refs[n][:, :rows, :] = out_refs[0][:, :rows, :]
+                for s in range(plan.slots):
+                    at = plan.prefix + s * rows
+                    out_refs[n][:, at : at + rows, :] = prefix_ref[used if plan.slots == 1 else s]
                 finish(plan, out_refs[n], x_scr[8:, :chans], x_scr[8:, chans:], vals_scr[0], vals_scr[1])
-                for copy in own:
-                    copy.wait()
 
 
 def tail_of(plan, got_ref, slot, tail_at):
@@ -544,7 +534,7 @@
 
 
 def norm_kernel(gated_ref, sq_ref, gain_ref, out_hbm, out_scr, sems):
-    inverse = lax.rsqrt(sq_ref[...] / (HEADS_GROUP * WIDTH) + EPS)
+    inverse = lax.rsqrt((sq_ref[0] + sq_ref[1]) / (HEADS_GROUP * WIDTH) + EPS)
     inverse = jnp.broadcast_to(inverse, (TOK, TOK)).T
     rows = TOK // NORM_PARTS
     copies = []
@@ -613,16 +603,18 @@
             jax.ShapeDtypeStruct((1,), jnp.int32),
         ),
         in_specs=[hbm()] * 12,
-        out_specs=(vmem(),) * (5 + len(PLANS)) + (smem(),),
+        out_specs=(vmem(),) * (5 + len(PLANS)) + (hbm(),),
         scratch_shapes=[pltpu.SMEM((PROMPTS,), jnp.int32)] * 2
         + [pltpu.VMEM(source.shape, source.dtype) for source in sources[2:6]]
         + [
             pltpu.VMEM(tail_x.shape, BF),
             pltpu.VMEM((2,) + tail_x.shape[:2] + (STATE,), BF),
             pltpu.VMEM(conv_x.shape, F32),
+            pltpu.VMEM(prefixes.shape, BF),
             pltpu.VMEM((TOK + 8, chans + STATE), F32),
             pltpu.VMEM((2, heads, STATE), F32),
-            pltpu.SemaphoreType.DMA((15 + SLOTS_HERE,)),
+            pltpu.SMEM((1,), jnp.int32),
+            pltpu.SemaphoreType.DMA((17,)),
         ],
     )(*[pinned(source) for source in sources + [prefixes]])
     messages, rest, number = found[: len(PLANS)], found[len(PLANS) : -1], found[-1]
@@ -670,14 +662,14 @@
         ],
     )
     pairs = [[i, i + 1] for i in range(0, head_devices, 2)]
-    total = lax.psum(squares, "head", axis_index_groups=pairs)
+    both = lax.all_gather(squares, "head", axis_index_groups=pairs)
     return call(
         norm_kernel,
         jax.ShapeDtypeStruct((TOK, chans), BF),
         in_specs=[vmem()] * 3,
         out_specs=hbm(),
         scratch_shapes=[pltpu.VMEM((TOK, chans), BF), pltpu.SemaphoreType.DMA((NORM_PARTS,))],
-    )(gated, total, norm_gain.reshape(1, chans))
+    )(gated, both, norm_gain.reshape(1, chans))
 
 
 def solution(mesh):

time: 50.9 us -> 53.2 us (1.045)
  blocking collectives: 43.5 us -> 46.1 us
    psum x1 -> x0, blocking collectives: 3.79 us -> none  [on_device(): total = lax.psum(squares, 'head', axis_index_groups=pairs)]
    all_gather x0 -> x1, blocking collectives: none -> 3.07 us  [on_device(): both = lax.all_gather(squares, 'head', axis_index_groups=pairs)]
    all_to_all x1, blocking collectives: 15.9 us -> 18.5 us  [second_part(): got2 = lax.all_to_all(send2, 'ctx', 0, 0)]
    all_to_all x1, blocking collectives: 23.9 us -> 24.5 us  [second_part(): got1 = lax.all_to_all(send1, 'ctx', 0, 0)]
where the time goes in v6:
time: 53.2 us; the launch traced here: 53 us
  blocking collectives  46.1 us (87%)
  Pallas kernels  6.18 us (12%)
  between operations  0.72 us (1%)
    all_to_all x1, blocking collectives, second_part(): got1 = lax.all_to_all(send1, 'ctx', 0, 0)  24.5 us
    all_to_all x1, blocking collectives, second_part(): got2 = lax.all_to_all(send2, 'ctx', 0, 0)  18.5 us
    all_gather x1, blocking collectives, on_device(): both = lax.all_gather(squares, 'head', axis_index_groups=pairs)  3.07 us
    pallas_call x1, Pallas kernels, on_device(): call(block_kernel, tuple((jax.ShapeDtypeStruct((devices, plan.rows, STATE...  2.5 us
    pallas_call x1, Pallas kernels, second_part(): call(functools.partial(read_kernel, plan), (jax.ShapeDtypeStruct((TOK, ch...  1.68 us
    pallas_call x1, Pallas kernels, second_part(): call(functools.partial(scan_kernel, plan), jax.ShapeDtypeStruct((devices,...  1.18 us

profile of v6, /device:TPU:1, one launch (start us, length us, event | category | flops | bytes accessed | tf_op | source)
XLA Modules:
  0.0 53.0 jit_solution(4948353415172645374)
XLA Ops:
  0.0 0.0 copy-start.3
  0.0 0.0 copy-start.2
  0.0 0.0 copy-start.1
  0.0 0.0 copy-start.4
  0.0 2.5 %shard_map.145 = (bf16[32,96,128]{2,1,0:T(8,128)(2,1)S(1)}, bf16[32,144,128]{2,1,0:T(8,128)(2,1)S(1)}, bf16[32,104,128]{2,1,0:T(8,128)(2,1)S(1)}, bf16[32,152,12...) custom-call(s32[4]{0:T(128)} %refs_0_.1, ...), custom_call_target="tpu_custom_call" | custom-call | tf_op jit(solution)/shard_map/pallas_call | solution.py:594
  3.2 0.0 copy-done.3
  3.2 0.0 copy-done.2
  3.2 0.0 copy-done.1
  3.2 0.0 copy-done.4
  3.2 0.0 copy-start
  3.2 45.9 %conditional.1 = ((f32[128,1024]{1,0:T(8,128)S(1)}, f32[1,128]{1,0:T(1,128)S(1)})) conditional(s32[]{:T(128)} %bitcast.6, (bf16[32,96,128]{2,1,0:T(8,128)(2,1)S(1)}, s32[4]{0:T(128)S(1)}, s32[4]{0:T(128)S(1)}, f32[3,4,128]{2,1,0:T(4,128)S(1)}, bf16[128,1024]{1,0:T(8,128)(2,1)S(1)}, ...), branch_computations={%region_0.0_spmd, %region_1.0_spmd, %region_2.0_spmd, %region_3.0_... | conditional | bytes 4718600 | solution.py:657
  3.3 24.5 %all_to_all.36.got_ref.sent_ref = bf16[32,104,128]{2,1,0:T(8,128)(2,1)S(1)} all-to-all(bf16[32,104,128]{2,1,0:T(8,128)(2,1)S(1)} %get-tuple-element.107), channel_id=1, replica_groups=mesh['head'=16,'ctx'=32] {'ctx'}, dimensions={0} | all-to-all | bytes 1703936 | tf_op jit(solution)/shard_map/cond/branch_2_fun/all_to_all | solution.py:623
  27.7 1.2 %branch_2_fun.2 = bf16[32,104,128]{2,1,0:T(8,128)(2,1)S(1)} custom-call(s32[4]{0:T(128)S(1)} %get-tuple-element.105.len_ref, s32[4]{0:T(128)S(1)} %get-tuple-element.106.slot_ref, bf16[32,104,128]{2,1,0:T(8,128)(2,1)S(1)} %all_to_all.36.got_ref.sent_ref, f32[3,4,128]{2,1,0:T(4,128)S(1)} %get-tuple-element.108.taps_ref), custom_call_target="tpu_custom_call" | custom-call | tf_op jit(solution)/shard_map/cond/branch_2_fun/pallas_call | solution.py:624
  28.9 18.5 %all_to_all.37.got_ref = bf16[32,104,128]{2,1,0:T(8,128)(2,1)S(1)} all-to-all(bf16[32,104,128]{2,1,0:T(8,128)(2,1)S(1)} %branch_2_fun.2), channel_id=1, replica_groups=mesh['head'=16,'ctx'=32] {'ctx'}, dimensions={0} | all-to-all | bytes 1703936 | tf_op jit(solution)/shard_map/cond/branch_2_fun/all_to_all | solution.py:636
  47.4 1.7 %branch_2_fun.3 = (f32[128,1024]{1,0:T(8,128)S(1)}, f32[1,128]{1,0:T(1,128)S(1)}) custom-call(s32[4]{0:T(128)S(1)} %get-tuple-element.105.len_ref, s32[4]{0:T(128)S(1)} %get-tuple-element.106.slot_ref, bf16[32,104,128]{2,1,0:T(8,128)(2,1)S(1)} %all_to_all.36.got_ref.sent_ref, bf16[32,104,128]{2,1,0:T(8,128)(2,1)S(1)} %all_to_all.37.got_ref, ...), custom_call_target="tpu_custom_call" | custom-call | tf_op jit(solution)/shard_map/cond/branch_2_fun/pallas_call | solution.py:637
  49.1 3.1 %all-gather.1.sq_ref = f32[2,1,128]{2,1,0:T(1,128)S(1)} all-gather(f32[1,1,128]{2,1,0:T(1,128)S(1)} %bitcast.21), channel_id=2, replica_groups={{0,32},{64,96},{128,160},{192,224},{256,288},{320,352},{384,416},{448,4..., dimensions={0}, use_global_device_ids=true | all-gather | bytes 1536 | tf_op jit(solution)/shard_map/all_gather | solution.py:665
  52.2 0.0 copy-done
  52.2 0.8 %shard_map.146 = bf16[128,1024]{1,0:T(8,128)(2,1)} custom-call(f32[128,1024]{1,0:T(8,128)S(1)} %get-tuple-element.147.gated_ref, f32[2,1,128]{2,1,0:T(1,128)S(1)} %all-gather.1.sq_ref, f32[1,1024]{1,0:T(1,128)S(1)} %bitcast.10), custom_call_target="tpu_custom_call" | custom-call | tf_op jit(solution)/shard_map/pallas_call | solution.py:666
Async XLA Ops:
  0.0 3.2 %copy-start.3 = (s32[4]{0:T(128)S(1)}, s32[4]{0:T(128)}, u32[]{:S(2)}) copy-start(s32[4]{0:T(128)} %refs_1_.1) | copy-start | bytes 52
  0.0 3.2 %copy-start.2 = (s32[4]{0:T(128)S(1)}, s32[4]{0:T(128)}, u32[]{:S(2)}) copy-start(s32[4]{0:T(128)} %refs_0_.1) | copy-start | bytes 52
  0.0 3.2 %copy-start.1 = (bf16[128,1024]{1,0:T(8,128)(2,1)S(1)}, bf16[128,1024]{1,0:T(8,128)(2,1)}, u32[]{:S(2)}) copy-start(bf16[128,1024]{1,0:T(8,128)(2,1)} %param.22) | copy-start | bytes 786436
  0.0 3.2 %copy-start.4 = (f32[16]{0:T(128)S(1)}, f32[16]{0:T(128)}, u32[]{:S(2)}) copy-start(f32[16]{0:T(128)} %param.27) | copy-start | bytes 196
  3.2 49.0 %copy-start = (f32[1024]{0:T(1024)S(1)}, f32[1024]{0:T(1024)}, u32[]{:S(2)}) copy-start(f32[1024]{0:T(1024)} %param.28) | copy-start | bytes 12292

commit v7 on v6

--- a/solution.py
+++ b/solution.py
@@ -37,13 +37,16 @@
         self.bp, at = at, at + LAGS * self.begun
         self.bt, at = at, at + LAGS * slots
         self.ct, at = at, at + LAGS * slots
-        self.cp, at = at, at + 1
+        self.packed = slots > 1
+        if not self.packed:
+            self.cp, at = at, at + 1
         self.used = at
         self.rows = (at + 7) // 8 * 8
 
 
 PLANS = (Plan(1, 2), Plan(SLOTS_HERE, 2), Plan(1, 3), Plan(SLOTS_HERE, PROMPTS))
 DECAY_LANE = LAGS + PROMPTS * LAGS
+FACTORS = 16
 WINDOWS = 40
 
 
@@ -285,11 +288,18 @@
         tails = jnp.concatenate(tails_x, axis=0)
         c_last = bc_ref[1].astype(F32)[TOK - LAGS :]
         b_tile = jnp.concatenate([b_raw[:LAGS], c_last[:2], b_raw[TOK - LAGS :]], axis=0)
-        foot = [at_start[:, chans:]] + tails_b + tails_c + [c_last[2:]]
+        foot = [at_start[:, chans:]] + tails_b + tails_c
+        gap = jnp.zeros((1, STATE), F32)
+        if plan.packed:
+            gap = jnp.concatenate([gap, c_last[2:]], axis=0)
+            unused = jnp.zeros((heads, STATE - 2 * FACTORS), F32)
+            high = jnp.concatenate([high[:, :FACTORS], low[:, :FACTORS], unused], axis=1)
+        else:
+            gap = jnp.concatenate([gap, gap], axis=0)
+            foot.append(c_last[2:])
         if plan.rows > plan.used:
             foot.append(jnp.zeros((plan.rows - plan.used, STATE), F32))
         foot = jnp.concatenate(foot, axis=0)
-        gap = jnp.zeros((2, STATE), F32)
         tile_row = iota((8, STATE), 0)
         for c in range(chans // STATE):
             lanes = slice(c * STATE, (c + 1) * STATE)
@@ -298,7 +308,8 @@
             for k in range(c * STATE // rows, (c + 1) * STATE // rows):
                 h = k * rows // WIDTH
                 tile = jnp.where(tile_row == LAGS, high[h : h + 1], x_tile)
-                tile = jnp.where(tile_row == LAGS + 1, low[h : h + 1], tile)
+                if not plan.packed:
+                    tile = jnp.where(tile_row == LAGS + 1, low[h : h + 1], tile)
                 out_ref[k, plan.xb : plan.bb, :] = tile.astype(BF)
                 out_ref[k, plan.bb :, :] = part
 
@@ -340,7 +351,11 @@
 
     x_scr[...] = got_ref[:, plan.xb : plan.xb + 8, :].astype(F32).reshape(devices * 8, STATE)
     b_scr[...] = got_ref[:, plan.bb : plan.bb + 8, :].astype(F32).reshape(devices * 8, STATE)
-    factors = x_scr[pl.ds(LAGS, devices, stride=8), :] + x_scr[pl.ds(LAGS + 1, devices, stride=8), :]
+    factors = x_scr[pl.ds(LAGS, devices, stride=8), :]
+    if plan.packed:
+        factors = factors[:, :FACTORS] + factors[:, FACTORS : 2 * FACTORS]
+    else:
+        factors = factors + x_scr[pl.ds(LAGS + 1, devices, stride=8), :]
     prompt_factors = jnp.sum(factors, axis=0, keepdims=True)
 
     def windows(scr, start_at, tail_at):
@@ -402,7 +417,10 @@
     from_prompts = jnp.where(
         turn == 0, x_act[0][devices:], jnp.where(turn == 1, x_act[1][devices:], x_act[2][devices:])
     )
-    pad = jnp.zeros((8 - LAGS, STATE), F32)
+    for i in range(LAGS):
+        x_scr[pl.ds(i, devices, stride=8), :] = x_act[i][:devices]
+    from_blocks = x_scr[...].reshape(devices, 8, STATE)
+    out_ref[:, plan.prompts * rows :, :] = jnp.where(turn == LAGS, from_blocks, from_prompts[None]).astype(BF)
 
     prefixes = []
     for p in range(PROMPTS):
@@ -417,8 +435,6 @@
     for d in range(devices):
         out_ref[d, :rows, :] = state.astype(BF)
         out_ref[d, rows:states, :] = jnp.zeros((states - rows, STATE), BF)
-        from_block = jnp.concatenate([x_act[i][d : d + 1] for i in range(LAGS)] + [pad], axis=0)
-        out_ref[d, states:, :] = jnp.where(turn == LAGS, from_block, from_prompts).astype(BF)
         base = state
         for p in range(PROMPTS):
             base = jnp.where(blocks[p] == d, wide[p], base)
@@ -462,10 +478,12 @@
     prompt = sum((token >= loc).astype(jnp.int32) for loc in locs) - 1
 
     bc_scr[8:, :] = jnp.concatenate([bc_ref[0], bc_ref[1]], axis=1).astype(F32)
-    before = sent_ref[(ctx + devices - 1) % devices, plan.bb :, :].astype(F32)
-    bc_scr[8 - LAGS : 8, :STATE] = before[8 - LAGS : 8]
-    c_last = plan.cp - plan.bb
-    bc_scr[8 - LAGS : 8, STATE:] = jnp.concatenate([before[LAGS : LAGS + 2], before[c_last : c_last + 1]], axis=0)
+    before = sent_ref[(ctx + devices - 1) % devices, plan.xb :, :].astype(F32)
+    bc_scr[8 - LAGS : 8, :STATE] = before[16 - LAGS : 16]
+    c_last = LAGS + 1 if plan.packed else plan.cp - plan.xb
+    bc_scr[8 - LAGS : 8, STATE:] = jnp.concatenate(
+        [before[8 + LAGS : 10 + LAGS], before[c_last : c_last + 1]], axis=0
+    )
     tails = []
     for p in range(PROMPTS):
         pair = [tail_of(plan, sent_ref, slot_ref[p], at) for at in (plan.bt, plan.ct)]

time: 53.2 us -> 61.5 us (1.16)
  blocking collectives: 46.1 us -> 54.2 us
    all_to_all x1, blocking collectives: 24.5 us -> 29.2 us  [second_part(): got1 = lax.all_to_all(send1, 'ctx', 0, 0)]
    all_to_all x1, blocking collectives: 18.5 us -> 21.9 us  [second_part(): got2 = lax.all_to_all(send2, 'ctx', 0, 0)]
where the time goes in v7:
time: 61.5 us; the launch traced here: 61.3 us
  blocking collectives  54.2 us (88%)
  Pallas kernels  6.3 us (10%)
  between operations  0.71 us (1%)
    all_to_all x1, blocking collectives, second_part(): got1 = lax.all_to_all(send1, 'ctx', 0, 0)  29.2 us
    all_to_all x1, blocking collectives, second_part(): got2 = lax.all_to_all(send2, 'ctx', 0, 0)  21.9 us
    all_gather x1, blocking collectives, on_device(): both = lax.all_gather(squares, 'head', axis_index_groups=pairs)  3.07 us
    pallas_call x1, Pallas kernels, on_device(): call(block_kernel, tuple((jax.ShapeDtypeStruct((devices, plan.rows, STATE...  2.52 us
    pallas_call x1, Pallas kernels, second_part(): call(functools.partial(read_kernel, plan), (jax.ShapeDtypeStruct((TOK, ch...  1.75 us

profile of v7, /device:TPU:1, one launch (start us, length us, event | category | flops | bytes accessed | tf_op | source)
XLA Modules:
  0.0 61.3 jit_solution(10184752201882207697)
XLA Ops:
  0.0 0.0 copy-start.3
  0.0 0.0 copy-start.2
  0.0 0.0 copy-start.1
  0.0 0.0 copy-start.4
  0.0 2.5 %shard_map.145 = (bf16[32,96,128]{2,1,0:T(8,128)(2,1)S(1)}, bf16[32,136,128]{2,1,0:T(8,128)(2,1)S(1)}, bf16[32,104,128]{2,1,0:T(8,128)(2,1)S(1)}, bf16[32,152,12...) custom-call(s32[4]{0:T(128)} %refs_0_.1, ...), custom_call_target="tpu_custom_call" | custom-call | tf_op jit(solution)/shard_map/pallas_call | solution.py:612
  3.2 0.0 copy-done.3
  3.2 0.0 copy-done.2
  3.2 0.0 copy-done.1
  3.2 0.0 copy-done.4
  3.2 0.0 copy-start
  3.2 54.1 %conditional.1 = ((f32[128,1024]{1,0:T(8,128)S(1)}, f32[1,128]{1,0:T(1,128)S(1)})) conditional(s32[]{:T(128)} %bitcast.6, (bf16[32,96,128]{2,1,0:T(8,128)(2,1)S(1)}, s32[4]{0:T(128)S(1)}, s32[4]{0:T(128)S(1)}, f32[3,4,128]{2,1,0:T(4,128)S(1)}, bf16[128,1024]{1,0:T(8,128)(2,1)S(1)}, ...), branch_computations={%region_0.0_spmd, %region_1.0_spmd, %region_2.0_spmd, %region_3.0_... | conditional | bytes 4718600 | solution.py:675
  3.3 29.2 %all_to_all.38.got_ref.sent_ref = bf16[32,152,128]{2,1,0:T(8,128)(2,1)S(1)} all-to-all(bf16[32,152,128]{2,1,0:T(8,128)(2,1)S(1)} %get-tuple-element.117), channel_id=1, replica_groups=mesh['head'=16,'ctx'=32] {'ctx'}, dimensions={0} | all-to-all | bytes 2490368 | tf_op jit(solution)/shard_map/cond/branch_3_fun/all_to_all | solution.py:641
  32.4 1.2 %branch_3_fun.2 = bf16[32,136,128]{2,1,0:T(8,128)(2,1)S(1)} custom-call(s32[4]{0:T(128)S(1)} %get-tuple-element.115.len_ref, s32[4]{0:T(128)S(1)} %get-tuple-element.116.slot_ref, bf16[32,152,128]{2,1,0:T(8,128)(2,1)S(1)} %all_to_all.38.got_ref.sent_ref, f32[3,4,128]{2,1,0:T(4,128)S(1)} %get-tuple-element.118.taps_ref), custom_call_target="tpu_custom_call" | custom-call | tf_op jit(solution)/shard_map/cond/branch_3_fun/pallas_call | solution.py:642
  33.7 21.9 %all_to_all.39.got_ref = bf16[32,136,128]{2,1,0:T(8,128)(2,1)S(1)} all-to-all(bf16[32,136,128]{2,1,0:T(8,128)(2,1)S(1)} %branch_3_fun.2), channel_id=1, replica_groups=mesh['head'=16,'ctx'=32] {'ctx'}, dimensions={0} | all-to-all | bytes 2228224 | tf_op jit(solution)/shard_map/cond/branch_3_fun/all_to_all | solution.py:654
  55.6 1.7 %branch_3_fun.3 = (f32[128,1024]{1,0:T(8,128)S(1)}, f32[1,128]{1,0:T(1,128)S(1)}) custom-call(s32[4]{0:T(128)S(1)} %get-tuple-element.115.len_ref, s32[4]{0:T(128)S(1)} %get-tuple-element.116.slot_ref, bf16[32,152,128]{2,1,0:T(8,128)(2,1)S(1)} %all_to_all.38.got_ref.sent_ref, bf16[32,136,128]{2,1,0:T(8,128)(2,1)S(1)} %all_to_all.39.got_ref, ...), custom_call_target="tpu_custom_call" | custom-call | tf_op jit(solution)/shard_map/cond/branch_3_fun/pallas_call | solution.py:655
  57.4 3.1 %all-gather.1.sq_ref = f32[2,1,128]{2,1,0:T(1,128)S(1)} all-gather(f32[1,1,128]{2,1,0:T(1,128)S(1)} %bitcast.21), channel_id=2, replica_groups={{0,32},{64,96},{128,160},{192,224},{256,288},{320,352},{384,416},{448,4..., dimensions={0}, use_global_device_ids=true | all-gather | bytes 1536 | tf_op jit(solution)/shard_map/all_gather | solution.py:683
  60.4 0.0 copy-done
  60.4 0.8 %shard_map.146 = bf16[128,1024]{1,0:T(8,128)(2,1)} custom-call(f32[128,1024]{1,0:T(8,128)S(1)} %get-tuple-element.147.gated_ref, f32[2,1,128]{2,1,0:T(1,128)S(1)} %all-gather.1.sq_ref, f32[1,1024]{1,0:T(1,128)S(1)} %bitcast.10), custom_call_target="tpu_custom_call" | custom-call | tf_op jit(solution)/shard_map/pallas_call | solution.py:684
Async XLA Ops:
  0.0 3.2 %copy-start.3 = (s32[4]{0:T(128)S(1)}, s32[4]{0:T(128)}, u32[]{:S(2)}) copy-start(s32[4]{0:T(128)} %refs_1_.1) | copy-start | bytes 52
  0.0 3.2 %copy-start.2 = (s32[4]{0:T(128)S(1)}, s32[4]{0:T(128)}, u32[]{:S(2)}) copy-start(s32[4]{0:T(128)} %refs_0_.1) | copy-start | bytes 52
  0.0 3.2 %copy-start.1 = (bf16[128,1024]{1,0:T(8,128)(2,1)S(1)}, bf16[128,1024]{1,0:T(8,128)(2,1)}, u32[]{:S(2)}) copy-start(bf16[128,1024]{1,0:T(8,128)(2,1)} %param.22) | copy-start | bytes 786436
  0.0 3.2 %copy-start.4 = (f32[16]{0:T(128)S(1)}, f32[16]{0:T(128)}, u32[]{:S(2)}) copy-start(f32[16]{0:T(128)} %param.27) | copy-start | bytes 196
  3.2 57.2 %copy-start = (f32[1024]{0:T(1024)S(1)}, f32[1024]{0:T(1024)}, u32[]{:S(2)}) copy-start(f32[1024]{0:T(1024)} %param.28) | copy-start | bytes 12292

commit v8 on v7

--- a/solution.py
+++ b/solution.py
@@ -341,7 +341,7 @@
     return tail
 
 
-def scan_kernel(plan, len_ref, slot_ref, got_ref, taps_ref, out_ref, x_scr, b_scr, in_scr, mix_scr):
+def scan_kernel(plan, len_ref, slot_ref, got_ref, taps_ref, out_ref, x_scr, b_scr, in_scr, mix_scr, begin_scr):
     devices = got_ref.shape[0]
     rows = plan.prefix
     ctx = lax.axis_index("ctx")
@@ -429,15 +429,15 @@
         if plan.slots > 1:
             place = pl.multiple_of(place + (slot % SLOTS_HERE) * rows, rows)
         prefixes.append(got_ref[slot // SLOTS_HERE, pl.ds(place, rows), :])
-    wide = [piece.astype(F32) for piece in prefixes]
+    for p in range(PROMPTS):
+        begin_scr[blocks[p]] = prefixes[p].astype(F32)
     state = jnp.zeros((rows, STATE), F32)
     states = plan.prompts * rows
     for d in range(devices):
         out_ref[d, :rows, :] = state.astype(BF)
         out_ref[d, rows:states, :] = jnp.zeros((states - rows, STATE), BF)
-        base = state
-        for p in range(PROMPTS):
-            base = jnp.where(blocks[p] == d, wide[p], base)
+        begins = functools.reduce(jnp.logical_or, [block == d for block in blocks])
+        base = jnp.where(begins, begin_scr[d], state)
         decay = factors[d : d + 1, DECAY_LANE : DECAY_LANE + 1]
         state = decay * base + (got_ref[d, :rows, :].astype(F32) + extra[d * rows : (d + 1) * rows])
     for p in range(PROMPTS):
@@ -649,6 +649,7 @@
                 pltpu.VMEM((devices * 8, STATE), F32),
                 pltpu.VMEM((STATE, STATE), F32),
                 pltpu.VMEM((chans, STATE), BF),
+                pltpu.VMEM((devices, rows, STATE), F32),
             ],
         )(prompt_lengths, cache_slot, got1, taps)
         got2 = lax.all_to_all(send2, "ctx", 0, 0)

time: 61.5 us -> 49.6 us (0.81)
  blocking collectives: 54.2 us -> 42.8 us
    all_to_all x1, blocking collectives: 21.9 us -> 15.9 us  [second_part(): got2 = lax.all_to_all(send2, 'ctx', 0, 0)]
    all_to_all x1, blocking collectives: 29.2 us -> 23.9 us  [second_part(): got1 = lax.all_to_all(send1, 'ctx', 0, 0)]
where the time goes in v8:
time: 49.6 us; the launch traced here: 49.4 us
  blocking collectives  42.8 us (86%)
  Pallas kernels  5.85 us (12%)
  between operations  0.72 us (1%)
    all_to_all x1, blocking collectives, second_part(): got1 = lax.all_to_all(send1, 'ctx', 0, 0)  23.9 us
    all_to_all x1, blocking collectives, second_part(): got2 = lax.all_to_all(send2, 'ctx', 0, 0)  15.9 us
    all_gather x1, blocking collectives, on_device(): both = lax.all_gather(squares, 'head', axis_index_groups=pairs)  3.07 us
    pallas_call x1, Pallas kernels, on_device(): call(block_kernel, tuple((jax.ShapeDtypeStruct((devices, plan.rows, STATE...  2.26 us
    pallas_call x1, Pallas kernels, second_part(): call(functools.partial(read_kernel, plan), (jax.ShapeDtypeStruct((TOK, ch...  1.64 us
    pallas_call x1, Pallas kernels, second_part(): call(functools.partial(scan_kernel, plan), jax.ShapeDtypeStruct((devices,...  1.12 us

profile of v8, /device:TPU:1, one launch (start us, length us, event | category | flops | bytes accessed | tf_op | source)
XLA Modules:
  0.0 49.4 jit_solution(3176177242766623156)
XLA Ops:
  0.0 0.0 copy-start.3
  0.0 0.0 copy-start.2
  0.0 0.0 copy-start.1
  0.0 0.0 copy-start.4
  0.0 2.3 %shard_map.145 = (bf16[32,96,128]{2,1,0:T(8,128)(2,1)S(1)}, bf16[32,136,128]{2,1,0:T(8,128)(2,1)S(1)}, bf16[32,104,128]{2,1,0:T(8,128)(2,1)S(1)}, bf16[32,152,12...) custom-call(s32[4]{0:T(128)} %refs_0_.1, ...), custom_call_target="tpu_custom_call" | custom-call | tf_op jit(solution)/shard_map/pallas_call | solution.py:612
  2.9 0.0 copy-done.3
  3.0 0.0 copy-done.2
  3.0 0.0 copy-done.1
  3.0 0.0 copy-done.4
  3.0 0.0 copy-start
  3.0 42.5 %conditional.1 = ((f32[128,1024]{1,0:T(8,128)S(1)}, f32[1,128]{1,0:T(1,128)S(1)})) conditional(s32[]{:T(128)} %bitcast.6, (bf16[32,96,128]{2,1,0:T(8,128)(2,1)S(1)}, s32[4]{0:T(128)S(1)}, s32[4]{0:T(128)S(1)}, f32[3,4,128]{2,1,0:T(4,128)S(1)}, bf16[128,1024]{1,0:T(8,128)(2,1)S(1)}, ...), branch_computations={%region_0.0_spmd, %region_1.0_spmd, %region_2.0_spmd, %region_3.0_... | conditional | bytes 4718600 | solution.py:676
  3.0 23.9 %all_to_all.32.got_ref.sent_ref = bf16[32,96,128]{2,1,0:T(8,128)(2,1)S(1)} all-to-all(bf16[32,96,128]{2,1,0:T(8,128)(2,1)S(1)} %get-tuple-element.87), channel_id=1, replica_groups=mesh['head'=16,'ctx'=32] {'ctx'}, dimensions={0} | all-to-all | bytes 1572864 | tf_op jit(solution)/shard_map/cond/branch_0_fun/all_to_all | solution.py:641
  26.9 1.1 %branch_0_fun.2 = bf16[32,72,128]{2,1,0:T(8,128)(2,1)S(1)} custom-call(s32[4]{0:T(128)S(1)} %get-tuple-element.85.len_ref, s32[4]{0:T(128)S(1)} %get-tuple-element.86.slot_ref, bf16[32,96,128]{2,1,0:T(8,128)(2,1)S(1)} %all_to_all.32.got_ref.sent_ref, f32[3,4,128]{2,1,0:T(4,128)S(1)} %get-tuple-element.88.taps_ref), custom_call_target="tpu_custom_call" | custom-call | tf_op jit(solution)/shard_map/cond/branch_0_fun/pallas_call | solution.py:642
  28.0 15.9 %all_to_all.33.got_ref = bf16[32,72,128]{2,1,0:T(8,128)(2,1)S(1)} all-to-all(bf16[32,72,128]{2,1,0:T(8,128)(2,1)S(1)} %branch_0_fun.2), channel_id=1, replica_groups=mesh['head'=16,'ctx'=32] {'ctx'}, dimensions={0} | all-to-all | bytes 1179648 | tf_op jit(solution)/shard_map/cond/branch_0_fun/all_to_all | solution.py:655
  43.9 1.6 %branch_0_fun.3 = (f32[128,1024]{1,0:T(8,128)S(1)}, f32[1,128]{1,0:T(1,128)S(1)}) custom-call(s32[4]{0:T(128)S(1)} %get-tuple-element.85.len_ref, s32[4]{0:T(128)S(1)} %get-tuple-element.86.slot_ref, bf16[32,96,128]{2,1,0:T(8,128)(2,1)S(1)} %all_to_all.32.got_ref.sent_ref, bf16[32,72,128]{2,1,0:T(8,128)(2,1)S(1)} %all_to_all.33.got_ref, ...), custom_call_target="tpu_custom_call" | custom-call | tf_op jit(solution)/shard_map/cond/branch_0_fun/pallas_call | solution.py:656
  45.5 3.1 %all-gather.1.sq_ref = f32[2,1,128]{2,1,0:T(1,128)S(1)} all-gather(f32[1,1,128]{2,1,0:T(1,128)S(1)} %bitcast.21), channel_id=2, replica_groups={{0,32},{64,96},{128,160},{192,224},{256,288},{320,352},{384,416},{448,4..., dimensions={0}, use_global_device_ids=true | all-gather | bytes 1536 | tf_op jit(solution)/shard_map/all_gather | solution.py:684
  48.6 0.0 copy-done
  48.6 0.8 %shard_map.146 = bf16[128,1024]{1,0:T(8,128)(2,1)} custom-call(f32[128,1024]{1,0:T(8,128)S(1)} %get-tuple-element.147.gated_ref, f32[2,1,128]{2,1,0:T(1,128)S(1)} %all-gather.1.sq_ref, f32[1,1024]{1,0:T(1,128)S(1)} %bitcast.10), custom_call_target="tpu_custom_call" | custom-call | tf_op jit(solution)/shard_map/pallas_call | solution.py:685
Async XLA Ops:
  0.0 2.9 %copy-start.3 = (s32[4]{0:T(128)S(1)}, s32[4]{0:T(128)}, u32[]{:S(2)}) copy-start(s32[4]{0:T(128)} %refs_1_.1) | copy-start | bytes 52
  0.0 3.0 %copy-start.2 = (s32[4]{0:T(128)S(1)}, s32[4]{0:T(128)}, u32[]{:S(2)}) copy-start(s32[4]{0:T(128)} %refs_0_.1) | copy-start | bytes 52
  0.0 3.0 %copy-start.1 = (bf16[128,1024]{1,0:T(8,128)(2,1)S(1)}, bf16[128,1024]{1,0:T(8,128)(2,1)}, u32[]{:S(2)}) copy-start(bf16[128,1024]{1,0:T(8,128)(2,1)} %param.22) | copy-start | bytes 786436
  0.0 3.0 %copy-start.4 = (f32[16]{0:T(128)S(1)}, f32[16]{0:T(128)}, u32[]{:S(2)}) copy-start(f32[16]{0:T(128)} %param.27) | copy-start | bytes 196
  3.0 45.6 %copy-start = (f32[1024]{0:T(1024)S(1)}, f32[1024]{0:T(1024)}, u32[]{:S(2)}) copy-start(f32[1024]{0:T(1024)} %param.28) | copy-start | bytes 12292
